TPU v7x, 256 devices: a whole 4x4x8 slice. The times are simulated.
256 devices in a mesh: node: 64 (over z, y, core), state: 4 (over x).
Axes of the slice: x: 4, y: 4, z: 8, core: 2. Of those that a mesh axis runs over, the one named last changes fastest.
Arguments:
- block: bfloat16 [64, 2097152], P('state', 'node'), may hold values from -6 to 6
- connectivity: int32 [125, 32768], P(None, 'node'), may hold values from 0 to 49151, as said below
- potential: float32 [125, 32768], P(None, 'node'), may hold values from 0.1 to 3
- cell_matrix: bfloat16 [125, 125], replicated, as said below
Outputs:
- orthonormal: bfloat16 [64, 2097152], P('state', 'node')
- factor: float32 [64, 64], replicated
Inputs may be any that keep to these rules, and one draw needn't show every extreme that they name: `connectivity`: in each slab, numbers below 8192 are the previous slab's last 8192 nodes and numbers from 40960 on are the next slab's first nodes. The numbers of the slab's k-th cell (k from 0) lie in k * 96 to k * 96 + 2 * 96 - 1, those of its last cell in k * 96 to k * 96 + 95; each cell reaches the lower end of its range. `cell_matrix`: Symmetric.
All inputs are finite; a program needn't handle non-finite values.
Results may differ from a plain program's by a relative error of at most 0.015.
Values may be sent and summed in bfloat16 or wider, within the bound.
No kernel may reach another device: no remote copies, remote signals or barrier semaphores. Data moves between devices by JAX's collectives and lax.ppermute only.
A program may use at most 64 MiB of HBM per device.

v0:
```python
import jax
import jax.numpy as jnp
from jax import lax
from jax.sharding import PartitionSpec as P

CENTER = 3.0
HALF_WIDTH = 3.0


def extended(block, sides, width):
    for axis, dim in sides:
        count = lax.axis_size(axis)
        forward = [(i, i + 1) for i in range(count - 1)]
        backward = [(target, source) for source, target in forward]
        low = lax.ppermute(
            lax.slice_in_dim(block, block.shape[dim] - width, None, axis=dim), axis, forward
        )
        high = lax.ppermute(lax.slice_in_dim(block, 0, width, axis=dim), axis, backward)
        block = jnp.concatenate([low, block, high], axis=dim)
    return block


def passed_along(block, axis, distance):
    devices = range(lax.axis_size(axis))
    route = [(i - distance, i) for i in devices if i - distance in devices]
    return lax.ppermute(block, axis, route)


def cell_terms(window, connectivity, potential, cell_matrix):
    states = window.shape[0]
    cells = connectivity.shape[1]
    stride = window.shape[1] // cells
    segments = window.reshape(states, cells, stride)
    following = jnp.concatenate(
        [segments[:, 1:], jnp.zeros((states, 1, stride), segments.dtype)], axis=1
    )
    paired = jnp.concatenate([segments, following], axis=2)
    offsets = jnp.arange(cells, dtype=jnp.int32) * stride
    local_links = connectivity - offsets[None, :]
    columns = jnp.arange(2 * stride, dtype=jnp.int32)
    group = min(cells, 128)
    pieces = []
    for first_cell in range(0, cells, group):
        links = local_links[:, first_cell : first_cell + group]
        picker = links[:, :, None] == columns[None, None, :]
        picker_half = picker.astype(jnp.bfloat16)
        part_pair = paired[:, first_cell : first_cell + group]
        values = jnp.einsum(
            "skn,jkn->sjk", part_pair, picker_half, preferred_element_type=jnp.float32
        )
        mixed = jnp.einsum(
            "ij,sjk->sik",
            cell_matrix,
            values.astype(jnp.bfloat16),
            preferred_element_type=jnp.float32,
        )
        mixed = mixed + potential[None, :, first_cell : first_cell + group] * values
        spread = jnp.einsum(
            "sjk,jkn->skn", mixed, picker.astype(jnp.float32), precision=lax.Precision.HIGHEST
        )
        pieces.append(spread)
    spread = jnp.concatenate(pieces, axis=1)
    lower = spread[:, :, :stride]
    upper = spread[:, :, stride:]
    shifted = jnp.concatenate([jnp.zeros((states, 1, stride), jnp.float32), upper[:, :-1]], axis=1)
    return (lower + shifted).reshape(states, cells * stride)


def operate(field, connectivity, potential, cell_matrix):
    owned = field.shape[1]
    margin = owned // 4
    window = extended(field, (("node", 1),), margin)
    summed = cell_terms(window, connectivity, potential, cell_matrix)
    result = summed[:, margin : margin + owned]
    from_above = passed_along(summed[:, :margin].astype(jnp.bfloat16), "node", -1).astype(
        jnp.float32
    )
    from_below = passed_along(summed[:, margin + owned :].astype(jnp.bfloat16), "node", 1).astype(
        jnp.float32
    )
    result = result.at[:, owned - margin :].add(from_above)
    result = result.at[:, :margin].add(from_below)
    return result


def factorize(intersection):
    factor = jnp.linalg.cholesky(intersection)
    identity = jnp.eye(intersection.shape[0], dtype=factor.dtype)
    inverse = lax.linalg.triangular_solve(factor, identity, left_side=True, lower=True).astype(
        jnp.bfloat16
    )
    return (factor, inverse)


def per_device(block, connectivity, potential, cell_matrix):
    start = block.astype(jnp.float32)
    image = operate(block, connectivity, potential, cell_matrix)
    first = ((image - CENTER * start) / HALF_WIDTH).astype(jnp.bfloat16)
    image = operate(first, connectivity, potential, cell_matrix)
    second = (2.0 * (image - CENTER * first.astype(jnp.float32)) / HALF_WIDTH - start).astype(
        jnp.bfloat16
    )
    total_nodes = block.shape[1] * lax.axis_size("node")
    panel = lax.all_gather(second, "state", axis=0, tiled=True)
    partial_intersection = jnp.einsum("an,bn->ab", panel, panel, preferred_element_type=jnp.float32)
    intersection = lax.psum(partial_intersection, "node") / total_nodes
    factor, inverse = factorize(intersection)
    rows = second.shape[0]
    mine = lax.dynamic_slice_in_dim(inverse, lax.axis_index("state") * rows, rows, 0)
    orthonormal = jnp.dot(mine, panel, preferred_element_type=jnp.float32).astype(jnp.bfloat16)
    return (orthonormal, factor)


def solution(mesh):
    return jax.shard_map(
        per_device,
        mesh=mesh,
        in_specs=(P("state", "node"), P(None, "node"), P(None, "node"), P()),
        out_specs=(P("state", "node"), P()),
        check_vma=False,
    )
```

profile of v0, /device:TPU:2, one launch (start us, length us, event | category | flops | bytes accessed | tf_op | source)
XLA Modules:
  0.0 566.9 jit_solution(16091128970053678684)
XLA Ops:
  8.4 1.8 collective-permute-start
  10.1 1.3 collective-permute-start.1
  16.8 3.2 reshape.132
  20.0 1.4 copy.18
  21.7 2.8 fusion.34
  24.5 3.0 fusion.123
  28.4 4.3 fusion.122
  33.6 4.3 fusion.121
  38.2 1.5 copy.37
  39.8 4.2 fusion.120
  44.3 1.4 copy.39
  45.8 11.6 %fusion.42 = f32[16,128,192]{2,0,1:T(8,128)S(1)} fusion(s32[125,128]{0,1:T(8,128)S(1)} %copy.16, f32[16,128,125]{2,0,1:T(8,128)S(1)} %copy.33, f32[16,125,128]{1,0,2:T(8,128)} %get-tuple-element.75, f32[125,128]{0,1:T(8,128)} %copy.19), kind=kOutput, calls=%fused_computation.59 | convolution fusion | flops 593408000 | bytes 3748864 | tf_op jit(solution)/shard_map/sjk,jkn->skn/dot_general | solution.py:58
  57.4 9.9 %fusion.44 = f32[16,128,192]{2,0,1:T(8,128)S(1)} fusion(s32[125,128]{0,1:T(8,128)S(1)} %copy-done.11, f32[16,128,125]{2,0,1:T(8,128)S(1)} %copy.35, f32[16,125,128]{1,0,2:T(8,128)S(1)} %copy-done.19, f32[125,128]{0,1:T(8,128)S(1)} %copy-done.14), kind=kOutput, calls=%fused_computation.61 | convolution fusion | flops 593408000 | bytes 3748864 | tf_op jit(solution)/shard_map/sjk,jkn->skn/dot_general | solution.py:58
  67.3 10.0 %fusion.46 = f32[16,128,192]{2,0,1:T(8,128)S(1)} fusion(s32[125,128]{0,1:T(8,128)S(1)} %copy.22, f32[16,128,125]{2,0,1:T(8,128)S(1)} %copy-done.7, f32[16,125,128]{1,0,2:T(8,128)S(1)} %copy-done.20, f32[125,128]{0,1:T(8,128)S(1)} %copy.23), kind=kOutput, calls=%fused_computation.63 | convolution fusion | flops 593408000 | bytes 3748864 | tf_op jit(solution)/shard_map/sjk,jkn->skn/dot_general | solution.py:58
  77.3 9.8 %fusion.48 = f32[16,128,192]{2,0,1:T(8,128)S(1)} fusion(s32[125,128]{0,1:T(8,128)S(1)} %copy.24, f32[16,128,125]{2,0,1:T(8,128)S(1)} %copy-done.9, f32[16,125,128]{1,0,2:T(8,128)S(1)} %copy-done.21, f32[125,128]{0,1:T(8,128)S(1)} %copy.25), kind=kOutput, calls=%fused_computation.65 | convolution fusion | flops 593408000 | bytes 3748864 | tf_op jit(solution)/shard_map/sjk,jkn->skn/dot_general | solution.py:58
  88.2 2.3 fusion.37
  90.5 3.2 copy.26
  93.8 4.0 reshape.133
  98.0 1.3 collective-permute-start.2
  100.0 6.8 %collective-permute-start.3 = (bf16[16,8192]{1,0:T(8,128)(2,1)S(1)}, bf16[16,8192]{1,0:T(8,128)(2,1)S(1)}, u32[]{:S(2)}, u32[]{:S(2)}) collective-permute-start(bf16[16,8192]{1,0:T(8,128)(2,1)S(1)} %get-tuple-element.54), channel_id=1, source_target_pairs={{0,4},{4,8},{8,12},{12,16},{16,20},{20,24},{24,28},{28,32},{32,36}... | collective-permute-start | bytes 786440 | tf_op jit(solution)/shard_map/ppermute | solution.py:26
  109.2 5.8 %collective-permute-start.4 = (bf16[16,8192]{1,0:T(8,128)(2,1)S(1)}, bf16[16,8192]{1,0:T(8,128)(2,1)S(1)}, u32[]{:S(2)}, u32[]{:S(2)}) collective-permute-start(bf16[16,8192]{1,0:T(8,128)(2,1)S(1)} %get-tuple-element.56), channel_id=1, source_target_pairs={{0,4},{4,8},{8,12},{12,16},{16,20},{20,24},{24,28},{28,32},{32,36}... | collective-permute-start | bytes 786440 | tf_op jit(solution)/shard_map/ppermute | solution.py:15
  115.0 1.3 collective-permute-start.5
  116.3 4.1 collective-permute-done.5
  121.7 3.2 reshape.134
  124.9 1.4 copy.28
  126.6 3.0 fusion.35
  129.6 3.0 fusion.127
  132.7 3.0 fusion.126
  135.7 3.0 fusion.125
  138.7 3.0 fusion.124
  142.0 1.5 copy.41
  143.8 1.4 copy.43
  147.0 11.7 %fusion.43 = f32[16,128,192]{2,0,1:T(8,128)S(1)} fusion(s32[125,128]{0,1:T(8,128)S(1)} %copy.16, f32[16,128,125]{2,0,1:T(8,128)} %copy.41, f32[16,125,128]{1,0,2:T(8,128)} %get-tuple-element.83, f32[125,128]{0,1:T(8,128)} %copy.19), kind=kOutput, calls=%fused_computation.60 | convolution fusion | flops 593408000 | bytes 3748864 | tf_op jit(solution)/shard_map/sjk,jkn->skn/dot_general | solution.py:58
  158.8 9.9 %fusion.45 = f32[16,128,192]{2,0,1:T(8,128)S(1)} fusion(s32[125,128]{0,1:T(8,128)S(1)} %copy-done.13, f32[16,128,125]{2,0,1:T(8,128)S(1)} %copy-done.8, f32[16,125,128]{1,0,2:T(8,128)S(1)} %copy-done.18, f32[125,128]{0,1:T(8,128)S(1)} %copy-done.15), kind=kOutput, calls=%fused_computation.62 | convolution fusion | flops 593408000 | bytes 3748864 | tf_op jit(solution)/shard_map/sjk,jkn->skn/dot_general | solution.py:58
  168.7 10.0 %fusion.47 = f32[16,128,192]{2,0,1:T(8,128)S(1)} fusion(s32[125,128]{0,1:T(8,128)S(1)} %copy.22, f32[16,128,125]{2,0,1:T(8,128)S(1)} %copy.45, f32[16,125,128]{1,0,2:T(8,128)S(1)} %copy-done.17, f32[125,128]{0,1:T(8,128)S(1)} %copy.23), kind=kOutput, calls=%fused_computation.64 | convolution fusion | flops 593408000 | bytes 3748864 | tf_op jit(solution)/shard_map/sjk,jkn->skn/dot_general | solution.py:58
  178.7 9.8 %fusion.49 = f32[16,128,192]{2,0,1:T(8,128)S(1)} fusion(s32[125,128]{0,1:T(8,128)S(1)} %copy.24, f32[16,128,125]{2,0,1:T(8,128)S(1)} %copy.47, f32[16,125,128]{1,0,2:T(8,128)S(1)} %copy-done.16, f32[125,128]{0,1:T(8,128)S(1)} %copy.25), kind=kOutput, calls=%fused_computation.66 | convolution fusion | flops 593408000 | bytes 3748864 | tf_op jit(solution)/shard_map/sjk,jkn->skn/dot_general | solution.py:58
  189.6 2.3 fusion.36
  192.0 3.2 copy.29
  195.2 4.0 reshape.135
  199.4 1.4 collective-permute-start.6
  201.0 7.3 %collective-permute-start.7 = (bf16[16,8192]{1,0:T(8,128)(2,1)S(1)}, bf16[16,8192]{1,0:T(8,128)(2,1)S(1)}, u32[]{:S(2)}, u32[]{:S(2)}) collective-permute-start(bf16[16,8192]{1,0:T(8,128)(2,1)S(1)} %get-tuple-element.52), channel_id=1, source_target_pairs={{0,4},{4,8},{8,12},{12,16},{16,20},{20,24},{24,28},{28,32},{32,36}... | collective-permute-start | bytes 786440 | tf_op jit(solution)/shard_map/ppermute | solution.py:26
  210.3 1.4 fusion.41
  211.7 75.3 %all-gather.2.cloned.1.call-done = bf16[64,32768]{1,0:T(8,128)(2,1)} async-done(((bf16[16,32768]{1,0:T(8,128)(2,1)}), bf16[64,32768]{1,0:T(8,128)(2,1)}) %all-gather.2.cloned.1.call-update) | async-done | bytes 4194320 | tf_op jit(solution)/shard_map/all_gather | solution.py:104
  287.0 4.7 fusion.128
  291.7 251.0 %psum.7 = f32[64,64]{0,1:T(8,128)S(1)} all-reduce(f32[64,64]{0,1:T(8,128)S(1)} %fusion.128), channel_id=1, replica_groups=mesh['node'=64,'state'=4] {'node'}, use_global_device_ids=true, to_apply=%region_1.0 | all-reduce | flops 4096 | bytes 32768 | tf_op jit(solution)/shard_map/psum | solution.py:106
  542.8 5.8 %cholesky.17 = f32[64,64]{1,0:T(8,128)S(1)} custom-call(f32[64,64]{1,0:T(8,128)S(1)} %fusion.104), custom_call_target="Cholesky" | custom-call | tf_op jit(solution)/shard_map/jit(cholesky)/cholesky | solution.py:87
  550.6 4.9 custom-call.6
  555.8 3.8 convolution_convert_fusion
  (104 shorter events, 23.2 us)
Async XLA Ops:
  7.2 20.4 %copy-start = (bf16[125,125]{1,0:T(8,128)(2,1)S(1)}, bf16[125,125]{1,0:T(8,128)(2,1)}, u32[]{:S(2)}) copy-start(bf16[125,125]{1,0:T(8,128)(2,1)} %param.15) | copy-start | bytes 93754
  7.2 8.4 %copy-start.1 = (bf16[16,32768]{1,0:T(8,128)(2,1)S(1)}, bf16[16,32768]{1,0:T(8,128)(2,1)}, u32[]{:S(2)}) copy-start(bf16[16,32768]{1,0:T(8,128)(2,1)} %param.12) | copy-start | bytes 3145732
  7.2 279.8 %all-gather.2.cloned.1.call-start = ((), (), s32[]{:S(2)}) async-start(), calls=%async_computation | async-start | bytes 5242880 | tf_op jit(solution)/shard_map/all_gather | solution.py:104
  8.4 7.1 %collective-permute-start = (bf16[16,8192]{1,0:T(8,128)(2,1)S(1)}, bf16[16,8192]{1,0:T(8,128)(2,1)S(1)}, u32[]{:S(2)}, u32[]{:S(2)}) collective-permute-start(bf16[16,8192]{1,0:T(8,128)(2,1)S(1)} %get-tuple-element.58), channel_id=1, source_target_pairs={{0,4},{4,8},{8,12},{12,16},{16,20},{20,24},{24,28},{28,32},{32,36}... | collective-permute-start | bytes 786440 | tf_op jit(solution)/shard_map/ppermute | solution.py:15
  10.1 5.4 collective-permute-start.1
  14.4 14.1 %copy-start.10 = (s32[125,128]{0,1:T(8,128)}, s32[125,128]{0,1:T(8,128)S(1)}, u32[]{:S(2)}) copy-start(s32[125,128]{0,1:T(8,128)S(1)} %copy.20) | copy-start | bytes 192004
  24.5 3.0 copy-start.6
  45.8 11.6 %copy-start.11 = (s32[125,128]{0,1:T(8,128)S(1)}, s32[125,128]{0,1:T(8,128)}, u32[]{:S(2)}) copy-start(s32[125,128]{0,1:T(8,128)} %copy-done.10) | copy-start | bytes 192004
  45.8 11.6 %copy-start.14 = (f32[125,128]{0,1:T(8,128)S(1)}, f32[125,128]{0,1:T(8,128)}, u32[]{:S(2)}) copy-start(f32[125,128]{0,1:T(8,128)} %copy.21) | copy-start | bytes 192004
  45.8 11.6 %copy-start.19 = (f32[16,125,128]{1,0,2:T(8,128)S(1)}, f32[16,125,128]{1,0,2:T(8,128)}, u32[]{:S(2)}) copy-start(f32[16,125,128]{1,0,2:T(8,128)} %get-tuple-element.73) | copy-start | bytes 3072004
  57.4 9.9 %copy-start.7 = (f32[16,128,125]{2,0,1:T(8,128)S(1)}, f32[16,128,125]{2,0,1:T(8,128)}, u32[]{:S(2)}) copy-start(f32[16,128,125]{2,0,1:T(8,128)} %copy.37) | copy-start | bytes 3072004
  57.4 9.9 %copy-start.20 = (f32[16,125,128]{1,0,2:T(8,128)S(1)}, f32[16,125,128]{1,0,2:T(8,128)}, u32[]{:S(2)}) copy-start(f32[16,125,128]{1,0,2:T(8,128)} %get-tuple-element.71) | copy-start | bytes 3072004
  67.3 10.0 %copy-start.9 = (f32[16,128,125]{2,0,1:T(8,128)S(1)}, f32[16,128,125]{2,0,1:T(8,128)}, u32[]{:S(2)}) copy-start(f32[16,128,125]{2,0,1:T(8,128)} %copy.39) | copy-start | bytes 3072004
  67.3 10.0 %copy-start.21 = (f32[16,125,128]{1,0,2:T(8,128)S(1)}, f32[16,125,128]{1,0,2:T(8,128)}, u32[]{:S(2)}) copy-start(f32[16,125,128]{1,0,2:T(8,128)} %get-tuple-element.69) | copy-start | bytes 3072004
  98.0 8.9 %collective-permute-start.2 = (bf16[16,8192]{1,0:T(8,128)(2,1)S(1)}, bf16[16,8192]{1,0:T(8,128)(2,1)S(1)}, u32[]{:S(2)}, u32[]{:S(2)}) collective-permute-start(bf16[16,8192]{1,0:T(8,128)(2,1)S(1)} %get-tuple-element.55), channel_id=1, source_target_pairs={{4,0},{8,4},{12,8},{16,12},{20,16},{24,20},{28,24},{32,28},{36,32}... | collective-permute-start | bytes 786440 | tf_op jit(solution)/shard_map/ppermute | solution.py:26
  99.9 8.9 %copy-start.2 = (bf16[16,32768]{1,0:T(8,128)(2,1)S(1)}, bf16[16,32768]{1,0:T(8,128)(2,1)}, u32[]{:S(2)}) copy-start(bf16[16,32768]{1,0:T(8,128)(2,1)} %param.12) | copy-start | bytes 3145732
  100.0 8.0 %collective-permute-start.3 = (bf16[16,8192]{1,0:T(8,128)(2,1)S(1)}, bf16[16,8192]{1,0:T(8,128)(2,1)S(1)}, u32[]{:S(2)}, u32[]{:S(2)}) collective-permute-start(bf16[16,8192]{1,0:T(8,128)(2,1)S(1)} %get-tuple-element.54), channel_id=1, source_target_pairs={{0,4},{4,8},{8,12},{12,16},{16,20},{20,24},{24,28},{28,32},{32,36}... | collective-permute-start | bytes 786440 | tf_op jit(solution)/shard_map/ppermute | solution.py:26
  109.2 11.3 %copy-start.4 = (bf16[16,32768]{1,0:T(8,128)(2,1)}, bf16[16,32768]{1,0:T(8,128)(2,1)S(1)}, u32[]{:S(2)}) copy-start(bf16[16,32768]{1,0:T(8,128)(2,1)S(1)} %fusion.40) | copy-start | bytes 3145732
  109.2 7.1 %collective-permute-start.4 = (bf16[16,8192]{1,0:T(8,128)(2,1)S(1)}, bf16[16,8192]{1,0:T(8,128)(2,1)S(1)}, u32[]{:S(2)}, u32[]{:S(2)}) collective-permute-start(bf16[16,8192]{1,0:T(8,128)(2,1)S(1)} %get-tuple-element.56), channel_id=1, source_target_pairs={{0,4},{4,8},{8,12},{12,16},{16,20},{20,24},{24,28},{28,32},{32,36}... | collective-permute-start | bytes 786440 | tf_op jit(solution)/shard_map/ppermute | solution.py:15
  115.0 5.4 collective-permute-start.5
  129.6 3.0 copy-start.12
  147.0 11.7 %copy-start.8 = (f32[16,128,125]{2,0,1:T(8,128)S(1)}, f32[16,128,125]{2,0,1:T(8,128)}, u32[]{:S(2)}) copy-start(f32[16,128,125]{2,0,1:T(8,128)} %copy.43) | copy-start | bytes 3072004
  147.0 11.7 %copy-start.13 = (s32[125,128]{0,1:T(8,128)S(1)}, s32[125,128]{0,1:T(8,128)}, u32[]{:S(2)}) copy-start(s32[125,128]{0,1:T(8,128)} %copy-done.10) | copy-start | bytes 192004
  147.0 11.7 %copy-start.15 = (f32[125,128]{0,1:T(8,128)S(1)}, f32[125,128]{0,1:T(8,128)}, u32[]{:S(2)}) copy-start(f32[125,128]{0,1:T(8,128)} %copy.21) | copy-start | bytes 192004
  147.0 11.7 %copy-start.18 = (f32[16,125,128]{1,0,2:T(8,128)S(1)}, f32[16,125,128]{1,0,2:T(8,128)}, u32[]{:S(2)}) copy-start(f32[16,125,128]{1,0,2:T(8,128)} %get-tuple-element.81) | copy-start | bytes 3072004
  158.8 9.9 %copy-start.17 = (f32[16,125,128]{1,0,2:T(8,128)S(1)}, f32[16,125,128]{1,0,2:T(8,128)}, u32[]{:S(2)}) copy-start(f32[16,125,128]{1,0,2:T(8,128)} %get-tuple-element.79) | copy-start | bytes 3072004
  168.6 10.1 %copy-start.16 = (f32[16,125,128]{1,0,2:T(8,128)S(1)}, f32[16,125,128]{1,0,2:T(8,128)}, u32[]{:S(2)}) copy-start(f32[16,125,128]{1,0,2:T(8,128)} %get-tuple-element.77) | copy-start | bytes 3072004
  199.4 10.9 %copy-start.3 = (bf16[16,32768]{1,0:T(8,128)(2,1)S(1)}, bf16[16,32768]{1,0:T(8,128)(2,1)}, u32[]{:S(2)}) copy-start(bf16[16,32768]{1,0:T(8,128)(2,1)} %param.12) | copy-start | bytes 3145732
  199.4 10.9 %copy-start.5 = (bf16[16,32768]{1,0:T(8,128)(2,1)S(1)}, bf16[16,32768]{1,0:T(8,128)(2,1)}, u32[]{:S(2)}) copy-start(bf16[16,32768]{1,0:T(8,128)(2,1)} %copy-done.4) | copy-start | bytes 3145732
  199.4 8.9 %collective-permute-start.6 = (bf16[16,8192]{1,0:T(8,128)(2,1)S(1)}, bf16[16,8192]{1,0:T(8,128)(2,1)S(1)}, u32[]{:S(2)}, u32[]{:S(2)}) collective-permute-start(bf16[16,8192]{1,0:T(8,128)(2,1)S(1)} %get-tuple-element.53), channel_id=1, source_target_pairs={{4,0},{8,4},{12,8},{16,12},{20,16},{24,20},{28,24},{32,28},{36,32}... | collective-permute-start | bytes 786440 | tf_op jit(solution)/shard_map/ppermute | solution.py:26
  201.0 8.4 %collective-permute-start.7 = (bf16[16,8192]{1,0:T(8,128)(2,1)S(1)}, bf16[16,8192]{1,0:T(8,128)(2,1)S(1)}, u32[]{:S(2)}, u32[]{:S(2)}) collective-permute-start(bf16[16,8192]{1,0:T(8,128)(2,1)S(1)} %get-tuple-element.52), channel_id=1, source_target_pairs={{0,4},{4,8},{8,12},{12,16},{16,20},{20,24},{24,28},{28,32},{32,36}... | collective-permute-start | bytes 786440 | tf_op jit(solution)/shard_map/ppermute | solution.py:26
Sparse Core Ops, SparseCore 0:
  211.9 75.0 all-gather.1
where the time goes:
time: 572 us; the launch traced here: 567 us
  blocking collectives  251 us (44%)
  matrix products  122 us (21%)
  waiting for transfers between devices  81.5 us (14%)
  local copies, waits for them, and re-layouts  37.1 us (6%)
  other arithmetic  33.2 us (6%)
  starting transfers between devices  27 us (5%)
  between operations  15.2 us (3%)
    psum x1, blocking collectives, per_device(): intersection = lax.psum(partial_intersection, 'node') / total_nodes  251 us
    dot_general x8, matrix products, cell_terms(): jnp.einsum('sjk,jkn->skn', mixed, picker.astype(jnp.float32), precision=l...  82.7 us
    all_gather x1, waiting for transfers between devices, per_device(): panel = lax.all_gather(second, 'state', axis=0, tiled=True)  75.3 us
    dot_general x8, matrix products, cell_terms(): jnp.einsum('skn,jkn->sjk', part_pair, picker_half, preferred_element_type...  27.9 us
    ppermute x4, starting transfers between devices, passed_along(): return lax.ppermute(block, axis, route)  16.9 us
  transfers between devices with their start and end apart: 9, of which 4 were waited for; matrix products, arithmetic and copies ran while one was open for 1% of the time, Pallas kernels for 0%

commit v1 on v0

v1 whole, which is shorter than its diff:
```python
import functools

import jax
import jax.numpy as jnp
from jax import lax
from jax.experimental import pallas as pl
from jax.experimental.pallas import tpu as pltpu
from jax.sharding import PartitionSpec as P

CENTER = 3.0
HALF_WIDTH = 3.0
LANE = 128
QUAD = 4
HALO = 6
UNROLL = 2
ABSENT = 1024
CELL_TILES = ((0, 1), (0, 1, 2), (1, 2), (2, 3))


def floor_div3(x):
    return (x + 999) // 3 - 333


def ranges(slot, low, high, tiles, edge, slots):
    groups = slots * tiles // 2

    def clip(origin, first, last):
        start = jnp.maximum(-floor_div3(origin - low), first)
        stop = jnp.minimum(floor_div3(high - origin), last)
        return start, origin + 3 * start, jnp.maximum(stop - start + 1, 0)

    own = clip(-edge - tiles * slot, 0, groups - 1)
    before = slot < slots // 2
    origin = jnp.where(
        before, -edge - slots * tiles - tiles * slot, slots * tiles - edge - tiles * slot
    )
    other = clip(origin, 0, groups - 1)
    shift = jnp.where(before, groups - 24, 0)
    return own, (other[0] - shift, other[1], other[2])


def operator_kernel(
    slots, tiles, edge, window_ref, own_ref, other_ref, matrix_ref, second_ref, gram_ref, field, acc
):
    slot = lax.axis_index("state")
    slab = lax.axis_index("node")
    slabs = lax.axis_size("node")
    states, width = window_ref.shape
    full = acc.shape[1]
    owned = tiles * LANE
    margin = HALO * LANE
    rows = lax.broadcasted_iota(jnp.int32, (LANE, LANE), 0).astype(jnp.float32)

    def sweep(source, cells_ref, first, tile, count):
        def body(step, carry):
            base = tile + HALO + 3 * UNROLL * step
            column = pl.multiple_of(base * LANE, LANE)
            out = [None] * (3 * UNROLL + 1)
            for part in range(UNROLL):
                at = pl.multiple_of(column + 3 * part * LANE, LANE)
                x = source[:, pl.ds(at, 4 * LANE)]
                line = QUAD * (first + UNROLL * step + part)
                pickers, values, values_half = [], [], []
                for cell in range(QUAD):
                    node = cells_ref[0, pl.ds(line + cell, 1), :]
                    picked = [
                        (rows == node + (96.0 * cell - 128.0 * t + ABSENT)).astype(jnp.bfloat16)
                        for t in CELL_TILES[cell]
                    ]
                    pickers.append(dict(zip(CELL_TILES[cell], picked)))
                    begin = CELL_TILES[cell][0] * LANE
                    end = (CELL_TILES[cell][-1] + 1) * LANE
                    value = jnp.dot(
                        x[:, begin:end],
                        jnp.concatenate(picked, axis=0),
                        preferred_element_type=jnp.float32,
                    )
                    values.append(value)
                    values_half.append(value.astype(jnp.bfloat16))
                mixed = jnp.dot(
                    jnp.concatenate(values_half, axis=0),
                    matrix_ref[...],
                    preferred_element_type=jnp.float32,
                )
                mixed_half = []
                for cell in range(QUAD):
                    level = cells_ref[1, pl.ds(line + cell, 1), :]
                    term = mixed[states * cell : states * (cell + 1)] + level * values[cell]
                    mixed_half.append(term.astype(jnp.bfloat16))
                for t in range(4):
                    cells = [c for c in range(QUAD) if t in CELL_TILES[c]]
                    spread = lax.dot_general(
                        jnp.concatenate([mixed_half[c] for c in cells], axis=1),
                        jnp.concatenate([pickers[c][t] for c in cells], axis=1),
                        (((1,), (1,)), ((), ())),
                        preferred_element_type=jnp.float32,
                    )
                    k = 3 * part + t
                    out[k] = spread if out[k] is None else out[k] + spread
            for k, spread in enumerate(out):
                at = pl.multiple_of(column + k * LANE, LANE)
                acc[:, pl.ds(at, LANE)] += spread
            return carry

        lax.fori_loop(0, (count + UNROLL - 1) // UNROLL, body, 0)

    def apply(source, low, high):
        own, other = ranges(slot, low, high, tiles, edge, slots)
        sweep(source, own_ref, *own)
        sweep(source, other_ref, *other)

    field[:, pl.ds(0, width)] = window_ref[...]
    field[:, pl.ds(width, full - width)] = jnp.zeros((states, full - width), field.dtype)
    acc[...] = jnp.zeros_like(acc)
    apply(field, -HALO, tiles + 2)

    def to_first(step, carry):
        at = pl.multiple_of(step * 2 * LANE, 2 * LANE)
        here = pl.ds(at, 2 * LANE)
        start = window_ref[:, here].astype(jnp.float32)
        field[:, here] = ((acc[:, here] - CENTER * start) / HALF_WIDTH).astype(field.dtype)
        acc[:, here] = jnp.zeros((states, 2 * LANE), jnp.float32)
        return carry

    lax.fori_loop(0, width // (2 * LANE), to_first, 0)

    @pl.when((slab == 0) & (slot == 0))
    def _():
        field[:, pl.ds(0, margin)] = jnp.zeros((states, margin), field.dtype)

    @pl.when((slab == slabs - 1) & (slot == slots - 1))
    def _():
        field[:, pl.ds(margin + owned, margin)] = jnp.zeros((states, margin), field.dtype)

    apply(field, -3, tiles - 1)

    def to_second(step, gram):
        at = pl.multiple_of(step * 4 * LANE, 4 * LANE)
        here = pl.ds(pl.multiple_of(at + margin, 2 * LANE), 4 * LANE)
        image = acc[:, here] - CENTER * field[:, here].astype(jnp.float32)
        start = window_ref[:, here].astype(jnp.float32)
        second = (2.0 * image / HALF_WIDTH - start).astype(second_ref.dtype)
        second_ref[:, pl.ds(at, 4 * LANE)] = second
        return gram + lax.dot_general(
            second, second, (((1,), (1,)), ((), ())), preferred_element_type=jnp.float32
        )

    gram_ref[...] = lax.fori_loop(
        0, owned // (4 * LANE), to_second, jnp.zeros((states, states), jnp.float32)
    )


def filtered(window, own, other, matrix, slots, tiles, edge):
    states, width = window.shape
    full = width + (3 * UNROLL + 1) * LANE
    return pl.pallas_call(
        functools.partial(operator_kernel, slots, tiles, edge),
        out_shape=(
            jax.ShapeDtypeStruct((states, tiles * LANE), window.dtype),
            jax.ShapeDtypeStruct((states, states), jnp.float32),
        ),
        in_specs=[pl.BlockSpec(memory_space=pltpu.VMEM)] * 4,
        out_specs=[pl.BlockSpec(memory_space=pltpu.VMEM)] * 2,
        scratch_shapes=[
            pltpu.VMEM((states, full), window.dtype),
            pltpu.VMEM((states, full), jnp.float32),
        ],
        compiler_params=pltpu.CompilerParams(vmem_limit_bytes=40 << 20),
        name="operator",
    )(window, own, other, matrix)


def exchanged_sum(x):
    slabs = lax.axis_size("node")
    for stride in (1, 8):
        if stride == 1:
            groups = [[8 * g + i for i in range(8)] for g in range(slabs // 8)]
        else:
            groups = [[g + 8 * i for i in range(slabs // 8)] for g in range(8)]
        copies = jnp.broadcast_to(x[None], (len(groups[0]), *x.shape))
        x = lax.all_to_all(copies, "node", 0, 0, axis_index_groups=groups).sum(0)
    copies = jnp.broadcast_to(x[None], (lax.axis_size("state"), *x.shape))
    return lax.all_to_all(copies, "state", 0, 0).sum(0)


def factorize(intersection):
    factor = jnp.linalg.cholesky(intersection)
    identity = jnp.eye(intersection.shape[0], dtype=factor.dtype)
    inverse = lax.linalg.triangular_solve(factor, identity, left_side=True, lower=True).astype(
        jnp.bfloat16
    )
    return (factor, inverse)


def per_device(block, connectivity, potential, cell_matrix):
    rows, owned = block.shape
    nodes, cells = connectivity.shape
    slots = lax.axis_size("state")
    slabs = lax.axis_size("node")
    slot = lax.axis_index("state")
    tiles = owned // slots // LANE
    edge = tiles
    margin = HALO * LANE

    up = [(i, i + 1) for i in range(slabs - 1)]
    down = [(i + 1, i) for i in range(slabs - 1)]
    low = lax.ppermute(block[:, owned - margin :], "node", up)
    high = lax.ppermute(block[:, :margin], "node", down)

    stride = 3 * LANE // QUAD
    local = connectivity - (jnp.arange(cells, dtype=jnp.int32) * stride + ABSENT)[None, :]
    pads = ((0, 0), (0, 0), (0, LANE - nodes))
    own = jnp.stack([local.astype(jnp.float32).T, potential.T])
    own = jnp.pad(own, pads)
    send = jnp.where(slot < slots // 2, own[:, cells - 24 * QUAD :], own[:, : 24 * QUAD])
    route = [(slots * i + j, slots * (i + 1) + j) for i in range(slabs - 1) for j in range(slots // 2)]
    route += [
        (slots * (i + 1) + j, slots * i + j)
        for i in range(slabs - 1)
        for j in range(slots // 2, slots)
    ]
    other = lax.ppermute(send, ("node", "state"), route)
    spare = QUAD * UNROLL
    own = jnp.pad(own, ((0, 0), (0, spare), (0, 0)))
    other = jnp.pad(other, ((0, 0), (0, spare), (0, 0)))
    matrix = jnp.pad(cell_matrix.T, ((0, LANE - nodes), (0, LANE - nodes)))

    extended = jnp.concatenate([low, block, high], axis=1)
    width = tiles * LANE + 2 * margin
    pieces = jnp.stack([extended[:, tiles * LANE * i :][:, :width] for i in range(slots)])
    window = lax.all_to_all(pieces, "state", 0, 0).reshape(rows * slots, width)

    second, partial_sum = filtered(window, own, other, matrix, slots, tiles, edge)
    intersection = exchanged_sum(partial_sum) / (owned * slabs)
    factor, inverse = factorize(intersection)
    orthonormal = jnp.dot(inverse, second, preferred_element_type=jnp.float32).astype(jnp.bfloat16)
    orthonormal = lax.all_to_all(orthonormal, "state", 0, 1, tiled=True)
    return (orthonormal, factor)


def solution(mesh):
    return jax.shard_map(
        per_device,
        mesh=mesh,
        in_specs=(P("state", "node"), P(None, "node"), P(None, "node"), P()),
        out_specs=(P("state", "node"), P()),
        check_vma=False,
    )
```

time: 572 us -> 147 us (0.26)
  blocking collectives: 251 us -> 71 us
  matrix products: 122 us -> 0.65 us
  waiting for transfers between devices: 81.5 us -> 14.3 us
  local copies, waits for them, and re-layouts: 37.1 us -> 3.72 us
  Pallas kernels: 0 us -> 25.6 us
  starting transfers between devices: 27 us -> 11.9 us
  other arithmetic: 33.2 us -> 18.2 us
  between operations: 15.2 us -> 0.88 us
    psum x1 -> x0, blocking collectives: 251 us -> none  [per_device(): intersection = lax.psum(partial_intersection, 'node') / total_nodes]
    dot_general x26 -> x1, matrix products: 122 us -> 0.41 us  [per_device(): jnp.dot(inverse, second, preferred_element_type=jnp.float32)]
    all_gather x1 -> x0, waiting for transfers between devices: 75.3 us -> none  [per_device(): panel = lax.all_gather(second, 'state', axis=0, tiled=True)]
    all_to_all x0 -> x4, blocking collectives: none -> 71 us  [the longest x2 29.8 us: exchanged_sum(): x = lax.all_to_all(copies, 'node', 0, 0, axis_index_groups=groups).sum(0)]
    pallas_call x0 -> x1, Pallas kernels: none -> 25.6 us  [filtered(): pl.pallas_call(functools.partial(operator_kernel, slots, tiles, edge), ou...]
    ppermute x8 -> x3, starting transfers between devices: 27 us -> 6.92 us  [the longest x1 3.9 us: per_device(): other = lax.ppermute(send, ('node', 'state'), route)]
    reshape x6 -> x0, local copies, waits for them, and re-layouts: 17 us -> none  [the longest x4 9.05 us: cell_terms(): segments = window.reshape(states, cells, stride)]
    concatenate x6 -> x0, other arithmetic: 10.5 us -> none  [the longest x2 5.81 us: cell_terms(): paired = jnp.concatenate([segments, following], axis=2)]
  transfers between devices with their start and end apart: 9 -> 4, of which waited for: 4 -> 3; matrix products, arithmetic and copies ran while one was open for 1% -> 0% of each run, Pallas kernels for 0% -> 0%
where the time goes in v1:
time: 147 us; the launch traced here: 146 us
  blocking collectives  71 us (48%)
  Pallas kernels  25.6 us (17%)
  other arithmetic  18.2 us (12%)
  waiting for transfers between devices  14.3 us (10%)
  starting transfers between devices  11.9 us (8%)
  local copies, waits for them, and re-layouts  3.72 us (3%)
    all_to_all x2, blocking collectives, exchanged_sum(): x = lax.all_to_all(copies, 'node', 0, 0, axis_index_groups=groups).sum(0)  29.8 us
    all_to_all x1, blocking collectives, exchanged_sum(): return lax.all_to_all(copies, 'state', 0, 0).sum(0)  26.3 us
    pallas_call x1, Pallas kernels, filtered(): pl.pallas_call(functools.partial(operator_kernel, slots, tiles, edge), ou...  25.6 us
    all_to_all x1, blocking collectives, per_device(): orthonormal = lax.all_to_all(orthonormal, 'state', 0, 1, tiled=True)  14.9 us
    all_to_all x1, waiting for transfers between devices, per_device(): window = lax.all_to_all(pieces, 'state', 0, 0).reshape(rows * slots, width)  10.4 us
    another operation x3, other arithmetic, factorize(): factor = jnp.linalg.cholesky(intersection)  6.52 us
    another operation x2, other arithmetic, factorize(): lax.linalg.triangular_solve(factor, identity, left_side=True, lower=True)  6.16 us
    all_to_all x1, starting transfers between devices, per_device(): window = lax.all_to_all(pieces, 'state', 0, 0).reshape(rows * slots, width)  4.96 us
  transfers between devices with their start and end apart: 4, of which 3 were waited for; matrix products, arithmetic and copies ran while one was open for 0% of the time, Pallas kernels for 0%

profile of v1, /device:TPU:2, one launch (start us, length us, event | category | flops | bytes accessed | tf_op | source)
XLA Modules:
  0.0 146.2 jit_solution(557717890108050645)
XLA Ops:
  0.6 0.8 fusion.4
  1.4 1.7 %collective-permute-start = (bf16[16,768]{1,0:T(8,128)(2,1)S(1)}, bf16[16,768]{1,0:T(8,128)(2,1)S(1)}, u32[]{:S(2)}, u32[]{:S(2)}) collective-permute-start(bf16[16,768]{1,0:T(8,128)(2,1)S(1)} %get-tuple-element.12), channel_id=1, source_target_pairs={{0,4},{4,8},{8,12},{12,16},{16,20},{20,24},{24,28},{28,32},{32,36}... | collective-permute-start | bytes 73736 | tf_op jit(solution)/shard_map/ppermute | solution.py:207
  3.1 1.3 collective-permute-start.1
  4.4 0.0 collective-permute-done
  4.4 3.1 %collective-permute-done.1 = bf16[16,768]{1,0:T(8,128)(2,1)S(1)} collective-permute-done((bf16[16,768]{1,0:T(8,128)(2,1)S(1)}, bf16[16,768]{1,0:T(8,128)(2,1)S(1)}, u32[]{:S(2)}, u32[]{:S(2)}) %collective-permute-start.1) | collective-permute-done | bytes 24608 | tf_op jit(solution)/shard_map/ppermute | solution.py:208
  7.6 1.3 fusion.1
  8.9 1.2 pad_maximum_fusion
  10.1 0.0 copy-start
  10.1 0.0 copy-start.1
  10.1 5.0 %all-to-all-start = ((bf16[4,16,9728]{2,1,0:T(8,128)(2,1)}), bf16[4,16,9728]{2,1,0:T(8,128)(2,1)S(1)}, u32[]{:S(2)}, u32[]{:S(2)}) async-start(bf16[4,16,9728]{2,1,0:T(8,128)(2,1)} %pad_maximum_fusion), calls=%async_computation | async-start | bytes 2490368 | tf_op jit(solution)/shard_map/all_to_all | solution.py:231
  15.1 0.0 copy-done
  15.1 0.1 copy.11
  15.2 0.0 copy-done.1
  15.2 0.1 copy.12
  15.4 0.1 convert_bitcast_fusion
  15.5 0.0 copy-start.2
  15.5 0.1 select_maximum_fusion
  15.6 3.9 %collective-permute-start.2 = (f32[2,96,128]{2,1,0:T(8,128)S(1)}, f32[2,96,128]{2,1,0:T(8,128)S(1)}, u32[]{:S(2)}, u32[]{:S(2)}) collective-permute-start(f32[2,96,128]{2,1,0:T(8,128)S(1)} %slice_select_fusion), channel_id=1, source_target_pairs={{0,4},{1,5},{4,8},{5,9},{8,12},{9,13},{12,16},{13,17},{16,20},{17,... | collective-permute-start | bytes 294920 | tf_op jit(solution)/shard_map/ppermute | solution.py:222
  19.6 0.0 copy-done.2
  19.6 0.1 copy.13
  19.7 0.7 collective-permute-done.2
  20.4 10.4 %all-to-all-done = bf16[4,16,9728]{2,1,0:T(8,128)(2,1)S(1)} async-done(((bf16[4,16,9728]{2,1,0:T(8,128)(2,1)}), bf16[4,16,9728]{2,1,0:T(8,128)(2,1)S(1)}, u32[]{:S(2)}, u32[]{:S(2)}) %all-to-all-start) | async-done | bytes 1245216 | tf_op jit(solution)/shard_map/all_to_all | solution.py:231
  30.9 25.6 %operator.1 = (bf16[64,8192]{1,0:T(8,128)(2,1)S(1)}, f32[64,64]{1,0:T(8,128)S(1)}) custom-call(bf16[64,9728]{1,0:T(8,128)(2,1)S(1)} %bitcast.32, f32[2,520,128]{2,1,0:T(8,128)S(1)} %pad.17.own_ref, f32[2,104,128]{2,1,0:T(8,128)S(1)} %pad.18.other_ref, bf16[128,128]{1,0:T(8,128)(2,1)S(1)} %pad.19.matrix_ref), custom_call_target="tpu_custom_call" | custom-call | tf_op jit(solution)/shard_map/operator/pallas_call | solution.py:156
  56.5 0.2 reshape.28
  56.7 12.5 %all_to_all.39 = f32[8,1,4096]{2,1,0:T(1,128)S(1)} all-to-all(f32[8,1,4096]{2,1,0:T(1,128)S(1)} %reshape.28), channel_id=1, replica_groups={{0,4,8,12,16,20,24,28},{32,36,40,44,48,52,56,60},{64,68,72,76,80,84,88,..., dimensions={0} | all-to-all | bytes 262144 | tf_op jit(solution)/shard_map/all_to_all | solution.py:181
  69.1 0.5 broadcast.75
  69.7 1.0 reduce.6
  70.6 0.1 reshape.29
  70.8 0.2 reshape.30
  71.0 17.3 %all_to_all.40 = f32[8,1,4096]{2,1,0:T(1,128)S(1)} all-to-all(f32[8,1,4096]{2,1,0:T(1,128)S(1)} %reshape.30), channel_id=1, replica_groups={{0,32,64,96,128,160,192,224},{4,36,68,100,132,164,196,228},{8,40,72,104..., dimensions={0} | all-to-all | bytes 262144 | tf_op jit(solution)/shard_map/all_to_all | solution.py:181
  88.3 1.0 reduce.7
  89.3 0.1 reshape.31
  89.4 0.1 reshape.32
  89.5 26.3 %all_to_all.41 = f32[4,1,4096]{2,1,0:T(1,128)S(1)} all-to-all(f32[4,1,4096]{2,1,0:T(1,128)S(1)} %reshape.32), channel_id=1, replica_groups=mesh['node'=64,'state'=4] {'state'}, dimensions={0} | all-to-all | bytes 131072 | tf_op jit(solution)/shard_map/all_to_all | solution.py:183
  115.8 0.8 reduce.8
  116.6 0.1 reshape.33
  116.8 0.1 copy.14
  116.9 5.8 %cholesky.17 = f32[64,64]{1,0:T(8,128)S(1)} custom-call(f32[64,64]{1,0:T(8,128)S(1)} %fusion.3), custom_call_target="Cholesky" | custom-call | tf_op jit(solution)/shard_map/jit(cholesky)/cholesky | solution.py:187
  122.8 0.6 compare_reduce_fusion
  123.4 1.3 select_bitcast_fusion
  124.7 4.9 %custom-call.6 = f32[1,64,64]{1,2,0:T(8,128)S(1)} custom-call(f32[1,64,64]{2,1,0:T(8,128)S(1)} %get-tuple-element.6), custom_call_target="InvertDiagBlocksLowerTriangular" | custom-call | tf_op jit(solution)/shard_map/triangular_solve | solution.py:189
  129.6 0.2 convolution_convert_fusion.1
  129.8 0.4 convolution_convert_fusion
  130.2 14.9 %all_to_all.42 = bf16[4,16,8192]{2,1,0:T(8,128)(2,1)S(1)} all-to-all(bf16[4,16,8192]{2,1,0:T(8,128)(2,1)S(1)} %bitcast.33), channel_id=1, replica_groups=mesh['node'=64,'state'=4] {'state'}, dimensions={0} | all-to-all | bytes 2097152 | tf_op jit(solution)/shard_map/all_to_all | solution.py:237
  145.2 1.0 copy.16
  (13 shorter events, 0.2 us)
Async XLA Ops:
  1.4 3.0 %collective-permute-start = (bf16[16,768]{1,0:T(8,128)(2,1)S(1)}, bf16[16,768]{1,0:T(8,128)(2,1)S(1)}, u32[]{:S(2)}, u32[]{:S(2)}) collective-permute-start(bf16[16,768]{1,0:T(8,128)(2,1)S(1)} %get-tuple-element.12), channel_id=1, source_target_pairs={{0,4},{4,8},{8,12},{12,16},{16,20},{20,24},{24,28},{28,32},{32,36}... | collective-permute-start | bytes 73736 | tf_op jit(solution)/shard_map/ppermute | solution.py:207
  3.1 4.5 %collective-permute-start.1 = (bf16[16,768]{1,0:T(8,128)(2,1)S(1)}, bf16[16,768]{1,0:T(8,128)(2,1)S(1)}, u32[]{:S(2)}, u32[]{:S(2)}) collective-permute-start(bf16[16,768]{1,0:T(8,128)(2,1)S(1)} %get-tuple-element.13), channel_id=1, source_target_pairs={{4,0},{8,4},{12,8},{16,12},{20,16},{24,20},{28,24},{32,28},{36,32}... | collective-permute-start | bytes 73736 | tf_op jit(solution)/shard_map/ppermute | solution.py:208
  10.1 5.0 %copy-start = (s32[125,512]{1,0:T(8,128)S(1)}, s32[125,512]{1,0:T(8,128)}, u32[]{:S(2)}) copy-start(s32[125,512]{1,0:T(8,128)} %param.5) | copy-start | bytes 768004
  10.1 5.1 %copy-start.1 = (f32[125,512]{1,0:T(8,128)S(1)}, f32[125,512]{1,0:T(8,128)}, u32[]{:S(2)}) copy-start(f32[125,512]{1,0:T(8,128)} %param.6) | copy-start | bytes 768004
  10.1 20.8 %all-to-all-start = ((bf16[4,16,9728]{2,1,0:T(8,128)(2,1)}), bf16[4,16,9728]{2,1,0:T(8,128)(2,1)S(1)}, u32[]{:S(2)}, u32[]{:S(2)}) async-start(bf16[4,16,9728]{2,1,0:T(8,128)(2,1)} %pad_maximum_fusion), calls=%async_computation | async-start | bytes 2490368 | tf_op jit(solution)/shard_map/all_to_all | solution.py:231
  15.5 4.1 %copy-start.2 = (bf16[125,125]{1,0:T(8,128)(2,1)S(1)}, bf16[125,125]{1,0:T(8,128)(2,1)}, u32[]{:S(2)}) copy-start(bf16[125,125]{1,0:T(8,128)(2,1)} %param.7) | copy-start | bytes 93754
  15.6 4.8 %collective-permute-start.2 = (f32[2,96,128]{2,1,0:T(8,128)S(1)}, f32[2,96,128]{2,1,0:T(8,128)S(1)}, u32[]{:S(2)}, u32[]{:S(2)}) collective-permute-start(f32[2,96,128]{2,1,0:T(8,128)S(1)} %slice_select_fusion), channel_id=1, source_target_pairs={{0,4},{1,5},{4,8},{5,9},{8,12},{9,13},{12,16},{13,17},{16,20},{17,... | collective-permute-start | bytes 294920 | tf_op jit(solution)/shard_map/ppermute | solution.py:222

commit v2 on v0

v2 whole, which is shorter than its diff:
```python
import functools

import jax
import jax.numpy as jnp
from jax import lax
from jax.experimental import pallas as pl
from jax.experimental.pallas import tpu as pltpu
from jax.sharding import Mesh
from jax.sharding import PartitionSpec as P

CENTER = 3.0
HALF_WIDTH = 3.0
LANE = 128
QUAD = 4
HALO = 6
SPARE = 5
NEAR = 24
ABSENT = 1024
CELL_TILES = ((0, 1), (0, 1, 2), (1, 2), (2, 3))
NODE_AXES = ("z", "y", "core")
STATE_AXIS = "x"
SIZES = (8, 4, 2, 4)
VMEM = pl.BlockSpec(memory_space=pltpu.VMEM)


def floor_div3(x):
    return (x + 999) // 3 - 333


def families(tiles):
    slots = lax.axis_size(STATE_AXIS)
    slot = lax.axis_index(STATE_AXIS)
    edge = tiles
    groups = slots * tiles // 2
    before = slot < slots // 2
    shift = jnp.where(before, groups - NEAR, 0)
    origin = jnp.where(before, -edge - slots * tiles, slots * tiles - edge) - tiles * slot
    return (
        (-edge - tiles * slot, 0, groups),
        (origin + 3 * shift, groups * QUAD, NEAR),
    )


def span(family, low, high):
    origin, line, groups = family
    start = jnp.maximum(-floor_div3(origin - low), 0)
    stop = jnp.minimum(floor_div3(high - origin), groups - 1)
    return line + QUAD * start, origin + 3 * start, jnp.maximum(stop - start + 1, 0)


def group_block(source, origin, acc, cells_ref, matrix_ref, segments):
    rows = lax.broadcasted_iota(jnp.int32, (LANE, LANE), 0).astype(jnp.float32)
    rows = rows.astype(jnp.bfloat16)
    one = jnp.ones((LANE, LANE), jnp.bfloat16)
    none = jnp.zeros((LANE, LANE), jnp.bfloat16)
    states, width = source.shape

    def picker(node, shift):
        row = jnp.broadcast_to(node + shift, (16, LANE)).astype(jnp.bfloat16)
        return jnp.where(rows == jnp.concatenate([row] * (LANE // 16), axis=0), one, none)

    gathered = []
    for index, (tile, lines) in enumerate(segments):
        for part, line in enumerate(lines):
            at = jnp.clip((tile + origin + 3 * part) * LANE, 0, width - 4 * LANE)
            x = source[:, pl.ds(pl.multiple_of(at, LANE), 4 * LANE)]
            pickers = []
            for cell in range(QUAD):
                node = cells_ref[0, pl.ds(line + cell, 1), :]
                pickers.append(
                    {
                        t: picker(node, 96.0 * cell - 128.0 * t + ABSENT)
                        for t in CELL_TILES[cell]
                    }
                )
            values = []
            for pair, begin in (((0, 1), 0), ((2, 3), 1)):
                weights = jnp.concatenate(
                    [
                        jnp.concatenate([pickers[c].get(t, none) for c in pair], axis=1)
                        for t in range(begin, begin + 3)
                    ],
                    axis=0,
                )
                values.append(
                    jnp.dot(
                        x[:, begin * LANE : (begin + 3) * LANE],
                        weights,
                        preferred_element_type=jnp.float32,
                    )
                )
            gathered.append((index, part, line, pickers, values))
    combined = []
    for index, part, line, pickers, values in gathered:
        half = jnp.concatenate([v.astype(jnp.bfloat16) for v in values], axis=0)
        mixed = jnp.dot(half, matrix_ref[...], preferred_element_type=jnp.float32)
        terms = []
        for pair in range(2):
            level = jnp.concatenate(
                [cells_ref[1, pl.ds(line + 2 * pair + i, 1), :] for i in range(2)], axis=1
            )
            term = mixed[states * pair : states * (pair + 1)] + level * values[pair]
            term = term.astype(jnp.bfloat16)
            terms += [term[:, :LANE], term[:, LANE:]]
        combined.append((index, part, pickers, terms))
    sums = [[None] * (3 * len(lines) + 1) for tile, lines in segments]
    for index, part, pickers, terms in combined:
        for begin, cells in ((0, (0, 1, 2)), (2, (1, 2, 3))):
            weights = jnp.concatenate(
                [
                    jnp.concatenate([pickers[c].get(t, none) for c in cells], axis=1)
                    for t in (begin, begin + 1)
                ],
                axis=0,
            )
            spread = lax.dot_general(
                jnp.concatenate([terms[c] for c in cells], axis=1),
                weights,
                (((1,), (1,)), ((), ())),
                preferred_element_type=jnp.float32,
            )
            for i in range(2):
                k = 3 * part + begin + i
                piece = spread[:, i * LANE : (i + 1) * LANE]
                total = sums[index][k]
                sums[index][k] = piece if total is None else total + piece
    for (tile, lines), pieces in zip(segments, sums):
        for k, piece in enumerate(pieces):
            at = pl.multiple_of((tile + HALO + k) * LANE, LANE)
            acc[:, pl.ds(at, LANE)] += piece


def lines_of(line, count, done, parts, blank):
    return [jnp.where(done + i < count, line + QUAD * (done + i), blank) for i in range(parts)]


def sweep(source, origin, acc, cells_ref, matrix_ref, spans, parts, blank):
    (line_a, tile_a, count_a), (line_b, tile_b, count_b) = spans
    steps_a = (count_a + parts - 1) // parts
    steps_b = (count_b + parts - 1) // parts

    def body(step, carry):
        first = step < steps_a
        done = parts * jnp.where(first, step, step - steps_a)
        line = jnp.where(first, line_a, line_b)
        tile = jnp.where(first, tile_a, tile_b) + 3 * done
        count = jnp.where(first, count_a, count_b)
        lines = lines_of(line, count, done, parts, blank)
        group_block(source, origin, acc, cells_ref, matrix_ref, [(tile, lines)])
        return carry

    lax.fori_loop(0, steps_a + steps_b, body, 0)


def interior_kernel(owned_ref, cells_ref, matrix_ref, acc_ref):
    tiles = owned_ref.shape[1] // LANE
    blank = cells_ref.shape[1] - QUAD
    acc_ref[...] = jnp.zeros_like(acc_ref)
    spans = [span(f, 0, tiles - 4) for f in families(tiles)]
    sweep(owned_ref, 0, acc_ref, cells_ref, matrix_ref, spans, 7, blank)


def rest_kernel(
    owned_ref, low_ref, high_ref, cells_ref, matrix_ref, acc_ref, second_ref, gram_ref, sum_ref, field
):
    states, owned = owned_ref.shape
    tiles = owned // LANE
    margin = HALO * LANE
    blank = cells_ref.shape[1] - QUAD
    slot = lax.axis_index(STATE_AXIS)
    slab = lax.axis_index(NODE_AXES[0])
    slabs = lax.axis_size(NODE_AXES[0])
    for axis in NODE_AXES[1:]:
        slab = slab * lax.axis_size(axis) + lax.axis_index(axis)
        slabs = slabs * lax.axis_size(axis)
    acc = sum_ref
    field[:, pl.ds(0, margin)] = low_ref[...]
    field[:, pl.ds(margin, owned)] = owned_ref[...]
    field[:, pl.ds(margin + owned, margin)] = high_ref[...]

    ends = []
    for low, high in ((-HALO, -1), (tiles - 3, tiles + 2)):
        for family in families(tiles):
            line, tile, count = span(family, low, high)
            tile = jnp.clip(tile, low, high)
            ends.append((tile, lines_of(line, count, 0, 2, blank)))
    group_block(field, HALO, acc, cells_ref, matrix_ref, ends)

    chunk = 4 * LANE
    whole = owned + 2 * margin

    def to_first(step, carry):
        here = pl.ds(pl.multiple_of(step * chunk, LANE), chunk)
        start = field[:, here].astype(jnp.float32)
        field[:, here] = ((acc[:, here] - CENTER * start) * (1.0 / HALF_WIDTH)).astype(field.dtype)
        acc[:, here] = jnp.zeros((states, chunk), jnp.float32)
        return carry

    lax.fori_loop(0, whole // chunk, to_first, 0)
    acc[:, pl.ds(whole, SPARE * LANE)] = jnp.zeros((states, SPARE * LANE), jnp.float32)

    @pl.when((slab == 0) & (slot == 0))
    def _():
        field[:, pl.ds(0, margin)] = jnp.zeros((states, margin), field.dtype)

    @pl.when((slab == slabs - 1) & (slot == lax.axis_size(STATE_AXIS) - 1))
    def _():
        field[:, pl.ds(margin + owned, margin)] = jnp.zeros((states, margin), field.dtype)

    spans = [span(f, -3, tiles - 1) for f in families(tiles)]
    sweep(field, HALO, acc, cells_ref, matrix_ref, spans, 8, blank)

    chunk = 8 * LANE

    def to_second(step, gram):
        at = pl.multiple_of(step * chunk, LANE)
        here = pl.ds(pl.multiple_of(at + margin, LANE), chunk)
        image = acc[:, here] - CENTER * field[:, here].astype(jnp.float32)
        start = owned_ref[:, pl.ds(at, chunk)].astype(jnp.float32)
        second = (image * (2.0 / HALF_WIDTH) - start).astype(second_ref.dtype)
        second_ref[:, pl.ds(at, chunk)] = second
        return gram + lax.dot_general(
            second, second, (((1,), (1,)), ((), ())), preferred_element_type=jnp.float32
        )

    gram = lax.fori_loop(0, owned // chunk, to_second, jnp.zeros((states, states), jnp.float32))
    gram_ref[...] = jnp.concatenate([gram[: states // 2], gram[states // 2 :]], axis=1)


def filtered(owned, low, high, cells, matrix):
    states, count = owned.shape
    full = count + (2 * HALO + SPARE) * LANE
    params = pltpu.CompilerParams(vmem_limit_bytes=24 << 20)
    acc = pl.pallas_call(
        interior_kernel,
        out_shape=jax.ShapeDtypeStruct((states, full), jnp.float32),
        in_specs=[VMEM] * 3,
        out_specs=VMEM,
        compiler_params=params,
        cost_estimate=pl.CostEstimate(
            flops=20_000_000_000, bytes_accessed=20_000_000, transcendentals=0
        ),
        name="interior",
    )(owned, cells, matrix)
    second, gram, unused = pl.pallas_call(
        rest_kernel,
        out_shape=(
            jax.ShapeDtypeStruct((states, count), owned.dtype),
            jax.ShapeDtypeStruct((states // 2, 2 * states), jnp.float32),
            jax.ShapeDtypeStruct((states, full), jnp.float32),
        ),
        in_specs=[VMEM] * 6,
        out_specs=[VMEM] * 3,
        input_output_aliases={5: 2},
        scratch_shapes=[pltpu.VMEM((states, count + 2 * HALO * LANE), owned.dtype)],
        compiler_params=params,
        name="rest",
    )(owned, low, high, cells, matrix, acc)
    return second, gram


def factor_kernel(total_nodes, parts_ref, second_ref, orthonormal_ref, factor_ref):
    states, owned = second_ref.shape
    packed = parts_ref[0]
    for i in range(1, parts_ref.shape[0]):
        packed = packed + parts_ref[i]
    packed = packed * (1.0 / total_nodes)
    matrix = jnp.concatenate([packed[:, :states], packed[:, states:]], axis=0)
    row_of = lax.broadcasted_iota(jnp.int32, (states, states), 0)
    col_of = lax.broadcasted_iota(jnp.int32, (states, states), 1)
    identity = jnp.where(row_of == col_of, 1.0, 0.0)
    both = jnp.concatenate([matrix, identity], axis=1)
    tall = 8
    bands = [both[tall * k : tall * (k + 1)] for k in range(states // tall)]
    within = lax.broadcasted_iota(jnp.int32, (tall, 2 * states), 0)
    for j in range(states):
        k, i = divmod(j, tall)
        row = bands[k][i : i + 1]
        scaled = row * (1.0 / row[:, j : j + 1])
        for b in range(k, len(bands)):
            update = bands[b][:, j : j + 1] * scaled
            if b == k:
                update = jnp.where(within > i, update, 0.0)
            bands[b] = bands[b] - update
    both = jnp.concatenate(bands, axis=0)
    left = both[:, :states]
    pivots = jnp.sum(jnp.where(row_of == col_of, left, 0.0), axis=1, keepdims=True)
    both = both * (1.0 / jnp.sqrt(pivots))
    left = jnp.where(col_of >= row_of, both[:, :states], 0.0)
    factor_ref[...] = left.T
    inverse = both[:, states:].astype(jnp.bfloat16)
    chunk = 16 * LANE

    def body(step, carry):
        here = pl.ds(pl.multiple_of(step * chunk, LANE), chunk)
        orthonormal_ref[:, here] = jnp.dot(
            inverse, second_ref[:, here], preferred_element_type=jnp.float32
        ).astype(orthonormal_ref.dtype)
        return carry

    lax.fori_loop(0, owned // chunk, body, 0)


def orthonormalized(parts, second, total_nodes):
    states = second.shape[0]
    return pl.pallas_call(
        functools.partial(factor_kernel, total_nodes),
        out_shape=(
            jax.ShapeDtypeStruct(second.shape, second.dtype),
            jax.ShapeDtypeStruct((states, states), jnp.float32),
        ),
        in_specs=[VMEM] * 2,
        out_specs=[VMEM] * 2,
        name="factor",
    )(parts, second)


def gathered_terms(x):
    x = x + lax.ppermute(x, "core", [(0, 1), (1, 0)])
    group = ("y", "x")
    size = lax.axis_size("y") * lax.axis_size("x")
    x = lax.all_to_all(jnp.broadcast_to(x[None], (size, *x.shape)), group, 0, 0).sum(0)
    copies = jnp.broadcast_to(x[None], (lax.axis_size("z"), *x.shape))
    return lax.all_to_all(copies, "z", 0, 0)


def neighbour_route(slabs, slots, up):
    pairs = [(i, i + 1) for i in range(slabs * slots - 1)]
    return pairs if up else [(j, i) for i, j in pairs]


def per_device(block, connectivity, potential, cell_matrix):
    nodes, cells = connectivity.shape
    slots = lax.axis_size(STATE_AXIS)
    slot = lax.axis_index(STATE_AXIS)
    slabs = lax.axis_size(NODE_AXES)
    everyone = (*NODE_AXES, STATE_AXIS)
    margin = HALO * LANE

    owned = lax.all_to_all(block, STATE_AXIS, 1, 0, tiled=True)

    stride = 3 * LANE // QUAD
    local = connectivity - (jnp.arange(cells, dtype=jnp.int32) * stride + ABSENT)[None, :]
    lines = jnp.stack([local.astype(jnp.float32).T, potential.T])
    lines = jnp.pad(lines, ((0, 0), (0, 0), (0, LANE - nodes)))
    near = NEAR * QUAD
    send = jnp.where(slot < slots // 2, lines[:, cells - near :], lines[:, :near])
    route = []
    for i in range(slabs - 1):
        for j in range(slots):
            lower, upper = slots * i + j, slots * (i + 1) + j
            route.append((lower, upper) if j < slots // 2 else (upper, lower))
    other = lax.ppermute(send, everyone, route)
    blank = jnp.zeros((2, 2 * QUAD, LANE), jnp.float32)
    lines = jnp.concatenate([lines, other, blank], axis=1)
    matrix = jnp.pad(cell_matrix.T, ((0, LANE - nodes), (0, LANE - nodes)))
    matrix = jnp.kron(jnp.eye(2, dtype=matrix.dtype), matrix)

    low = lax.ppermute(owned[:, -margin:], everyone, neighbour_route(slabs, slots, True))
    high = lax.ppermute(owned[:, :margin], everyone, neighbour_route(slabs, slots, False))
    second, gram = filtered(owned, low, high, lines, matrix)
    parts = gathered_terms(gram)
    orthonormal, factor = orthonormalized(parts, second, block.shape[1] * slabs)
    orthonormal = lax.all_to_all(orthonormal, STATE_AXIS, 0, 1, tiled=True)
    return (orthonormal, factor)


def solution(mesh):
    fine = Mesh(mesh.devices.reshape(SIZES), (*NODE_AXES, STATE_AXIS))
    return jax.shard_map(
        per_device,
        mesh=fine,
        in_specs=(P(STATE_AXIS, NODE_AXES), P(None, NODE_AXES), P(None, NODE_AXES), P()),
        out_specs=(P(STATE_AXIS, NODE_AXES), P()),
        check_vma=False,
    )
```

time: 572 us -> 114 us (0.20)
  blocking collectives: 251 us -> 58.5 us
  matrix products: 122 us -> 0 us
  waiting for transfers between devices: 81.5 us -> 11.5 us
  other arithmetic: 33.2 us -> 0.55 us
  local copies, waits for them, and re-layouts: 37.1 us -> 4.89 us
  Pallas kernels: 0 us -> 24.4 us
  between operations: 15.2 us -> 0.83 us
  starting transfers between devices: 27 us -> 13 us
    psum x1 -> x0, blocking collectives: 251 us -> none  [per_device(): intersection = lax.psum(partial_intersection, 'node') / total_nodes]
    dot_general x26 -> x0, matrix products: 122 us -> none  [the longest x8 82.7 us: cell_terms(): jnp.einsum('sjk,jkn->skn', mixed, picker.astype(jnp.float32), precision=l...]
    all_gather x1 -> x0, waiting for transfers between devices: 75.3 us -> none  [per_device(): panel = lax.all_gather(second, 'state', axis=0, tiled=True)]
    all_to_all x0 -> x3, blocking collectives: none -> 58.5 us  [the longest x1 24.2 us: gathered_terms(): lax.all_to_all(jnp.broadcast_to(x[None], (size, *x.shape)), group, 0, 0)]
    pallas_call x0 -> x3, Pallas kernels: none -> 24.4 us  [the longest x1 10.9 us: filtered(): pl.pallas_call(rest_kernel, out_shape=(jax.ShapeDtypeStruct((states, coun...]
    ppermute x8 -> x4, starting transfers between devices: 27 us -> 7.14 us  [the longest x1 3.37 us: per_device(): lax.ppermute(owned[:, :margin], everyone, neighbour_route(slabs, slots, F...]
    reshape x6 -> x0, local copies, waits for them, and re-layouts: 17 us -> none  [the longest x4 9.05 us: cell_terms(): segments = window.reshape(states, cells, stride)]
    another operation x8 -> x2, other arithmetic: 13.6 us -> 0.19 us  [per_device(): lines = jnp.stack([local.astype(jnp.float32).T, potential.T])]
  transfers between devices with their start and end apart: 9 -> 5, of which waited for: 4 -> 3; matrix products, arithmetic and copies ran while one was open for 1% -> 1% of each run, Pallas kernels for 0% -> 4%
where the time goes in v2:
time: 114 us
  blocking collectives  58.5 us (51%)
  Pallas kernels  24.4 us (21%)
  starting transfers between devices  13 us (11%)
  waiting for transfers between devices  11.5 us (10%)
  local copies, waits for them, and re-layouts  4.89 us (4%)
    all_to_all x1, blocking collectives, gathered_terms(): lax.all_to_all(jnp.broadcast_to(x[None], (size, *x.shape)), group, 0, 0)  24.2 us
    all_to_all x1, blocking collectives, gathered_terms(): return lax.all_to_all(copies, 'z', 0, 0)  17.5 us
    all_to_all x1, blocking collectives, per_device(): orthonormal = lax.all_to_all(orthonormal, STATE_AXIS, 0, 1, tiled=True)  16.9 us
    pallas_call x1, Pallas kernels, filtered(): pl.pallas_call(rest_kernel, out_shape=(jax.ShapeDtypeStruct((states, coun...  10.9 us
    all_to_all x1, waiting for transfers between devices, per_device(): owned = lax.all_to_all(block, STATE_AXIS, 1, 0, tiled=True)  9.81 us
    pallas_call x1, Pallas kernels, orthonormalized(): pl.pallas_call(functools.partial(factor_kernel, total_nodes), out_shape=(...  8.87 us
    all_to_all x1, starting transfers between devices, per_device(): owned = lax.all_to_all(block, STATE_AXIS, 1, 0, tiled=True)  5.89 us
    pallas_call x1, Pallas kernels, filtered(): pl.pallas_call(interior_kernel, out_shape=jax.ShapeDtypeStruct((states, f...  4.68 us
  transfers between devices with their start and end apart: 5, of which 3 were waited for; matrix products, arithmetic and copies ran while one was open for 1% of the time, Pallas kernels for 4%

profile of v2, /device:TPU:2, one launch (start us, length us, event | category | flops | bytes accessed | tf_op | source)
XLA Modules:
  0.0 113.7 jit_solution(7963190764540108425)
XLA Ops:
  0.6 0.0 copy-start.1
  0.6 0.0 copy-start.2
  0.6 2.3 %copy.23 = bf16[2,4,8,8192]{3,2,0,1:T(8,128)(2,1)} copy(bf16[2,4,8,8192]{3,2,1,0:T(8,128)(2,1)} %bitcast.30) | data formatting | bytes 2097152 | tf_op jit(solution)/shard_map/all_to_all | solution.py:340
  3.0 0.0 copy-start.3
  3.0 5.9 %all-to-all-start = ((bf16[16,4,8192]{2,0,1:T(8,128)(2,1)}), bf16[16,4,8192]{2,0,1:T(8,128)(2,1)S(1)}, u32[]{:S(2)}, u32[]{:S(2)}) async-start(bf16[16,4,8192]{2,0,1:T(8,128)(2,1)} %bitcast.22), calls=%async_computation | async-start | bytes 2097152 | tf_op jit(solution)/shard_map/all_to_all | solution.py:340
  8.9 0.0 copy-done.1
  8.9 0.1 copy.13
  9.0 0.0 copy-done.2
  9.0 0.1 copy.14
  9.2 0.1 convert_bitcast_fusion
  9.3 0.1 select_maximum_fusion
  9.4 1.3 %collective-permute-start.2 = (f32[2,96,128]{2,1,0:T(8,128)S(1)}, f32[2,96,128]{2,1,0:T(8,128)S(1)}, u32[]{:S(2)}, u32[]{:S(2)}) collective-permute-start(f32[2,96,128]{2,1,0:T(8,128)S(1)} %slice_select_fusion), channel_id=1, source_target_pairs={{0,4},{1,5},{6,2},{7,3},{4,8},{5,9},{10,6},{11,7},{8,12},{9,13},{1... | collective-permute-start | bytes 294920 | tf_op jit(solution)/shard_map/ppermute | solution.py:353
  10.7 0.0 copy-done.3
  10.7 0.1 copy.17
  10.9 0.2 broadcast_multiply_fusion
  11.1 0.1 pad.12.clone
  11.1 0.5 collective-permute-done.2
  11.6 0.1 maximum_maximum_fusion.cells_ref
  11.8 9.8 %all-to-all-done = bf16[16,4,8192]{2,0,1:T(8,128)(2,1)S(1)} async-done(((bf16[16,4,8192]{2,0,1:T(8,128)(2,1)}), bf16[16,4,8192]{2,0,1:T(8,128)(2,1)S(1)}, u32[]{:S(2)}, u32[]{:S(2)}) %all-to-all-start) | async-done | bytes 1048608 | tf_op jit(solution)/shard_map/all_to_all | solution.py:340
  21.6 3.4 %collective-permute-start.1 = (bf16[64,768]{1,0:T(8,128)(2,1)S(1)}, bf16[64,768]{1,0:T(8,128)(2,1)S(1)}, u32[]{:S(2)}, u32[]{:S(2)}) collective-permute-start(bf16[64,768]{1,0:T(8,128)(2,1)S(1)} %get-tuple-element.10), channel_id=1, source_target_pairs={{1,0},{2,1},{3,2},{4,3},{5,4},{6,5},{7,6},{8,7},{9,8},{10,9},{11,1... | collective-permute-start | bytes 294920 | tf_op jit(solution)/shard_map/ppermute | solution.py:360
  25.0 2.5 %collective-permute-start = (bf16[64,768]{1,0:T(8,128)(2,1)S(1)}, bf16[64,768]{1,0:T(8,128)(2,1)S(1)}, u32[]{:S(2)}, u32[]{:S(2)}) collective-permute-start(bf16[64,768]{1,0:T(8,128)(2,1)S(1)} %get-tuple-element.11), channel_id=1, source_target_pairs={{0,1},{1,2},{2,3},{3,4},{4,5},{5,6},{6,7},{7,8},{8,9},{9,10},{10,1... | collective-permute-start | bytes 294920 | tf_op jit(solution)/shard_map/ppermute | solution.py:359
  27.4 4.7 %interior.1.acc_ref = f32[64,10368]{1,0:T(8,128)S(1)} custom-call(bf16[64,8192]{1,0:T(8,128)(2,1)S(1)} %bitcast.25, f32[2,616,128]{2,1,0:T(8,128)S(1)} %maximum_maximum_fusion.cells_ref, bf16[256,256]{1,0:T(8,128)(2,1)S(1)} %bitcast.27), custom_call_target="tpu_custom_call" | custom-call | flops 20000000000 | bytes 20000000 | tf_op jit(solution)/shard_map/interior/pallas_call | solution.py:234
  32.1 0.0 collective-permute-done.1.high_ref
  32.1 0.0 collective-permute-done.low_ref
  32.2 10.9 %rest.1 = (bf16[64,8192]{1,0:T(8,128)(2,1)S(1)}, f32[32,128]{1,0:T(8,128)S(1)}, f32[64,10368]{1,0:T(8,128)S(1)}) custom-call(bf16[64,8192]{1,0:T(8,128)(2,1)S(1)} %bitcast.26, bf16[64,768]{1,0:T(8,128)(2,1)S(1)} %collective-permute-done.low_ref, bf16[64,768]{1,0:T(8,128)(2,1)S(1)} %collective-permute-done.1.high_ref, ...), custom_call_target="tpu_custom_call", output_to_operand_aliasing={{2}: (5, {})} | custom-call | tf_op jit(solution)/shard_map/rest/pallas_call | solution.py:245
  43.0 0.0 copy-start
  43.0 1.0 copy-done
  44.0 0.0 collective-permute-start.3
  44.0 1.2 %collective-permute-done.3 = f32[32,128]{1,0:T(8,128)S(1)} collective-permute-done((f32[32,128]{1,0:T(8,128)S(1)}, f32[32,128]{1,0:T(8,128)S(1)}, u32[]{:S(2)}, u32[]{:S(2)}) %collective-permute-start.3) | collective-permute-done | bytes 16416 | tf_op jit(solution)/shard_map/ppermute | solution.py:319
  45.2 24.2 %all_to_all.48 = f32[16,32,128]{2,1,0:T(8,128)S(1)} all-to-all(f32[16,32,128]{2,1,0:T(8,128)S(1)} %broadcast_in_dim.11), channel_id=1, replica_groups=mesh['z'=8,'y'=4,'core'=2,'x'=4] {'y','x'}, dimensions={0} | all-to-all | bytes 524288 | tf_op jit(solution)/shard_map/all_to_all | solution.py:322
  69.5 17.5 %all_to_all.49.parts_ref = f32[8,32,128]{2,1,0:T(8,128)} all-to-all(f32[8,32,128]{2,1,0:T(8,128)S(1)} %broadcast_in_dim.12), channel_id=1, replica_groups=mesh['z'=8,'y'=4,'core'=2,'x'=4] {'z'}, dimensions={0} | all-to-all | bytes 262144 | tf_op jit(solution)/shard_map/all_to_all | solution.py:324
  86.9 8.9 %factor.1 = (bf16[64,8192]{1,0:T(8,128)(2,1)}, f32[64,64]{1,0:T(8,128)}) custom-call(f32[8,32,128]{2,1,0:T(8,128)} %all_to_all.49.parts_ref, bf16[64,8192]{1,0:T(8,128)(2,1)} %copy-done), custom_call_target="tpu_custom_call" | custom-call | tf_op jit(solution)/shard_map/factor/pallas_call | solution.py:306
  95.8 16.9 %all_to_all.50 = bf16[4,16,8192]{2,1,0:T(8,128)(2,1)S(1)} all-to-all(bf16[4,16,8192]{2,1,0:T(8,128)(2,1)} %bitcast.32), channel_id=1, replica_groups=mesh['z'=8,'y'=4,'core'=2,'x'=4] {'x'}, dimensions={0} | all-to-all | bytes 2097152 | tf_op jit(solution)/shard_map/all_to_all | solution.py:364
  112.6 1.0 copy.19
  (11 shorter events, 0.1 us)
Async XLA Ops:
  0.6 8.2 %copy-start.1 = (s32[125,512]{1,0:T(8,128)S(1)}, s32[125,512]{1,0:T(8,128)}, u32[]{:S(2)}) copy-start(s32[125,512]{1,0:T(8,128)} %param.5) | copy-start | bytes 768004
  0.6 8.4 %copy-start.2 = (f32[125,512]{1,0:T(8,128)S(1)}, f32[125,512]{1,0:T(8,128)}, u32[]{:S(2)}) copy-start(f32[125,512]{1,0:T(8,128)} %param.6) | copy-start | bytes 768004
  3.0 7.7 %copy-start.3 = (bf16[125,125]{1,0:T(8,128)(2,1)S(1)}, bf16[125,125]{1,0:T(8,128)(2,1)}, u32[]{:S(2)}) copy-start(bf16[125,125]{1,0:T(8,128)(2,1)} %param.7) | copy-start | bytes 93754
  3.0 18.6 %all-to-all-start = ((bf16[16,4,8192]{2,0,1:T(8,128)(2,1)}), bf16[16,4,8192]{2,0,1:T(8,128)(2,1)S(1)}, u32[]{:S(2)}, u32[]{:S(2)}) async-start(bf16[16,4,8192]{2,0,1:T(8,128)(2,1)} %bitcast.22), calls=%async_computation | async-start | bytes 2097152 | tf_op jit(solution)/shard_map/all_to_all | solution.py:340
  9.4 2.2 %collective-permute-start.2 = (f32[2,96,128]{2,1,0:T(8,128)S(1)}, f32[2,96,128]{2,1,0:T(8,128)S(1)}, u32[]{:S(2)}, u32[]{:S(2)}) collective-permute-start(f32[2,96,128]{2,1,0:T(8,128)S(1)} %slice_select_fusion), channel_id=1, source_target_pairs={{0,4},{1,5},{6,2},{7,3},{4,8},{5,9},{10,6},{11,7},{8,12},{9,13},{1... | collective-permute-start | bytes 294920 | tf_op jit(solution)/shard_map/ppermute | solution.py:353
  21.6 10.6 %collective-permute-start.1 = (bf16[64,768]{1,0:T(8,128)(2,1)S(1)}, bf16[64,768]{1,0:T(8,128)(2,1)S(1)}, u32[]{:S(2)}, u32[]{:S(2)}) collective-permute-start(bf16[64,768]{1,0:T(8,128)(2,1)S(1)} %get-tuple-element.10), channel_id=1, source_target_pairs={{1,0},{2,1},{3,2},{4,3},{5,4},{6,5},{7,6},{8,7},{9,8},{10,9},{11,1... | collective-permute-start | bytes 294920 | tf_op jit(solution)/shard_map/ppermute | solution.py:360
  25.0 7.2 %collective-permute-start = (bf16[64,768]{1,0:T(8,128)(2,1)S(1)}, bf16[64,768]{1,0:T(8,128)(2,1)S(1)}, u32[]{:S(2)}, u32[]{:S(2)}) collective-permute-start(bf16[64,768]{1,0:T(8,128)(2,1)S(1)} %get-tuple-element.11), channel_id=1, source_target_pairs={{0,1},{1,2},{2,3},{3,4},{4,5},{5,6},{6,7},{7,8},{8,9},{9,10},{10,1... | collective-permute-start | bytes 294920 | tf_op jit(solution)/shard_map/ppermute | solution.py:359
  43.0 1.0 copy-start
  44.0 1.2 %collective-permute-start.3 = (f32[32,128]{1,0:T(8,128)S(1)}, f32[32,128]{1,0:T(8,128)S(1)}, u32[]{:S(2)}, u32[]{:S(2)}) collective-permute-start(f32[32,128]{1,0:T(8,128)S(1)} %get-tuple-element.6), channel_id=1, source_target_pairs={{0,4},{4,0},{1,5},{5,1},{2,6},{6,2},{3,7},{7,3},{8,12},{12,8},{9,1... | collective-permute-start | bytes 49160 | tf_op jit(solution)/shard_map/ppermute | solution.py:319

commit v3 on v2

--- a/solution.py
+++ b/solution.py
@@ -13,7 +13,7 @@
 LANE = 128
 QUAD = 4
 HALO = 6
-SPARE = 5
+SPARE = 27
 NEAR = 24
 ABSENT = 1024
 CELL_TILES = ((0, 1), (0, 1, 2), (1, 2), (2, 3))
@@ -48,50 +48,51 @@
     return line + QUAD * start, origin + 3 * start, jnp.maximum(stop - start + 1, 0)
 
 
-def group_block(source, origin, acc, cells_ref, matrix_ref, segments):
-    rows = lax.broadcasted_iota(jnp.int32, (LANE, LANE), 0).astype(jnp.float32)
-    rows = rows.astype(jnp.bfloat16)
+def group_block(source, origin, acc, cells_ref, columns_ref, matrix_ref, segments):
+    def counted(axis):
+        index = lax.broadcasted_iota(jnp.int32, (LANE, LANE), axis)
+        return index.astype(jnp.float32).astype(jnp.bfloat16)
+
+    down, along = counted(0), counted(1)
     one = jnp.ones((LANE, LANE), jnp.bfloat16)
     none = jnp.zeros((LANE, LANE), jnp.bfloat16)
     states, width = source.shape
-
-    def picker(node, shift):
-        row = jnp.broadcast_to(node + shift, (16, LANE)).astype(jnp.bfloat16)
-        return jnp.where(rows == jnp.concatenate([row] * (LANE // 16), axis=0), one, none)
-
-    gathered = []
-    for index, (tile, lines) in enumerate(segments):
-        for part, line in enumerate(lines):
-            at = jnp.clip((tile + origin + 3 * part) * LANE, 0, width - 4 * LANE)
-            x = source[:, pl.ds(pl.multiple_of(at, LANE), 4 * LANE)]
-            pickers = []
-            for cell in range(QUAD):
-                node = cells_ref[0, pl.ds(line + cell, 1), :]
-                pickers.append(
-                    {
-                        t: picker(node, 96.0 * cell - 128.0 * t + ABSENT)
-                        for t in CELL_TILES[cell]
-                    }
-                )
-            values = []
-            for pair, begin in (((0, 1), 0), ((2, 3), 1)):
-                weights = jnp.concatenate(
-                    [
-                        jnp.concatenate([pickers[c].get(t, none) for c in pair], axis=1)
-                        for t in range(begin, begin + 3)
-                    ],
-                    axis=0,
-                )
-                values.append(
-                    jnp.dot(
-                        x[:, begin * LANE : (begin + 3) * LANE],
-                        weights,
-                        preferred_element_type=jnp.float32,
-                    )
-                )
-            gathered.append((index, part, line, pickers, values))
-    combined = []
-    for index, part, line, pickers, values in gathered:
+    sums = [[None] * (3 * len(lines) + 1) for tile, lines in segments]
+    groups = [
+        (index, part, tile, line)
+        for index, (tile, lines) in enumerate(segments)
+        for part, line in enumerate(lines)
+    ]
+
+    def shift(cell, t):
+        return 96.0 * cell - 128.0 * t + ABSENT
+
+    def gather(index, part, tile, line):
+        at = jnp.clip((tile + origin + 3 * part) * LANE, 0, width - 4 * LANE)
+        x = source[:, pl.ds(pl.multiple_of(at, LANE), 4 * LANE)]
+        pickers = []
+        for cell in range(QUAD):
+            node = cells_ref[0, pl.ds(line + cell, 1), :]
+            picked = {}
+            for t in CELL_TILES[cell]:
+                row = jnp.broadcast_to(node + shift(cell, t), (16, LANE)).astype(jnp.bfloat16)
+                row = jnp.concatenate([row] * (LANE // 16), axis=0)
+                picked[t] = jnp.where(down == row, one, none)
+            pickers.append(picked)
+        values = []
+        for pair, begin in (((0, 1), 0), ((2, 3), 1)):
+            weights = jnp.concatenate(
+                [
+                    jnp.concatenate([pickers[c].get(t, none) for c in pair], axis=1)
+                    for t in range(begin, begin + 3)
+                ],
+                axis=0,
+            )
+            x_part = x[:, begin * LANE : (begin + 3) * LANE]
+            values.append(jnp.dot(x_part, weights, preferred_element_type=jnp.float32))
+        return values
+
+    def mix(values, index, part, tile, line):
         half = jnp.concatenate([v.astype(jnp.bfloat16) for v in values], axis=0)
         mixed = jnp.dot(half, matrix_ref[...], preferred_element_type=jnp.float32)
         terms = []
@@ -102,21 +103,31 @@
             term = mixed[states * pair : states * (pair + 1)] + level * values[pair]
             term = term.astype(jnp.bfloat16)
             terms += [term[:, :LANE], term[:, LANE:]]
-        combined.append((index, part, pickers, terms))
-    sums = [[None] * (3 * len(lines) + 1) for tile, lines in segments]
-    for index, part, pickers, terms in combined:
+        return terms
+
+    def scatter(terms, index, part, tile, line):
+        begin = pl.multiple_of(line // LANE * LANE, LANE)
+        columns = pltpu.roll(columns_ref[:, pl.ds(begin, LANE)], LANE - (line - begin), 1)
+        placers = []
+        for cell in range(QUAD):
+            node = jnp.broadcast_to(columns[:, cell : cell + 1], (LANE, LANE))
+            placers.append(
+                {
+                    t: jnp.where(along == (node + shift(cell, t)).astype(jnp.bfloat16), one, none)
+                    for t in CELL_TILES[cell]
+                }
+            )
         for begin, cells in ((0, (0, 1, 2)), (2, (1, 2, 3))):
             weights = jnp.concatenate(
                 [
-                    jnp.concatenate([pickers[c].get(t, none) for c in cells], axis=1)
-                    for t in (begin, begin + 1)
+                    jnp.concatenate([placers[c].get(t, none) for t in (begin, begin + 1)], axis=1)
+                    for c in cells
                 ],
                 axis=0,
             )
-            spread = lax.dot_general(
+            spread = jnp.dot(
                 jnp.concatenate([terms[c] for c in cells], axis=1),
                 weights,
-                (((1,), (1,)), ((), ())),
                 preferred_element_type=jnp.float32,
             )
             for i in range(2):
@@ -124,17 +135,26 @@
                 piece = spread[:, i * LANE : (i + 1) * LANE]
                 total = sums[index][k]
                 sums[index][k] = piece if total is None else total + piece
-    for (tile, lines), pieces in zip(segments, sums):
-        for k, piece in enumerate(pieces):
+        lines = segments[index][1]
+        for k in range(3 * part, 3 * part + (4 if part == len(lines) - 1 else 3)):
             at = pl.multiple_of((tile + HALO + k) * LANE, LANE)
-            acc[:, pl.ds(at, LANE)] += piece
+            acc[:, pl.ds(at, LANE)] += sums[index][k]
+
+    values, terms = {}, {}
+    for step in range(len(groups) + 2):
+        if step < len(groups):
+            values[step] = gather(*groups[step])
+        if 0 <= step - 1 < len(groups):
+            terms[step - 1] = mix(values.pop(step - 1), *groups[step - 1])
+        if 0 <= step - 2:
+            scatter(terms.pop(step - 2), *groups[step - 2])
 
 
 def lines_of(line, count, done, parts, blank):
     return [jnp.where(done + i < count, line + QUAD * (done + i), blank) for i in range(parts)]
 
 
-def sweep(source, origin, acc, cells_ref, matrix_ref, spans, parts, blank):
+def sweep(source, origin, acc, cells_ref, columns_ref, matrix_ref, spans, parts, blank):
     (line_a, tile_a, count_a), (line_b, tile_b, count_b) = spans
     steps_a = (count_a + parts - 1) // parts
     steps_b = (count_b + parts - 1) // parts
@@ -146,22 +166,33 @@
         tile = jnp.where(first, tile_a, tile_b) + 3 * done
         count = jnp.where(first, count_a, count_b)
         lines = lines_of(line, count, done, parts, blank)
-        group_block(source, origin, acc, cells_ref, matrix_ref, [(tile, lines)])
+        group_block(source, origin, acc, cells_ref, columns_ref, matrix_ref, [(tile, lines)])
         return carry
 
     lax.fori_loop(0, steps_a + steps_b, body, 0)
 
 
-def interior_kernel(owned_ref, cells_ref, matrix_ref, acc_ref):
+def interior_kernel(owned_ref, cells_ref, columns_ref, matrix_ref, acc_ref):
     tiles = owned_ref.shape[1] // LANE
     blank = cells_ref.shape[1] - QUAD
-    acc_ref[...] = jnp.zeros_like(acc_ref)
+    whole = owned_ref.shape[1] + 2 * HALO * LANE
+    acc_ref[:, pl.ds(0, whole)] = jnp.zeros((acc_ref.shape[0], whole), jnp.float32)
     spans = [span(f, 0, tiles - 4) for f in families(tiles)]
-    sweep(owned_ref, 0, acc_ref, cells_ref, matrix_ref, spans, 7, blank)
+    sweep(owned_ref, 0, acc_ref, cells_ref, columns_ref, matrix_ref, spans, 7, blank)
 
 
 def rest_kernel(
-    owned_ref, low_ref, high_ref, cells_ref, matrix_ref, acc_ref, second_ref, gram_ref, sum_ref, field
+    owned_ref,
+    low_ref,
+    high_ref,
+    cells_ref,
+    columns_ref,
+    matrix_ref,
+    acc_ref,
+    second_ref,
+    gram_ref,
+    sum_ref,
+    field,
 ):
     states, owned = owned_ref.shape
     tiles = owned // LANE
@@ -184,7 +215,7 @@
             line, tile, count = span(family, low, high)
             tile = jnp.clip(tile, low, high)
             ends.append((tile, lines_of(line, count, 0, 2, blank)))
-    group_block(field, HALO, acc, cells_ref, matrix_ref, ends)
+    group_block(field, HALO, acc, cells_ref, columns_ref, matrix_ref, ends)
 
     chunk = 4 * LANE
     whole = owned + 2 * margin
@@ -197,7 +228,6 @@
         return carry
 
     lax.fori_loop(0, whole // chunk, to_first, 0)
-    acc[:, pl.ds(whole, SPARE * LANE)] = jnp.zeros((states, SPARE * LANE), jnp.float32)
 
     @pl.when((slab == 0) & (slot == 0))
     def _():
@@ -208,7 +238,7 @@
         field[:, pl.ds(margin + owned, margin)] = jnp.zeros((states, margin), field.dtype)
 
     spans = [span(f, -3, tiles - 1) for f in families(tiles)]
-    sweep(field, HALO, acc, cells_ref, matrix_ref, spans, 8, blank)
+    sweep(field, HALO, acc, cells_ref, columns_ref, matrix_ref, spans, 11, blank)
 
     chunk = 8 * LANE
 
@@ -227,21 +257,21 @@
     gram_ref[...] = jnp.concatenate([gram[: states // 2], gram[states // 2 :]], axis=1)
 
 
-def filtered(owned, low, high, cells, matrix):
+def filtered(owned, low, high, cells, columns, matrix):
     states, count = owned.shape
     full = count + (2 * HALO + SPARE) * LANE
     params = pltpu.CompilerParams(vmem_limit_bytes=24 << 20)
     acc = pl.pallas_call(
         interior_kernel,
         out_shape=jax.ShapeDtypeStruct((states, full), jnp.float32),
-        in_specs=[VMEM] * 3,
+        in_specs=[VMEM] * 4,
         out_specs=VMEM,
         compiler_params=params,
         cost_estimate=pl.CostEstimate(
             flops=20_000_000_000, bytes_accessed=20_000_000, transcendentals=0
         ),
         name="interior",
-    )(owned, cells, matrix)
+    )(owned, cells, columns, matrix)
     second, gram, unused = pl.pallas_call(
         rest_kernel,
         out_shape=(
@@ -249,13 +279,13 @@
             jax.ShapeDtypeStruct((states // 2, 2 * states), jnp.float32),
             jax.ShapeDtypeStruct((states, full), jnp.float32),
         ),
-        in_specs=[VMEM] * 6,
+        in_specs=[VMEM] * 7,
         out_specs=[VMEM] * 3,
-        input_output_aliases={5: 2},
+        input_output_aliases={6: 2},
         scratch_shapes=[pltpu.VMEM((states, count + 2 * HALO * LANE), owned.dtype)],
         compiler_params=params,
         name="rest",
-    )(owned, low, high, cells, matrix, acc)
+    )(owned, low, high, cells, columns, matrix, acc)
     return second, gram
 
 
@@ -271,21 +301,32 @@
     identity = jnp.where(row_of == col_of, 1.0, 0.0)
     both = jnp.concatenate([matrix, identity], axis=1)
     tall = 8
+    shape = (tall, 2 * states)
     bands = [both[tall * k : tall * (k + 1)] for k in range(states // tall)]
-    within = lax.broadcasted_iota(jnp.int32, (tall, 2 * states), 0)
-    for j in range(states):
-        k, i = divmod(j, tall)
-        row = bands[k][i : i + 1]
-        scaled = row * (1.0 / row[:, j : j + 1])
-        for b in range(k, len(bands)):
-            update = bands[b][:, j : j + 1] * scaled
-            if b == k:
-                update = jnp.where(within > i, update, 0.0)
-            bands[b] = bands[b] - update
+    within = lax.broadcasted_iota(jnp.int32, shape, 0)
+    for k in range(len(bands)):
+        later = bands[k + 1 :]
+        rows = [jnp.broadcast_to(bands[k][i : i + 1], shape) for i in range(tall)]
+
+        def replicated(values, i):
+            return jnp.broadcast_to(values[:, tall * k + i : tall * k + i + 1], shape)
+
+        pivot = {(i, l): replicated(rows[i], l) for i in range(tall) for l in range(i, tall)}
+        columns = [[replicated(band, i) for band in later] for i in range(tall)]
+        done = jnp.zeros(shape, jnp.float32)
+        for i in range(tall):
+            inverse = 1.0 / pivot[i, i]
+            scaled = rows[i] * inverse
+            done = jnp.where(within == i, rows[i] * lax.rsqrt(pivot[i, i]), done)
+            later = [band - c * scaled for band, c in zip(later, columns[i])]
+            for m in range(i + 1, tall):
+                ratio = pivot[i, m] * inverse
+                rows[m] = rows[m] - pivot[i, m] * scaled
+                for l in range(m, tall):
+                    pivot[m, l] = pivot[m, l] - ratio * pivot[i, l]
+                columns[m] = [c - d * ratio for c, d in zip(columns[m], columns[i])]
+        bands[k:] = [done, *later]
     both = jnp.concatenate(bands, axis=0)
-    left = both[:, :states]
-    pivots = jnp.sum(jnp.where(row_of == col_of, left, 0.0), axis=1, keepdims=True)
-    both = both * (1.0 / jnp.sqrt(pivots))
     left = jnp.where(col_of >= row_of, both[:, :states], 0.0)
     factor_ref[...] = left.T
     inverse = both[:, states:].astype(jnp.bfloat16)
@@ -311,8 +352,56 @@
         ),
         in_specs=[VMEM] * 2,
         out_specs=[VMEM] * 2,
+        compiler_params=pltpu.CompilerParams(vmem_limit_bytes=8 << 20),
         name="factor",
     )(parts, second)
+
+
+def split_kernel(block_ref, pieces_ref, done):
+    copies = []
+    for i in range(pieces_ref.shape[0]):
+        width = pieces_ref.shape[2]
+        part = block_ref.at[:, pl.ds(i * width, width)]
+        copies.append(pltpu.make_async_copy(part, pieces_ref.at[i], done.at[i]))
+        copies[-1].start()
+    for copy in copies:
+        copy.wait()
+
+
+def join_kernel(pieces_ref, block_ref, done):
+    copies = []
+    for i in range(pieces_ref.shape[0]):
+        width = pieces_ref.shape[2]
+        part = block_ref.at[:, pl.ds(i * width, width)]
+        copies.append(pltpu.make_async_copy(pieces_ref.at[i], part, done.at[i]))
+        copies[-1].start()
+    for copy in copies:
+        copy.wait()
+
+
+def quarters(block, count):
+    shape = (count, block.shape[0], block.shape[1] // count)
+    return pl.pallas_call(
+        split_kernel,
+        out_shape=jax.ShapeDtypeStruct(shape, block.dtype),
+        in_specs=[pl.BlockSpec(memory_space=pltpu.HBM)],
+        out_specs=pl.BlockSpec(memory_space=pltpu.HBM),
+        scratch_shapes=[pltpu.SemaphoreType.DMA((count,))],
+        name="quarters",
+    )(block)
+
+
+def joined(pieces):
+    count, states, width = pieces.shape
+    return pl.pallas_call(
+        join_kernel,
+        out_shape=jax.ShapeDtypeStruct((states, count * width), pieces.dtype),
+        in_specs=[VMEM],
+        out_specs=pl.BlockSpec(memory_space=pl.ANY),
+        scratch_shapes=[pltpu.SemaphoreType.DMA((count,))],
+        compiler_params=pltpu.CompilerParams(vmem_limit_bytes=4 << 20),
+        name="joined",
+    )(pieces)
 
 
 def gathered_terms(x):
@@ -337,7 +426,11 @@
     everyone = (*NODE_AXES, STATE_AXIS)
     margin = HALO * LANE
 
-    owned = lax.all_to_all(block, STATE_AXIS, 1, 0, tiled=True)
+    pieces, connectivity, potential = lax.optimization_barrier(
+        (quarters(block, slots), connectivity, potential)
+    )
+    pieces = lax.all_to_all(pieces, STATE_AXIS, 0, 0)
+    owned = pieces.reshape(-1, pieces.shape[2])
 
     stride = 3 * LANE // QUAD
     local = connectivity - (jnp.arange(cells, dtype=jnp.int32) * stride + ABSENT)[None, :]
@@ -351,18 +444,22 @@
             lower, upper = slots * i + j, slots * (i + 1) + j
             route.append((lower, upper) if j < slots // 2 else (upper, lower))
     other = lax.ppermute(send, everyone, route)
-    blank = jnp.zeros((2, 2 * QUAD, LANE), jnp.float32)
-    lines = jnp.concatenate([lines, other, blank], axis=1)
+    blank = jnp.zeros((2, LANE - near, LANE), jnp.float32)
+    other = jnp.concatenate([other, blank], axis=1)
+    lines = jnp.concatenate([lines, other], axis=1)
+    columns = jnp.pad(local.astype(jnp.float32), ((0, LANE - nodes), (0, 0)))
+    columns = jnp.concatenate([columns, other[0].T], axis=1)
     matrix = jnp.pad(cell_matrix.T, ((0, LANE - nodes), (0, LANE - nodes)))
     matrix = jnp.kron(jnp.eye(2, dtype=matrix.dtype), matrix)
 
     low = lax.ppermute(owned[:, -margin:], everyone, neighbour_route(slabs, slots, True))
     high = lax.ppermute(owned[:, :margin], everyone, neighbour_route(slabs, slots, False))
-    second, gram = filtered(owned, low, high, lines, matrix)
+    second, gram = filtered(owned, low, high, lines, columns, matrix)
     parts = gathered_terms(gram)
     orthonormal, factor = orthonormalized(parts, second, block.shape[1] * slabs)
-    orthonormal = lax.all_to_all(orthonormal, STATE_AXIS, 0, 1, tiled=True)
-    return (orthonormal, factor)
+    pieces = orthonormal.reshape(slots, -1, orthonormal.shape[1])
+    pieces = lax.all_to_all(pieces, STATE_AXIS, 0, 0)
+    return (joined(pieces), factor)
 
 
 def solution(mesh):

time: 114 us -> 133 us (1.17)
  Pallas kernels: 24.4 us -> 51.3 us
  local copies, waits for them, and re-layouts: 4.89 us -> 0.53 us
  blocking collectives: 58.5 us -> 55.3 us
    pallas_call x0 -> x2, Pallas kernels: none -> 33.9 us  [the longest x1 32.9 us: quarters(): pl.pallas_call(split_kernel, out_shape=jax.ShapeDtypeStruct(shape, block....]
    pallas_call x1, Pallas kernels: 8.87 us -> 3.46 us  [orthonormalized(): pl.pallas_call(functools.partial(factor_kernel, total_nodes), out_shape=(...]
    all_to_all x2 -> x0, local copies, waits for them, and re-layouts: 3.36 us -> none  [the longest x1 2.32 us: per_device(): owned = lax.all_to_all(block, STATE_AXIS, 1, 0, tiled=True)]
    all_to_all x1, blocking collectives: 24.2 us -> 22.2 us  [gathered_terms(): lax.all_to_all(jnp.broadcast_to(x[None], (size, *x.shape)), group, 0, 0)]
  transfers between devices with their start and end apart: 5 -> 5, of which waited for: 3 -> 3; matrix products, arithmetic and copies ran while one was open for 1% -> 1% of each run, Pallas kernels for 4% -> 3%
where the time goes in v3:
time: 133 us
  blocking collectives  55.3 us (42%)
  Pallas kernels  51.3 us (39%)
  starting transfers between devices  12.9 us (10%)
  waiting for transfers between devices  11.5 us (9%)
    pallas_call x1, Pallas kernels, quarters(): pl.pallas_call(split_kernel, out_shape=jax.ShapeDtypeStruct(shape, block....  32.9 us
    all_to_all x1, blocking collectives, gathered_terms(): lax.all_to_all(jnp.broadcast_to(x[None], (size, *x.shape)), group, 0, 0)  22.2 us
    all_to_all x1, blocking collectives, gathered_terms(): return lax.all_to_all(copies, 'z', 0, 0)  17.3 us
    all_to_all x1, blocking collectives, per_device(): pieces = lax.all_to_all(pieces, STATE_AXIS, 0, 0)  15.8 us
    all_to_all x1, waiting for transfers between devices, per_device(): pieces = lax.all_to_all(pieces, STATE_AXIS, 0, 0)  9.89 us
    pallas_call x1, Pallas kernels, filtered(): pl.pallas_call(rest_kernel, out_shape=(jax.ShapeDtypeStruct((states, coun...  9.76 us
    all_to_all x1, starting transfers between devices, per_device(): pieces = lax.all_to_all(pieces, STATE_AXIS, 0, 0)  5.77 us
    pallas_call x1, Pallas kernels, filtered(): pl.pallas_call(interior_kernel, out_shape=jax.ShapeDtypeStruct((states, f...  4.19 us
  transfers between devices with their start and end apart: 5, of which 3 were waited for; matrix products, arithmetic and copies ran while one was open for 1% of the time, Pallas kernels for 3%

profile of v3, /device:TPU:2, one launch (start us, length us, event | category | flops | bytes accessed | tf_op | source)
XLA Modules:
  0.0 133.0 jit_solution(9147924819614948175)
XLA Ops:
  0.6 0.0 copy-start.1
  0.6 0.0 copy-start
  0.7 0.0 copy-start.2
  0.7 32.9 %quarters.1 = bf16[4,16,8192]{2,1,0:T(8,128)(2,1)} custom-call(bf16[16,32768]{1,0:T(8,128)(2,1)} %block_ref.1), custom_call_target="tpu_custom_call" | custom-call | tf_op jit(solution)/shard_map/quarters/pallas_call | solution.py:384
  33.6 5.8 %all-to-all-start = ((bf16[4,16,8192]{2,1,0:T(8,128)(2,1)}), bf16[4,16,8192]{2,1,0:T(8,128)(2,1)S(1)}, u32[]{:S(2)}, u32[]{:S(2)}) async-start(bf16[4,16,8192]{2,1,0:T(8,128)(2,1)} %quarters.1), calls=%async_computation | async-start | bytes 2097152 | tf_op jit(solution)/shard_map/all_to_all | solution.py:432
  39.3 0.0 copy-done
  39.4 0.0 copy-done.1
  39.4 0.1 slice_select_fusion
  39.5 1.3 collective-permute-start.2
  40.9 0.0 copy-done.2
  40.9 0.1 copy.13
  41.1 0.2 broadcast_multiply_fusion
  41.3 0.1 pad.20.clone
  41.3 0.5 collective-permute-done.2
  41.8 0.1 maximum_maximum_fusion
  41.9 0.2 copy.12.cells_ref
  42.2 9.9 %all-to-all-done = bf16[4,16,8192]{2,1,0:T(8,128)(2,1)S(1)} async-done(((bf16[4,16,8192]{2,1,0:T(8,128)(2,1)}), bf16[4,16,8192]{2,1,0:T(8,128)(2,1)S(1)}, u32[]{:S(2)}, u32[]{:S(2)}) %all-to-all-start) | async-done | bytes 1048608 | tf_op jit(solution)/shard_map/all_to_all | solution.py:432
  52.1 3.4 %collective-permute-start.1 = (bf16[64,768]{1,0:T(8,128)(2,1)S(1)}, bf16[64,768]{1,0:T(8,128)(2,1)S(1)}, u32[]{:S(2)}, u32[]{:S(2)}) collective-permute-start(bf16[64,768]{1,0:T(8,128)(2,1)S(1)} %get-tuple-element.16), channel_id=1, source_target_pairs={{1,0},{2,1},{3,2},{4,3},{5,4},{6,5},{7,6},{8,7},{9,8},{10,9},{11,1... | collective-permute-start | bytes 294920 | tf_op jit(solution)/shard_map/ppermute | solution.py:456
  55.4 2.5 %collective-permute-start = (bf16[64,768]{1,0:T(8,128)(2,1)S(1)}, bf16[64,768]{1,0:T(8,128)(2,1)S(1)}, u32[]{:S(2)}, u32[]{:S(2)}) collective-permute-start(bf16[64,768]{1,0:T(8,128)(2,1)S(1)} %get-tuple-element.17), channel_id=1, source_target_pairs={{0,1},{1,2},{2,3},{3,4},{4,5},{5,6},{6,7},{7,8},{8,9},{9,10},{10,1... | collective-permute-start | bytes 294920 | tf_op jit(solution)/shard_map/ppermute | solution.py:455
  57.9 4.2 %interior.1.acc_ref = f32[64,13184]{1,0:T(8,128)S(1)} custom-call(bf16[64,8192]{1,0:T(8,128)(2,1)S(1)} %bitcast.20, f32[2,640,128]{2,1,0:T(8,128)S(1)} %copy.12.cells_ref, f32[128,640]{1,0:T(8,128)S(1)} %select_maximum_fusion.1.columns_ref, bf16[256,256]{1,0:T(8,128)(2,1)S(1)} %bitcast.23), custom_call_target="tpu_custom_call" | custom-call | flops 20000000000 | bytes 20000000 | tf_op jit(solution)/shard_map/interior/pallas_call | solution.py:264
  62.1 0.0 collective-permute-done.1.high_ref
  62.1 0.0 collective-permute-done.low_ref
  62.1 9.8 %rest.1 = (bf16[64,8192]{1,0:T(8,128)(2,1)S(1)}, f32[32,128]{1,0:T(8,128)S(1)}, f32[64,13184]{1,0:T(8,128)S(1)}) custom-call(bf16[64,8192]{1,0:T(8,128)(2,1)S(1)} %bitcast.21, bf16[64,768]{1,0:T(8,128)(2,1)S(1)} %collective-permute-done.low_ref, bf16[64,768]{1,0:T(8,128)(2,1)S(1)} %collective-permute-done.1.high_ref, ...), custom_call_target="tpu_custom_call", output_to_operand_aliasing={{2}: (6, {})} | custom-call | tf_op jit(solution)/shard_map/rest/pallas_call | solution.py:275
  71.9 0.0 collective-permute-start.3
  71.9 1.2 collective-permute-done.3
  73.2 22.2 %all_to_all.20 = f32[16,32,128]{2,1,0:T(8,128)S(1)} all-to-all(f32[16,32,128]{2,1,0:T(8,128)S(1)} %broadcast_in_dim.11), channel_id=1, replica_groups=mesh['z'=8,'y'=4,'core'=2,'x'=4] {'y','x'}, dimensions={0} | all-to-all | bytes 524288 | tf_op jit(solution)/shard_map/all_to_all | solution.py:411
  95.4 17.3 %all_to_all.21.parts_ref = f32[8,32,128]{2,1,0:T(8,128)S(1)} all-to-all(f32[8,32,128]{2,1,0:T(8,128)S(1)} %broadcast_in_dim.12), channel_id=1, replica_groups=mesh['z'=8,'y'=4,'core'=2,'x'=4] {'z'}, dimensions={0} | all-to-all | bytes 262144 | tf_op jit(solution)/shard_map/all_to_all | solution.py:413
  112.8 3.5 %factor.1 = (bf16[64,8192]{1,0:T(8,128)(2,1)S(1)}, f32[64,64]{1,0:T(8,128)}) custom-call(f32[8,32,128]{2,1,0:T(8,128)S(1)} %all_to_all.21.parts_ref, bf16[64,8192]{1,0:T(8,128)(2,1)S(1)} %get-tuple-element.13.second_ref), custom_call_target="tpu_custom_call" | custom-call | tf_op jit(solution)/shard_map/factor/pallas_call | solution.py:347
  116.2 15.8 %all_to_all.22.pieces_ref = bf16[4,16,8192]{2,1,0:T(8,128)(2,1)S(1)} all-to-all(bf16[4,16,8192]{2,1,0:T(8,128)(2,1)S(1)} %bitcast.22), channel_id=1, replica_groups=mesh['z'=8,'y'=4,'core'=2,'x'=4] {'x'}, dimensions={0} | all-to-all | bytes 2097152 | tf_op jit(solution)/shard_map/all_to_all | solution.py:461
  132.0 1.0 joined.1
  (15 shorter events, 0.2 us)
Async XLA Ops:
  0.6 38.7 %copy-start.1 = (f32[125,512]{1,0:T(8,128)S(1)}, f32[125,512]{1,0:T(8,128)}, u32[]{:S(2)}) copy-start(f32[125,512]{1,0:T(8,128)} %param.6) | copy-start | bytes 768004
  0.6 38.7 %copy-start = (s32[125,512]{1,0:T(8,128)S(1)}, s32[125,512]{1,0:T(8,128)}, u32[]{:S(2)}) copy-start(s32[125,512]{1,0:T(8,128)} %param.5) | copy-start | bytes 768004
  0.7 40.2 %copy-start.2 = (bf16[125,125]{1,0:T(8,128)(2,1)S(1)}, bf16[125,125]{1,0:T(8,128)(2,1)}, u32[]{:S(2)}) copy-start(bf16[125,125]{1,0:T(8,128)(2,1)} %param.7) | copy-start | bytes 93754
  33.6 18.5 %all-to-all-start = ((bf16[4,16,8192]{2,1,0:T(8,128)(2,1)}), bf16[4,16,8192]{2,1,0:T(8,128)(2,1)S(1)}, u32[]{:S(2)}, u32[]{:S(2)}) async-start(bf16[4,16,8192]{2,1,0:T(8,128)(2,1)} %quarters.1), calls=%async_computation | async-start | bytes 2097152 | tf_op jit(solution)/shard_map/all_to_all | solution.py:432
  39.5 2.3 %collective-permute-start.2 = (f32[2,96,128]{1,2,0:T(8,128)S(1)}, f32[2,96,128]{1,2,0:T(8,128)S(1)}, u32[]{:S(2)}, u32[]{:S(2)}) collective-permute-start(f32[2,96,128]{1,2,0:T(8,128)S(1)} %slice_select_fusion), channel_id=1, source_target_pairs={{0,4},{1,5},{6,2},{7,3},{4,8},{5,9},{10,6},{11,7},{8,12},{9,13},{1... | collective-permute-start | bytes 294920 | tf_op jit(solution)/shard_map/ppermute | solution.py:446
  52.1 10.1 %collective-permute-start.1 = (bf16[64,768]{1,0:T(8,128)(2,1)S(1)}, bf16[64,768]{1,0:T(8,128)(2,1)S(1)}, u32[]{:S(2)}, u32[]{:S(2)}) collective-permute-start(bf16[64,768]{1,0:T(8,128)(2,1)S(1)} %get-tuple-element.16), channel_id=1, source_target_pairs={{1,0},{2,1},{3,2},{4,3},{5,4},{6,5},{7,6},{8,7},{9,8},{10,9},{11,1... | collective-permute-start | bytes 294920 | tf_op jit(solution)/shard_map/ppermute | solution.py:456
  55.4 6.7 %collective-permute-start = (bf16[64,768]{1,0:T(8,128)(2,1)S(1)}, bf16[64,768]{1,0:T(8,128)(2,1)S(1)}, u32[]{:S(2)}, u32[]{:S(2)}) collective-permute-start(bf16[64,768]{1,0:T(8,128)(2,1)S(1)} %get-tuple-element.17), channel_id=1, source_target_pairs={{0,1},{1,2},{2,3},{3,4},{4,5},{5,6},{6,7},{7,8},{8,9},{9,10},{10,1... | collective-permute-start | bytes 294920 | tf_op jit(solution)/shard_map/ppermute | solution.py:455
  71.9 1.2 collective-permute-start.3

commit v4 on v3

--- a/solution.py
+++ b/solution.py
@@ -13,7 +13,7 @@
 LANE = 128
 QUAD = 4
 HALO = 6
-SPARE = 27
+SPARE = 2
 NEAR = 24
 ABSENT = 1024
 CELL_TILES = ((0, 1), (0, 1, 2), (1, 2), (2, 3))
@@ -150,26 +150,13 @@
             scatter(terms.pop(step - 2), *groups[step - 2])
 
 
-def lines_of(line, count, done, parts, blank):
-    return [jnp.where(done + i < count, line + QUAD * (done + i), blank) for i in range(parts)]
-
-
-def sweep(source, origin, acc, cells_ref, columns_ref, matrix_ref, spans, parts, blank):
-    (line_a, tile_a, count_a), (line_b, tile_b, count_b) = spans
-    steps_a = (count_a + parts - 1) // parts
-    steps_b = (count_b + parts - 1) // parts
-
-    def body(step, carry):
-        first = step < steps_a
-        done = parts * jnp.where(first, step, step - steps_a)
-        line = jnp.where(first, line_a, line_b)
-        tile = jnp.where(first, tile_a, tile_b) + 3 * done
-        count = jnp.where(first, count_a, count_b)
-        lines = lines_of(line, count, done, parts, blank)
-        group_block(source, origin, acc, cells_ref, columns_ref, matrix_ref, [(tile, lines)])
-        return carry
-
-    lax.fori_loop(0, steps_a + steps_b, body, 0)
+def lines_of(line, count, parts, blank):
+    return [jnp.where(i < count, line + QUAD * i, blank) for i in range(parts)]
+
+
+def segment(family, low, high, parts, blank):
+    line, tile, count = span(family, low, high)
+    return jnp.clip(tile, low, low + 3), lines_of(line, count, parts, blank)
 
 
 def interior_kernel(owned_ref, cells_ref, columns_ref, matrix_ref, acc_ref):
@@ -177,8 +164,9 @@
     blank = cells_ref.shape[1] - QUAD
     whole = owned_ref.shape[1] + 2 * HALO * LANE
     acc_ref[:, pl.ds(0, whole)] = jnp.zeros((acc_ref.shape[0], whole), jnp.float32)
-    spans = [span(f, 0, tiles - 4) for f in families(tiles)]
-    sweep(owned_ref, 0, acc_ref, cells_ref, columns_ref, matrix_ref, spans, 7, blank)
+    parts = (tiles - 1) // 3
+    inner = [segment(f, 0, tiles - 4, parts, blank) for f in families(tiles)]
+    group_block(owned_ref, 0, acc_ref, cells_ref, columns_ref, matrix_ref, inner)
 
 
 def rest_kernel(
@@ -209,12 +197,11 @@
     field[:, pl.ds(margin, owned)] = owned_ref[...]
     field[:, pl.ds(margin + owned, margin)] = high_ref[...]
 
-    ends = []
-    for low, high in ((-HALO, -1), (tiles - 3, tiles + 2)):
-        for family in families(tiles):
-            line, tile, count = span(family, low, high)
-            tile = jnp.clip(tile, low, high)
-            ends.append((tile, lines_of(line, count, 0, 2, blank)))
+    ends = [
+        segment(family, low, low + HALO - 1, 2, blank)
+        for low in (-HALO, tiles - 3)
+        for family in families(tiles)
+    ]
     group_block(field, HALO, acc, cells_ref, columns_ref, matrix_ref, ends)
 
     chunk = 4 * LANE
@@ -237,8 +224,13 @@
     def _():
         field[:, pl.ds(margin + owned, margin)] = jnp.zeros((states, margin), field.dtype)
 
-    spans = [span(f, -3, tiles - 1) for f in families(tiles)]
-    sweep(field, HALO, acc, cells_ref, columns_ref, matrix_ref, spans, 11, blank)
+    parts = (tiles + 2) // 3
+    own, other = families(tiles)
+    whole_range = [
+        segment(own, -3, tiles - 1, parts + 1, blank),
+        segment(other, -3, tiles - 1, parts, blank),
+    ]
+    group_block(field, HALO, acc, cells_ref, columns_ref, matrix_ref, whole_range)
 
     chunk = 8 * LANE
 
@@ -357,15 +349,28 @@
     )(parts, second)
 
 
-def split_kernel(block_ref, pieces_ref, done):
-    copies = []
-    for i in range(pieces_ref.shape[0]):
-        width = pieces_ref.shape[2]
-        part = block_ref.at[:, pl.ds(i * width, width)]
-        copies.append(pltpu.make_async_copy(part, pieces_ref.at[i], done.at[i]))
-        copies[-1].start()
-    for copy in copies:
-        copy.wait()
+def split_kernel(block_ref, pieces_ref, held, came, went):
+    count, states, width = pieces_ref.shape
+    tall = 8
+    moves = [(i, r) for r in range(0, states, tall) for i in range(count)]
+
+    def arriving(k):
+        i, r = moves[k]
+        part = block_ref.at[pl.ds(r, tall), pl.ds(i * width, width)]
+        return pltpu.make_async_copy(part, held.at[k], came.at[k])
+
+    def leaving(k):
+        i, r = moves[k]
+        part = pieces_ref.at[i, pl.ds(r, tall), :]
+        return pltpu.make_async_copy(held.at[k], part, went.at[k])
+
+    for k in range(len(moves)):
+        arriving(k).start()
+    for k in range(len(moves)):
+        arriving(k).wait()
+        leaving(k).start()
+    for k in range(len(moves)):
+        leaving(k).wait()
 
 
 def join_kernel(pieces_ref, block_ref, done):
@@ -381,12 +386,17 @@
 
 def quarters(block, count):
     shape = (count, block.shape[0], block.shape[1] // count)
+    moves = count * block.shape[0] // 8
     return pl.pallas_call(
         split_kernel,
         out_shape=jax.ShapeDtypeStruct(shape, block.dtype),
         in_specs=[pl.BlockSpec(memory_space=pltpu.HBM)],
         out_specs=pl.BlockSpec(memory_space=pltpu.HBM),
-        scratch_shapes=[pltpu.SemaphoreType.DMA((count,))],
+        scratch_shapes=[
+            pltpu.VMEM((moves, 8, shape[2]), block.dtype),
+            pltpu.SemaphoreType.DMA((moves,)),
+            pltpu.SemaphoreType.DMA((moves,)),
+        ],
         name="quarters",
     )(block)
 

time: 133 us -> 101 us (0.76)
  Pallas kernels: 51.3 us -> 24.6 us
  blocking collectives: 55.3 us -> 49.3 us
    pallas_call x1, Pallas kernels: 32.9 us -> 2.13 us  [quarters(): pl.pallas_call(split_kernel, out_shape=jax.ShapeDtypeStruct(shape, block....]
    all_to_all x1, blocking collectives: 22.2 us -> 16.2 us  [gathered_terms(): lax.all_to_all(jnp.broadcast_to(x[None], (size, *x.shape)), group, 0, 0)]
    pallas_call x1, Pallas kernels: 4.19 us -> 6.85 us  [filtered(): pl.pallas_call(interior_kernel, out_shape=jax.ShapeDtypeStruct((states, f...]
    pallas_call x1, Pallas kernels: 9.76 us -> 11.1 us  [filtered(): pl.pallas_call(rest_kernel, out_shape=(jax.ShapeDtypeStruct((states, coun...]
  transfers between devices with their start and end apart: 5 -> 5, of which waited for: 3 -> 3; matrix products, arithmetic and copies ran while one was open for 1% -> 1% of each run, Pallas kernels for 3% -> 7%
where the time goes in v4:
time: 101 us; the launch traced here: 100 us
  blocking collectives  49.3 us (49%)
  Pallas kernels  24.6 us (24%)
  starting transfers between devices  12.9 us (13%)
  waiting for transfers between devices  11.5 us (11%)
  between operations  1.01 us (1%)
    all_to_all x1, blocking collectives, gathered_terms(): return lax.all_to_all(copies, 'z', 0, 0)  17.3 us
    all_to_all x1, blocking collectives, gathered_terms(): lax.all_to_all(jnp.broadcast_to(x[None], (size, *x.shape)), group, 0, 0)  16.2 us
    all_to_all x1, blocking collectives, per_device(): pieces = lax.all_to_all(pieces, STATE_AXIS, 0, 0)  15.8 us
    pallas_call x1, Pallas kernels, filtered(): pl.pallas_call(rest_kernel, out_shape=(jax.ShapeDtypeStruct((states, coun...  11.1 us
    all_to_all x1, waiting for transfers between devices, per_device(): pieces = lax.all_to_all(pieces, STATE_AXIS, 0, 0)  9.89 us
    pallas_call x1, Pallas kernels, filtered(): pl.pallas_call(interior_kernel, out_shape=jax.ShapeDtypeStruct((states, f...  6.85 us
    all_to_all x1, starting transfers between devices, per_device(): pieces = lax.all_to_all(pieces, STATE_AXIS, 0, 0)  5.77 us
    pallas_call x1, Pallas kernels, orthonormalized(): pl.pallas_call(functools.partial(factor_kernel, total_nodes), out_shape=(...  3.47 us
  transfers between devices with their start and end apart: 5, of which 3 were waited for; matrix products, arithmetic and copies ran while one was open for 1% of the time, Pallas kernels for 7%

profile of v4, /device:TPU:2, one launch (start us, length us, event | category | flops | bytes accessed | tf_op | source)
XLA Modules:
  0.0 100.4 jit_solution(16530619907576372047)
XLA Ops:
  0.6 0.0 copy-start.1
  0.6 0.0 copy-start
  0.6 2.1 %quarters.1 = bf16[4,16,8192]{2,1,0:T(8,128)(2,1)} custom-call(bf16[16,32768]{1,0:T(8,128)(2,1)} %block_ref.1), custom_call_target="tpu_custom_call" | custom-call | tf_op jit(solution)/shard_map/quarters/pallas_call | solution.py:390
  2.8 0.0 copy-start.2
  2.8 5.8 %all-to-all-start = ((bf16[4,16,8192]{2,1,0:T(8,128)(2,1)}), bf16[4,16,8192]{2,1,0:T(8,128)(2,1)S(1)}, u32[]{:S(2)}, u32[]{:S(2)}) async-start(bf16[4,16,8192]{2,1,0:T(8,128)(2,1)} %quarters.1), calls=%async_computation | async-start | bytes 2097152 | tf_op jit(solution)/shard_map/all_to_all | solution.py:442
  8.6 0.0 copy-done
  8.6 0.0 copy-done.1
  8.7 0.1 slice_select_fusion
  8.8 1.3 %collective-permute-start.2 = (f32[2,96,128]{1,2,0:T(8,128)S(1)}, f32[2,96,128]{1,2,0:T(8,128)S(1)}, u32[]{:S(2)}, u32[]{:S(2)}) collective-permute-start(f32[2,96,128]{1,2,0:T(8,128)S(1)} %slice_select_fusion), channel_id=1, source_target_pairs={{0,4},{1,5},{6,2},{7,3},{4,8},{5,9},{10,6},{11,7},{8,12},{9,13},{1... | collective-permute-start | bytes 294920 | tf_op jit(solution)/shard_map/ppermute | solution.py:456
  10.1 0.0 copy-done.2
  10.1 0.1 copy.13
  10.3 0.2 broadcast_multiply_fusion
  10.5 0.1 pad.20.clone
  10.6 0.5 collective-permute-done.2
  11.0 0.1 maximum_maximum_fusion
  11.1 0.2 copy.12.cells_ref
  11.4 9.9 %all-to-all-done = bf16[4,16,8192]{2,1,0:T(8,128)(2,1)S(1)} async-done(((bf16[4,16,8192]{2,1,0:T(8,128)(2,1)}), bf16[4,16,8192]{2,1,0:T(8,128)(2,1)S(1)}, u32[]{:S(2)}, u32[]{:S(2)}) %all-to-all-start) | async-done | bytes 1048608 | tf_op jit(solution)/shard_map/all_to_all | solution.py:442
  21.3 3.4 %collective-permute-start.1 = (bf16[64,768]{1,0:T(8,128)(2,1)S(1)}, bf16[64,768]{1,0:T(8,128)(2,1)S(1)}, u32[]{:S(2)}, u32[]{:S(2)}) collective-permute-start(bf16[64,768]{1,0:T(8,128)(2,1)S(1)} %get-tuple-element.16), channel_id=1, source_target_pairs={{1,0},{2,1},{3,2},{4,3},{5,4},{6,5},{7,6},{8,7},{9,8},{10,9},{11,1... | collective-permute-start | bytes 294920 | tf_op jit(solution)/shard_map/ppermute | solution.py:466
  24.7 2.5 %collective-permute-start = (bf16[64,768]{1,0:T(8,128)(2,1)S(1)}, bf16[64,768]{1,0:T(8,128)(2,1)S(1)}, u32[]{:S(2)}, u32[]{:S(2)}) collective-permute-start(bf16[64,768]{1,0:T(8,128)(2,1)S(1)} %get-tuple-element.17), channel_id=1, source_target_pairs={{0,1},{1,2},{2,3},{3,4},{4,5},{5,6},{6,7},{7,8},{8,9},{9,10},{10,1... | collective-permute-start | bytes 294920 | tf_op jit(solution)/shard_map/ppermute | solution.py:465
  27.2 6.9 %interior.1.acc_ref = f32[64,9984]{1,0:T(8,128)S(1)} custom-call(bf16[64,8192]{1,0:T(8,128)(2,1)S(1)} %bitcast.20, f32[2,640,128]{2,1,0:T(8,128)S(1)} %copy.12.cells_ref, f32[128,640]{1,0:T(8,128)S(1)} %select_maximum_fusion.1.columns_ref, bf16[256,256]{1,0:T(8,128)(2,1)S(1)} %bitcast.23), custom_call_target="tpu_custom_call" | custom-call | flops 20000000000 | bytes 20000000 | tf_op jit(solution)/shard_map/interior/pallas_call | solution.py:256
  34.0 0.0 collective-permute-done.1.high_ref
  34.0 0.0 collective-permute-done.low_ref
  34.0 11.1 %rest.1 = (bf16[64,8192]{1,0:T(8,128)(2,1)S(1)}, f32[32,128]{1,0:T(8,128)S(1)}, f32[64,9984]{1,0:T(8,128)S(1)}) custom-call(bf16[64,8192]{1,0:T(8,128)(2,1)S(1)} %bitcast.21, bf16[64,768]{1,0:T(8,128)(2,1)S(1)} %collective-permute-done.low_ref, bf16[64,768]{1,0:T(8,128)(2,1)S(1)} %collective-permute-done.1.high_ref, ...), custom_call_target="tpu_custom_call", output_to_operand_aliasing={{2}: (6, {})} | custom-call | tf_op jit(solution)/shard_map/rest/pallas_call | solution.py:267
  45.2 0.0 collective-permute-start.3
  45.2 1.2 %collective-permute-done.3 = f32[32,128]{1,0:T(8,128)S(1)} collective-permute-done((f32[32,128]{1,0:T(8,128)S(1)}, f32[32,128]{1,0:T(8,128)S(1)}, u32[]{:S(2)}, u32[]{:S(2)}) %collective-permute-start.3) | collective-permute-done | bytes 16416 | tf_op jit(solution)/shard_map/ppermute | solution.py:418
  46.4 16.2 %all_to_all.20 = f32[16,32,128]{2,1,0:T(8,128)S(1)} all-to-all(f32[16,32,128]{2,1,0:T(8,128)S(1)} %broadcast_in_dim.11), channel_id=1, replica_groups=mesh['z'=8,'y'=4,'core'=2,'x'=4] {'y','x'}, dimensions={0} | all-to-all | bytes 524288 | tf_op jit(solution)/shard_map/all_to_all | solution.py:421
  62.7 17.3 %all_to_all.21.parts_ref = f32[8,32,128]{2,1,0:T(8,128)S(1)} all-to-all(f32[8,32,128]{2,1,0:T(8,128)S(1)} %broadcast_in_dim.12), channel_id=1, replica_groups=mesh['z'=8,'y'=4,'core'=2,'x'=4] {'z'}, dimensions={0} | all-to-all | bytes 262144 | tf_op jit(solution)/shard_map/all_to_all | solution.py:423
  80.0 3.5 %factor.1 = (bf16[64,8192]{1,0:T(8,128)(2,1)S(1)}, f32[64,64]{1,0:T(8,128)}) custom-call(f32[8,32,128]{2,1,0:T(8,128)S(1)} %all_to_all.21.parts_ref, bf16[64,8192]{1,0:T(8,128)(2,1)S(1)} %get-tuple-element.13.second_ref), custom_call_target="tpu_custom_call" | custom-call | tf_op jit(solution)/shard_map/factor/pallas_call | solution.py:339
  83.5 15.8 %all_to_all.22.pieces_ref = bf16[4,16,8192]{2,1,0:T(8,128)(2,1)S(1)} all-to-all(bf16[4,16,8192]{2,1,0:T(8,128)(2,1)S(1)} %bitcast.22), channel_id=1, replica_groups=mesh['z'=8,'y'=4,'core'=2,'x'=4] {'x'}, dimensions={0} | all-to-all | bytes 2097152 | tf_op jit(solution)/shard_map/all_to_all | solution.py:471
  99.3 1.0 joined.1
  (15 shorter events, 0.2 us)
Async XLA Ops:
  0.6 8.0 %copy-start.1 = (f32[125,512]{1,0:T(8,128)S(1)}, f32[125,512]{1,0:T(8,128)}, u32[]{:S(2)}) copy-start(f32[125,512]{1,0:T(8,128)} %param.6) | copy-start | bytes 768004
  0.6 7.9 %copy-start = (s32[125,512]{1,0:T(8,128)S(1)}, s32[125,512]{1,0:T(8,128)}, u32[]{:S(2)}) copy-start(s32[125,512]{1,0:T(8,128)} %param.5) | copy-start | bytes 768004
  2.8 7.3 %copy-start.2 = (bf16[125,125]{1,0:T(8,128)(2,1)S(1)}, bf16[125,125]{1,0:T(8,128)(2,1)}, u32[]{:S(2)}) copy-start(bf16[125,125]{1,0:T(8,128)(2,1)} %param.7) | copy-start | bytes 93754
  2.8 18.5 %all-to-all-start = ((bf16[4,16,8192]{2,1,0:T(8,128)(2,1)}), bf16[4,16,8192]{2,1,0:T(8,128)(2,1)S(1)}, u32[]{:S(2)}, u32[]{:S(2)}) async-start(bf16[4,16,8192]{2,1,0:T(8,128)(2,1)} %quarters.1), calls=%async_computation | async-start | bytes 2097152 | tf_op jit(solution)/shard_map/all_to_all | solution.py:442
  8.8 2.3 %collective-permute-start.2 = (f32[2,96,128]{1,2,0:T(8,128)S(1)}, f32[2,96,128]{1,2,0:T(8,128)S(1)}, u32[]{:S(2)}, u32[]{:S(2)}) collective-permute-start(f32[2,96,128]{1,2,0:T(8,128)S(1)} %slice_select_fusion), channel_id=1, source_target_pairs={{0,4},{1,5},{6,2},{7,3},{4,8},{5,9},{10,6},{11,7},{8,12},{9,13},{1... | collective-permute-start | bytes 294920 | tf_op jit(solution)/shard_map/ppermute | solution.py:456
  21.3 12.7 %collective-permute-start.1 = (bf16[64,768]{1,0:T(8,128)(2,1)S(1)}, bf16[64,768]{1,0:T(8,128)(2,1)S(1)}, u32[]{:S(2)}, u32[]{:S(2)}) collective-permute-start(bf16[64,768]{1,0:T(8,128)(2,1)S(1)} %get-tuple-element.16), channel_id=1, source_target_pairs={{1,0},{2,1},{3,2},{4,3},{5,4},{6,5},{7,6},{8,7},{9,8},{10,9},{11,1... | collective-permute-start | bytes 294920 | tf_op jit(solution)/shard_map/ppermute | solution.py:466
  24.7 9.4 %collective-permute-start = (bf16[64,768]{1,0:T(8,128)(2,1)S(1)}, bf16[64,768]{1,0:T(8,128)(2,1)S(1)}, u32[]{:S(2)}, u32[]{:S(2)}) collective-permute-start(bf16[64,768]{1,0:T(8,128)(2,1)S(1)} %get-tuple-element.17), channel_id=1, source_target_pairs={{0,1},{1,2},{2,3},{3,4},{4,5},{5,6},{6,7},{7,8},{8,9},{9,10},{10,1... | collective-permute-start | bytes 294920 | tf_op jit(solution)/shard_map/ppermute | solution.py:465
  45.2 1.2 %collective-permute-start.3 = (f32[32,128]{1,0:T(8,128)S(1)}, f32[32,128]{1,0:T(8,128)S(1)}, u32[]{:S(2)}, u32[]{:S(2)}) collective-permute-start(f32[32,128]{1,0:T(8,128)S(1)} %get-tuple-element.12), channel_id=1, source_target_pairs={{0,4},{4,0},{1,5},{5,1},{2,6},{6,2},{3,7},{7,3},{8,12},{12,8},{9,1... | collective-permute-start | bytes 49160 | tf_op jit(solution)/shard_map/ppermute | solution.py:418

commit v5 on v4

--- a/solution.py
+++ b/solution.py
@@ -159,30 +159,39 @@
     return jnp.clip(tile, low, low + 3), lines_of(line, count, parts, blank)
 
 
-def interior_kernel(owned_ref, cells_ref, columns_ref, matrix_ref, acc_ref):
-    tiles = owned_ref.shape[1] // LANE
+def interior_kernel(ends_ref, middle_ref, cells_ref, columns_ref, matrix_ref, acc_ref, window_ref):
+    margin = HALO * LANE
+    inner = middle_ref.shape[1]
+    whole = window_ref.shape[1]
+    tiles = inner // LANE + 2 * HALO
     blank = cells_ref.shape[1] - QUAD
-    whole = owned_ref.shape[1] + 2 * HALO * LANE
+    window_ref[:, pl.ds(margin, margin)] = ends_ref[:, pl.ds(0, margin)]
+    window_ref[:, pl.ds(2 * margin, inner)] = middle_ref[...]
+    window_ref[:, pl.ds(2 * margin + inner, margin)] = ends_ref[:, pl.ds(margin, margin)]
+    nothing = jnp.zeros((window_ref.shape[0], margin), window_ref.dtype)
+    window_ref[:, pl.ds(0, margin)] = nothing
+    window_ref[:, pl.ds(whole - margin, margin)] = nothing
     acc_ref[:, pl.ds(0, whole)] = jnp.zeros((acc_ref.shape[0], whole), jnp.float32)
     parts = (tiles - 1) // 3
-    inner = [segment(f, 0, tiles - 4, parts, blank) for f in families(tiles)]
-    group_block(owned_ref, 0, acc_ref, cells_ref, columns_ref, matrix_ref, inner)
+    inner_range = [segment(f, 0, tiles - 4, parts, blank) for f in families(tiles)]
+    group_block(window_ref, HALO, acc_ref, cells_ref, columns_ref, matrix_ref, inner_range)
 
 
 def rest_kernel(
-    owned_ref,
     low_ref,
     high_ref,
     cells_ref,
     columns_ref,
     matrix_ref,
     acc_ref,
+    window_ref,
     second_ref,
     gram_ref,
     sum_ref,
+    start_ref,
     field,
 ):
-    states, owned = owned_ref.shape
+    states, owned = second_ref.shape
     tiles = owned // LANE
     margin = HALO * LANE
     blank = cells_ref.shape[1] - QUAD
@@ -193,23 +202,22 @@
         slab = slab * lax.axis_size(axis) + lax.axis_index(axis)
         slabs = slabs * lax.axis_size(axis)
     acc = sum_ref
-    field[:, pl.ds(0, margin)] = low_ref[...]
-    field[:, pl.ds(margin, owned)] = owned_ref[...]
-    field[:, pl.ds(margin + owned, margin)] = high_ref[...]
+    start_ref[:, pl.ds(0, margin)] = low_ref[...]
+    start_ref[:, pl.ds(margin + owned, margin)] = high_ref[...]
 
     ends = [
         segment(family, low, low + HALO - 1, 2, blank)
         for low in (-HALO, tiles - 3)
         for family in families(tiles)
     ]
-    group_block(field, HALO, acc, cells_ref, columns_ref, matrix_ref, ends)
+    group_block(start_ref, HALO, acc, cells_ref, columns_ref, matrix_ref, ends)
 
     chunk = 4 * LANE
     whole = owned + 2 * margin
 
     def to_first(step, carry):
         here = pl.ds(pl.multiple_of(step * chunk, LANE), chunk)
-        start = field[:, here].astype(jnp.float32)
+        start = start_ref[:, here].astype(jnp.float32)
         field[:, here] = ((acc[:, here] - CENTER * start) * (1.0 / HALF_WIDTH)).astype(field.dtype)
         acc[:, here] = jnp.zeros((states, chunk), jnp.float32)
         return carry
@@ -238,7 +246,7 @@
         at = pl.multiple_of(step * chunk, LANE)
         here = pl.ds(pl.multiple_of(at + margin, LANE), chunk)
         image = acc[:, here] - CENTER * field[:, here].astype(jnp.float32)
-        start = owned_ref[:, pl.ds(at, chunk)].astype(jnp.float32)
+        start = start_ref[:, here].astype(jnp.float32)
         second = (image * (2.0 / HALF_WIDTH) - start).astype(second_ref.dtype)
         second_ref[:, pl.ds(at, chunk)] = second
         return gram + lax.dot_general(
@@ -249,35 +257,38 @@
     gram_ref[...] = jnp.concatenate([gram[: states // 2], gram[states // 2 :]], axis=1)
 
 
-def filtered(owned, low, high, cells, columns, matrix):
-    states, count = owned.shape
-    full = count + (2 * HALO + SPARE) * LANE
+def filtered(ends, middle, low, high, cells, columns, matrix):
+    states, count = ends.shape[0], ends.shape[1] + middle.shape[1]
+    width = count + 2 * HALO * LANE
+    total = jax.ShapeDtypeStruct((states, width + SPARE * LANE), jnp.float32)
+    window = jax.ShapeDtypeStruct((states, width), ends.dtype)
     params = pltpu.CompilerParams(vmem_limit_bytes=24 << 20)
-    acc = pl.pallas_call(
+    acc, start = pl.pallas_call(
         interior_kernel,
-        out_shape=jax.ShapeDtypeStruct((states, full), jnp.float32),
-        in_specs=[VMEM] * 4,
-        out_specs=VMEM,
+        out_shape=(total, window),
+        in_specs=[VMEM] * 5,
+        out_specs=[VMEM] * 2,
         compiler_params=params,
         cost_estimate=pl.CostEstimate(
             flops=20_000_000_000, bytes_accessed=20_000_000, transcendentals=0
         ),
         name="interior",
-    )(owned, cells, columns, matrix)
-    second, gram, unused = pl.pallas_call(
+    )(ends, middle, cells, columns, matrix)
+    second, gram, *unused = pl.pallas_call(
         rest_kernel,
         out_shape=(
-            jax.ShapeDtypeStruct((states, count), owned.dtype),
+            jax.ShapeDtypeStruct((states, count), ends.dtype),
             jax.ShapeDtypeStruct((states // 2, 2 * states), jnp.float32),
-            jax.ShapeDtypeStruct((states, full), jnp.float32),
+            total,
+            window,
         ),
         in_specs=[VMEM] * 7,
-        out_specs=[VMEM] * 3,
-        input_output_aliases={6: 2},
-        scratch_shapes=[pltpu.VMEM((states, count + 2 * HALO * LANE), owned.dtype)],
+        out_specs=[VMEM] * 4,
+        input_output_aliases={5: 2, 6: 3},
+        scratch_shapes=[pltpu.VMEM((states, width), ends.dtype)],
         compiler_params=params,
         name="rest",
-    )(owned, low, high, cells, columns, matrix, acc)
+    )(low, high, cells, columns, matrix, acc, start)
     return second, gram
 
 
@@ -349,8 +360,10 @@
     )(parts, second)
 
 
-def split_kernel(block_ref, pieces_ref, held, came, went):
-    count, states, width = pieces_ref.shape
+def split_kernel(block_ref, ends_ref, middle_ref, held, came, went):
+    count, states, inner = middle_ref.shape
+    margin = ends_ref.shape[2] // 2
+    width = inner + 2 * margin
     tall = 8
     moves = [(i, r) for r in range(0, states, tall) for i in range(count)]
 
@@ -361,16 +374,27 @@
 
     def leaving(k):
         i, r = moves[k]
-        part = pieces_ref.at[i, pl.ds(r, tall), :]
-        return pltpu.make_async_copy(held.at[k], part, went.at[k])
+        low, high = pl.ds(0, margin), pl.ds(margin, margin)
+        last = pl.ds(margin + inner, margin)
+        pairs = [
+            (held.at[k, :, low], ends_ref.at[i, pl.ds(r, tall), low]),
+            (held.at[k, :, last], ends_ref.at[i, pl.ds(r, tall), high]),
+            (held.at[k, :, pl.ds(margin, inner)], middle_ref.at[i, pl.ds(r, tall), :]),
+        ]
+        return [
+            pltpu.make_async_copy(part, target, went.at[k, j])
+            for j, (part, target) in enumerate(pairs)
+        ]
 
     for k in range(len(moves)):
         arriving(k).start()
     for k in range(len(moves)):
         arriving(k).wait()
-        leaving(k).start()
+        for copy in leaving(k):
+            copy.start()
     for k in range(len(moves)):
-        leaving(k).wait()
+        for copy in leaving(k):
+            copy.wait()
 
 
 def join_kernel(pieces_ref, block_ref, done):
@@ -385,17 +409,21 @@
 
 
 def quarters(block, count):
-    shape = (count, block.shape[0], block.shape[1] // count)
-    moves = count * block.shape[0] // 8
+    states, width = block.shape[0], block.shape[1] // count
+    margin = HALO * LANE
+    moves = count * states // 8
     return pl.pallas_call(
         split_kernel,
-        out_shape=jax.ShapeDtypeStruct(shape, block.dtype),
+        out_shape=(
+            jax.ShapeDtypeStruct((count, states, 2 * margin), block.dtype),
+            jax.ShapeDtypeStruct((count, states, width - 2 * margin), block.dtype),
+        ),
         in_specs=[pl.BlockSpec(memory_space=pltpu.HBM)],
-        out_specs=pl.BlockSpec(memory_space=pltpu.HBM),
+        out_specs=[pl.BlockSpec(memory_space=pltpu.HBM)] * 2,
         scratch_shapes=[
-            pltpu.VMEM((moves, 8, shape[2]), block.dtype),
+            pltpu.VMEM((moves, 8, width), block.dtype),
             pltpu.SemaphoreType.DMA((moves,)),
-            pltpu.SemaphoreType.DMA((moves,)),
+            pltpu.SemaphoreType.DMA((moves, 3)),
         ],
         name="quarters",
     )(block)
@@ -436,11 +464,11 @@
     everyone = (*NODE_AXES, STATE_AXIS)
     margin = HALO * LANE
 
-    pieces, connectivity, potential = lax.optimization_barrier(
-        (quarters(block, slots), connectivity, potential)
+    ends, middle, connectivity, potential = lax.optimization_barrier(
+        (*quarters(block, slots), connectivity, potential)
     )
-    pieces = lax.all_to_all(pieces, STATE_AXIS, 0, 0)
-    owned = pieces.reshape(-1, pieces.shape[2])
+    ends = lax.all_to_all(ends, STATE_AXIS, 0, 0).reshape(-1, ends.shape[2])
+    middle = lax.all_to_all(middle, STATE_AXIS, 0, 0).reshape(-1, middle.shape[2])
 
     stride = 3 * LANE // QUAD
     local = connectivity - (jnp.arange(cells, dtype=jnp.int32) * stride + ABSENT)[None, :]
@@ -462,9 +490,9 @@
     matrix = jnp.pad(cell_matrix.T, ((0, LANE - nodes), (0, LANE - nodes)))
     matrix = jnp.kron(jnp.eye(2, dtype=matrix.dtype), matrix)
 
-    low = lax.ppermute(owned[:, -margin:], everyone, neighbour_route(slabs, slots, True))
-    high = lax.ppermute(owned[:, :margin], everyone, neighbour_route(slabs, slots, False))
-    second, gram = filtered(owned, low, high, lines, columns, matrix)
+    low = lax.ppermute(ends[:, margin:], everyone, neighbour_route(slabs, slots, True))
+    high = lax.ppermute(ends[:, :margin], everyone, neighbour_route(slabs, slots, False))
+    second, gram = filtered(ends, middle, low, high, lines, columns, matrix)
     parts = gathered_terms(gram)
     orthonormal, factor = orthonormalized(parts, second, block.shape[1] * slabs)
     pieces = orthonormal.reshape(slots, -1, orthonormal.shape[1])

time: 101 us -> 102 us (level)
  starting transfers between devices: 12.9 us -> 17.7 us
  blocking collectives: 49.3 us -> 46.2 us
  waiting for transfers between devices: 11.5 us -> 8.76 us
  other arithmetic: 0.48 us -> 2.38 us
    all_to_all x1 -> x2, starting transfers between devices: 5.77 us -> 10.5 us  [the longest x1 5.61 us: per_device(): ends = lax.all_to_all(ends, STATE_AXIS, 0, 0).reshape(-1, ends.shape[2])]
    all_to_all x1, blocking collectives: 16.2 us -> 13.3 us  [gathered_terms(): lax.all_to_all(jnp.broadcast_to(x[None], (size, *x.shape)), group, 0, 0)]
    all_to_all x1 -> x2, waiting for transfers between devices: 9.89 us -> 7.58 us  [the longest x1 6.59 us: per_device(): lax.all_to_all(middle, STATE_AXIS, 0, 0).reshape(-1, middle.shape[2])]
    another operation x2, other arithmetic: 0.06 us -> 1.96 us  [per_device(): lines = jnp.stack([local.astype(jnp.float32).T, potential.T])]
  transfers between devices with their start and end apart: 5 -> 6, of which waited for: 3 -> 3; matrix products, arithmetic and copies ran while one was open for 1% -> 3% of each run, Pallas kernels for 7% -> 7%
where the time goes in v5:
time: 102 us; the launch traced here: 101 us
  blocking collectives  46.2 us (45%)
  Pallas kernels  24.8 us (24%)
  starting transfers between devices  17.7 us (17%)
  waiting for transfers between devices  8.76 us (9%)
  other arithmetic  2.38 us (2%)
    all_to_all x1, blocking collectives, gathered_terms(): return lax.all_to_all(copies, 'z', 0, 0)  17.3 us
    all_to_all x1, blocking collectives, per_device(): pieces = lax.all_to_all(pieces, STATE_AXIS, 0, 0)  15.5 us
    all_to_all x1, blocking collectives, gathered_terms(): lax.all_to_all(jnp.broadcast_to(x[None], (size, *x.shape)), group, 0, 0)  13.3 us
    pallas_call x1, Pallas kernels, filtered(): pl.pallas_call(rest_kernel, out_shape=(jax.ShapeDtypeStruct((states, coun...  11.1 us
    pallas_call x1, Pallas kernels, filtered(): pl.pallas_call(interior_kernel, out_shape=(total, window), in_specs=[VMEM...  6.93 us
    all_to_all x1, waiting for transfers between devices, per_device(): lax.all_to_all(middle, STATE_AXIS, 0, 0).reshape(-1, middle.shape[2])  6.59 us
    all_to_all x1, starting transfers between devices, per_device(): ends = lax.all_to_all(ends, STATE_AXIS, 0, 0).reshape(-1, ends.shape[2])  5.61 us
    all_to_all x1, starting transfers between devices, per_device(): lax.all_to_all(middle, STATE_AXIS, 0, 0).reshape(-1, middle.shape[2])  4.93 us
  transfers between devices with their start and end apart: 6, of which 3 were waited for; matrix products, arithmetic and copies ran while one was open for 3% of the time, Pallas kernels for 7%

profile of v5, /device:TPU:2, one launch (start us, length us, event | category | flops | bytes accessed | tf_op | source)
XLA Modules:
  0.0 101.4 jit_solution(12248913729933335543)
XLA Ops:
  0.6 0.0 copy-start
  0.6 0.0 copy-start.1
  0.7 2.3 %quarters.1 = (bf16[4,16,1536]{2,1,0:T(8,128)(2,1)}, bf16[4,16,6656]{2,1,0:T(8,128)(2,1)}) custom-call(bf16[16,32768]{1,0:T(8,128)(2,1)} %block_ref.1), custom_call_target="tpu_custom_call" | custom-call | tf_op jit(solution)/shard_map/quarters/pallas_call | solution.py:415
  2.9 5.6 %all-to-all-start = ((bf16[4,16,1536]{2,1,0:T(8,128)(2,1)}), bf16[4,16,1536]{2,1,0:T(8,128)(2,1)S(1)}, u32[]{:S(2)}, u32[]{:S(2)}) async-start(bf16[4,16,1536]{2,1,0:T(8,128)(2,1)} %get-tuple-element.16), calls=%async_computation | async-start | bytes 393216 | tf_op jit(solution)/shard_map/all_to_all | solution.py:470
  8.5 1.0 fusion.2
  9.5 1.0 select_maximum_fusion
  10.5 0.1 slice_select_fusion
  10.6 1.3 %collective-permute-start.2 = (f32[2,96,128]{1,2,0:T(8,128)S(1)}, f32[2,96,128]{1,2,0:T(8,128)S(1)}, u32[]{:S(2)}, u32[]{:S(2)}) collective-permute-start(f32[2,96,128]{1,2,0:T(8,128)S(1)} %slice_select_fusion), channel_id=1, source_target_pairs={{0,4},{1,5},{6,2},{7,3},{4,8},{5,9},{10,6},{11,7},{8,12},{9,13},{1... | collective-permute-start | bytes 294920 | tf_op jit(solution)/shard_map/ppermute | solution.py:484
  11.9 0.0 copy-done
  12.0 0.0 copy-done.1
  12.0 0.1 copy.14
  12.1 0.2 broadcast_multiply_fusion
  12.3 0.1 pad.20.clone
  12.4 1.0 all-to-all-done
  13.4 4.9 %all-to-all-start.1 = ((bf16[4,16,6656]{2,1,0:T(8,128)(2,1)}), bf16[4,16,6656]{2,1,0:T(8,128)(2,1)S(1)}, u32[]{:S(2)}, u32[]{:S(2)}) async-start(bf16[4,16,6656]{2,1,0:T(8,128)(2,1)} %get-tuple-element.19), calls=%async_computation.1 | async-start | bytes 1703936 | tf_op jit(solution)/shard_map/all_to_all | solution.py:471
  18.3 0.0 collective-permute-done.2
  18.3 0.1 maximum_maximum_fusion
  18.4 0.2 copy.13.cells_ref
  18.7 2.0 %collective-permute-start.1 = (bf16[64,768]{1,0:T(8,128)(2,1)S(1)}, bf16[64,768]{1,0:T(8,128)(2,1)S(1)}, u32[]{:S(2)}, u32[]{:S(2)}) collective-permute-start(bf16[64,768]{1,0:T(8,128)(2,1)S(1)} %get-tuple-element.26), channel_id=1, source_target_pairs={{1,0},{2,1},{3,2},{4,3},{5,4},{6,5},{7,6},{8,7},{9,8},{10,9},{11,1... | collective-permute-start | bytes 294920 | tf_op jit(solution)/shard_map/ppermute | solution.py:494
  20.7 3.9 %collective-permute-start = (bf16[64,768]{1,0:T(8,128)(2,1)S(1)}, bf16[64,768]{1,0:T(8,128)(2,1)S(1)}, u32[]{:S(2)}, u32[]{:S(2)}) collective-permute-start(bf16[64,768]{1,0:T(8,128)(2,1)S(1)} %get-tuple-element.27), channel_id=1, source_target_pairs={{0,1},{1,2},{2,3},{3,4},{4,5},{5,6},{6,7},{7,8},{8,9},{9,10},{10,1... | collective-permute-start | bytes 294920 | tf_op jit(solution)/shard_map/ppermute | solution.py:493
  24.6 6.6 %all-to-all-done.1 = bf16[4,16,6656]{2,1,0:T(8,128)(2,1)S(1)} async-done(((bf16[4,16,6656]{2,1,0:T(8,128)(2,1)}), bf16[4,16,6656]{2,1,0:T(8,128)(2,1)S(1)}, u32[]{:S(2)}, u32[]{:S(2)}) %all-to-all-start.1) | async-done | bytes 852000 | tf_op jit(solution)/shard_map/all_to_all | solution.py:471
  31.2 6.9 %interior.1 = (f32[64,9984]{1,0:T(8,128)S(1)}, bf16[64,9728]{1,0:T(8,128)(2,1)S(1)}) custom-call(bf16[64,1536]{1,0:T(8,128)(2,1)S(1)} %bitcast.23, bf16[64,6656]{1,0:T(8,128)(2,1)S(1)} %bitcast.21, f32[2,640,128]{2,1,0:T(8,128)S(1)} %copy.13.cells_ref, f32[128,640]{1,0:T(8,128)S(1)} %select_maximum_fusion.1.columns_ref, bf16[256,256]{1,0:T(8,128)(2,1)S(1)} %bitcast.24), custom_call_target="tpu_custom_call" | custom-call | flops 20000000000 | bytes 20000000 | tf_op jit(solution)/shard_map/interior/pallas_call | solution.py:266
  38.1 0.0 collective-permute-done.1.high_ref
  38.1 0.0 collective-permute-done.low_ref
  38.1 11.1 %rest.1 = (bf16[64,8192]{1,0:T(8,128)(2,1)S(1)}, f32[32,128]{1,0:T(8,128)S(1)}, f32[64,9984]{1,0:T(8,128)S(1)}, bf16[64,9728]{1,0:T(8,128)(2,1)S(1)}) custom-call(bf16[64,768]{1,0:T(8,128)(2,1)S(1)} %collective-permute-done.low_ref, bf16[64,768]{1,0:T(8,128)(2,1)S(1)} %collective-permute-done.1.high_ref, ...), custom_call_target="tpu_custom_call", output_to_operand_aliasing={{2}: (5, {}), {3}: (6, {})} | custom-call | tf_op jit(solution)/shard_map/rest/pallas_call | solution.py:277
  49.2 0.0 collective-permute-start.3
  49.3 1.2 %collective-permute-done.3 = f32[32,128]{1,0:T(8,128)S(1)} collective-permute-done((f32[32,128]{1,0:T(8,128)S(1)}, f32[32,128]{1,0:T(8,128)S(1)}, u32[]{:S(2)}, u32[]{:S(2)}) %collective-permute-start.3) | collective-permute-done | bytes 16416 | tf_op jit(solution)/shard_map/ppermute | solution.py:446
  50.5 13.3 %all_to_all.25 = f32[16,32,128]{2,1,0:T(8,128)S(1)} all-to-all(f32[16,32,128]{2,1,0:T(8,128)S(1)} %broadcast_in_dim.11), channel_id=1, replica_groups=mesh['z'=8,'y'=4,'core'=2,'x'=4] {'y','x'}, dimensions={0} | all-to-all | bytes 524288 | tf_op jit(solution)/shard_map/all_to_all | solution.py:449
  63.9 17.3 %all_to_all.26.parts_ref = f32[8,32,128]{2,1,0:T(8,128)S(1)} all-to-all(f32[8,32,128]{2,1,0:T(8,128)S(1)} %broadcast_in_dim.12), channel_id=1, replica_groups=mesh['z'=8,'y'=4,'core'=2,'x'=4] {'z'}, dimensions={0} | all-to-all | bytes 262144 | tf_op jit(solution)/shard_map/all_to_all | solution.py:451
  81.2 3.5 %factor.1 = (bf16[64,8192]{1,0:T(8,128)(2,1)S(1)}, f32[64,64]{1,0:T(8,128)}) custom-call(f32[8,32,128]{2,1,0:T(8,128)S(1)} %all_to_all.26.parts_ref, bf16[64,8192]{1,0:T(8,128)(2,1)S(1)} %get-tuple-element.23.second_ref), custom_call_target="tpu_custom_call" | custom-call | tf_op jit(solution)/shard_map/factor/pallas_call | solution.py:350
  84.7 15.5 %all_to_all.27.pieces_ref = bf16[4,16,8192]{2,1,0:T(8,128)(2,1)S(1)} all-to-all(bf16[4,16,8192]{2,1,0:T(8,128)(2,1)S(1)} %bitcast.20), channel_id=1, replica_groups=mesh['z'=8,'y'=4,'core'=2,'x'=4] {'x'}, dimensions={0} | all-to-all | bytes 2097152 | tf_op jit(solution)/shard_map/all_to_all | solution.py:499
  100.2 1.0 joined.1
  (13 shorter events, 0.2 us)
Async XLA Ops:
  0.6 11.3 %copy-start = (s32[125,512]{1,0:T(8,128)S(1)}, s32[125,512]{1,0:T(8,128)}, u32[]{:S(2)}) copy-start(s32[125,512]{1,0:T(8,128)} %param.5) | copy-start | bytes 768004
  0.6 11.3 %copy-start.1 = (bf16[125,125]{1,0:T(8,128)(2,1)S(1)}, bf16[125,125]{1,0:T(8,128)(2,1)}, u32[]{:S(2)}) copy-start(bf16[125,125]{1,0:T(8,128)(2,1)} %param.7) | copy-start | bytes 93754
  2.9 10.5 %all-to-all-start = ((bf16[4,16,1536]{2,1,0:T(8,128)(2,1)}), bf16[4,16,1536]{2,1,0:T(8,128)(2,1)S(1)}, u32[]{:S(2)}, u32[]{:S(2)}) async-start(bf16[4,16,1536]{2,1,0:T(8,128)(2,1)} %get-tuple-element.16), calls=%async_computation | async-start | bytes 393216 | tf_op jit(solution)/shard_map/all_to_all | solution.py:470
  10.6 7.7 %collective-permute-start.2 = (f32[2,96,128]{1,2,0:T(8,128)S(1)}, f32[2,96,128]{1,2,0:T(8,128)S(1)}, u32[]{:S(2)}, u32[]{:S(2)}) collective-permute-start(f32[2,96,128]{1,2,0:T(8,128)S(1)} %slice_select_fusion), channel_id=1, source_target_pairs={{0,4},{1,5},{6,2},{7,3},{4,8},{5,9},{10,6},{11,7},{8,12},{9,13},{1... | collective-permute-start | bytes 294920 | tf_op jit(solution)/shard_map/ppermute | solution.py:484
  13.4 17.8 %all-to-all-start.1 = ((bf16[4,16,6656]{2,1,0:T(8,128)(2,1)}), bf16[4,16,6656]{2,1,0:T(8,128)(2,1)S(1)}, u32[]{:S(2)}, u32[]{:S(2)}) async-start(bf16[4,16,6656]{2,1,0:T(8,128)(2,1)} %get-tuple-element.19), calls=%async_computation.1 | async-start | bytes 1703936 | tf_op jit(solution)/shard_map/all_to_all | solution.py:471
  18.7 19.4 %collective-permute-start.1 = (bf16[64,768]{1,0:T(8,128)(2,1)S(1)}, bf16[64,768]{1,0:T(8,128)(2,1)S(1)}, u32[]{:S(2)}, u32[]{:S(2)}) collective-permute-start(bf16[64,768]{1,0:T(8,128)(2,1)S(1)} %get-tuple-element.26), channel_id=1, source_target_pairs={{1,0},{2,1},{3,2},{4,3},{5,4},{6,5},{7,6},{8,7},{9,8},{10,9},{11,1... | collective-permute-start | bytes 294920 | tf_op jit(solution)/shard_map/ppermute | solution.py:494
  20.7 17.4 %collective-permute-start = (bf16[64,768]{1,0:T(8,128)(2,1)S(1)}, bf16[64,768]{1,0:T(8,128)(2,1)S(1)}, u32[]{:S(2)}, u32[]{:S(2)}) collective-permute-start(bf16[64,768]{1,0:T(8,128)(2,1)S(1)} %get-tuple-element.27), channel_id=1, source_target_pairs={{0,1},{1,2},{2,3},{3,4},{4,5},{5,6},{6,7},{7,8},{8,9},{9,10},{10,1... | collective-permute-start | bytes 294920 | tf_op jit(solution)/shard_map/ppermute | solution.py:493
  49.2 1.2 %collective-permute-start.3 = (f32[32,128]{1,0:T(8,128)S(1)}, f32[32,128]{1,0:T(8,128)S(1)}, u32[]{:S(2)}, u32[]{:S(2)}) collective-permute-start(f32[32,128]{1,0:T(8,128)S(1)} %get-tuple-element.22), channel_id=1, source_target_pairs={{0,4},{4,0},{1,5},{5,1},{2,6},{6,2},{3,7},{7,3},{8,12},{12,8},{9,1... | collective-permute-start | bytes 49160 | tf_op jit(solution)/shard_map/ppermute | solution.py:446

commit v6 on v5

--- a/solution.py
+++ b/solution.py
@@ -360,41 +360,30 @@
     )(parts, second)
 
 
-def split_kernel(block_ref, ends_ref, middle_ref, held, came, went):
-    count, states, inner = middle_ref.shape
-    margin = ends_ref.shape[2] // 2
-    width = inner + 2 * margin
+def cut_kernel(spans, block_ref, pieces_ref, held, came, went):
+    count, states, width = pieces_ref.shape
+    quarter = block_ref.shape[1] // count
     tall = 8
-    moves = [(i, r) for r in range(0, states, tall) for i in range(count)]
-
-    def arriving(k):
-        i, r = moves[k]
-        part = block_ref.at[pl.ds(r, tall), pl.ds(i * width, width)]
-        return pltpu.make_async_copy(part, held.at[k], came.at[k])
-
-    def leaving(k):
-        i, r = moves[k]
-        low, high = pl.ds(0, margin), pl.ds(margin, margin)
-        last = pl.ds(margin + inner, margin)
-        pairs = [
-            (held.at[k, :, low], ends_ref.at[i, pl.ds(r, tall), low]),
-            (held.at[k, :, last], ends_ref.at[i, pl.ds(r, tall), high]),
-            (held.at[k, :, pl.ds(margin, inner)], middle_ref.at[i, pl.ds(r, tall), :]),
-        ]
-        return [
-            pltpu.make_async_copy(part, target, went.at[k, j])
-            for j, (part, target) in enumerate(pairs)
-        ]
-
-    for k in range(len(moves)):
-        arriving(k).start()
-    for k in range(len(moves)):
-        arriving(k).wait()
-        for copy in leaving(k):
-            copy.start()
-    for k in range(len(moves)):
-        for copy in leaving(k):
-            copy.wait()
+    arriving, leaving = [], []
+    for r in range(0, states, tall):
+        for i in range(count):
+            k = len(leaving)
+            at = 0
+            for j, (begin, size) in enumerate(spans):
+                part = block_ref.at[pl.ds(r, tall), pl.ds(i * quarter + begin, size)]
+                place = held.at[k, :, pl.ds(at, size)]
+                arriving.append(pltpu.make_async_copy(part, place, came.at[k, j]))
+                at += size
+            piece = pieces_ref.at[i, pl.ds(r, tall), :]
+            leaving.append(pltpu.make_async_copy(held.at[k], piece, went.at[k]))
+    for copy in arriving:
+        copy.start()
+    for k, copy in enumerate(leaving):
+        for j in range(len(spans)):
+            arriving[k * len(spans) + j].wait()
+        copy.start()
+    for copy in leaving:
+        copy.wait()
 
 
 def join_kernel(pieces_ref, block_ref, done):
@@ -408,24 +397,20 @@
         copy.wait()
 
 
-def quarters(block, count):
-    states, width = block.shape[0], block.shape[1] // count
-    margin = HALO * LANE
+def cut(block, count, spans, name):
+    states, width = block.shape[0], sum(size for begin, size in spans)
     moves = count * states // 8
     return pl.pallas_call(
-        split_kernel,
-        out_shape=(
-            jax.ShapeDtypeStruct((count, states, 2 * margin), block.dtype),
-            jax.ShapeDtypeStruct((count, states, width - 2 * margin), block.dtype),
-        ),
+        functools.partial(cut_kernel, spans),
+        out_shape=jax.ShapeDtypeStruct((count, states, width), block.dtype),
         in_specs=[pl.BlockSpec(memory_space=pltpu.HBM)],
-        out_specs=[pl.BlockSpec(memory_space=pltpu.HBM)] * 2,
+        out_specs=pl.BlockSpec(memory_space=pltpu.HBM),
         scratch_shapes=[
             pltpu.VMEM((moves, 8, width), block.dtype),
+            pltpu.SemaphoreType.DMA((moves, len(spans))),
             pltpu.SemaphoreType.DMA((moves,)),
-            pltpu.SemaphoreType.DMA((moves, 3)),
         ],
-        name="quarters",
+        name=name,
     )(block)
 
 
@@ -464,10 +449,12 @@
     everyone = (*NODE_AXES, STATE_AXIS)
     margin = HALO * LANE
 
-    ends, middle, connectivity, potential = lax.optimization_barrier(
-        (*quarters(block, slots), connectivity, potential)
-    )
+    quarter = block.shape[1] // slots
+    ends = cut(block, slots, ((0, margin), (quarter - margin, margin)), "ends")
+    ends, block = lax.optimization_barrier((ends, block))
+    middle = cut(block, slots, ((margin, quarter - 2 * margin),), "middle")
     ends = lax.all_to_all(ends, STATE_AXIS, 0, 0).reshape(-1, ends.shape[2])
+    ends, connectivity, potential = lax.optimization_barrier((ends, connectivity, potential))
     middle = lax.all_to_all(middle, STATE_AXIS, 0, 0).reshape(-1, middle.shape[2])
 
     stride = 3 * LANE // QUAD

time: 102 us -> 102 us (level)
  waiting for transfers between devices: 8.76 us -> 5.74 us
  blocking collectives: 46.2 us -> 48.8 us
  other arithmetic: 2.38 us -> 0.48 us
  Pallas kernels: 24.8 us -> 26.2 us
    all_to_all x1, waiting for transfers between devices: 6.59 us -> 2.93 us  [per_device(): lax.all_to_all(middle, STATE_AXIS, 0, 0).reshape(-1, middle.shape[2])]
    all_to_all x1, blocking collectives: 13.3 us -> 15.6 us  [gathered_terms(): lax.all_to_all(jnp.broadcast_to(x[None], (size, *x.shape)), group, 0, 0)]
    another operation x2, other arithmetic: 1.96 us -> 0.06 us  [per_device(): lines = jnp.stack([local.astype(jnp.float32).T, potential.T])]
    pallas_call x1 -> x2, Pallas kernels: 2.26 us -> 3.73 us  [cut(): pl.pallas_call(functools.partial(cut_kernel, spans), out_shape=jax.ShapeD...]
  transfers between devices with their start and end apart: 6 -> 6, of which waited for: 3 -> 3; matrix products, arithmetic and copies ran while one was open for 3% -> 2% of each run, Pallas kernels for 7% -> 9%
where the time goes in v6:
time: 102 us; the launch traced here: 101 us
  blocking collectives  48.8 us (48%)
  Pallas kernels  26.2 us (26%)
  starting transfers between devices  17.8 us (17%)
  waiting for transfers between devices  5.74 us (6%)
  local copies, waits for them, and re-layouts  1.29 us (1%)
  between operations  1.02 us (1%)
    all_to_all x1, blocking collectives, gathered_terms(): return lax.all_to_all(copies, 'z', 0, 0)  17.3 us
    all_to_all x1, blocking collectives, per_device(): pieces = lax.all_to_all(pieces, STATE_AXIS, 0, 0)  15.8 us
    all_to_all x1, blocking collectives, gathered_terms(): lax.all_to_all(jnp.broadcast_to(x[None], (size, *x.shape)), group, 0, 0)  15.6 us
    pallas_call x1, Pallas kernels, filtered(): pl.pallas_call(rest_kernel, out_shape=(jax.ShapeDtypeStruct((states, coun...  11.1 us
    pallas_call x1, Pallas kernels, filtered(): pl.pallas_call(interior_kernel, out_shape=(total, window), in_specs=[VMEM...  6.93 us
    all_to_all x1, starting transfers between devices, per_device(): ends = lax.all_to_all(ends, STATE_AXIS, 0, 0).reshape(-1, ends.shape[2])  5.75 us
    all_to_all x1, starting transfers between devices, per_device(): lax.all_to_all(middle, STATE_AXIS, 0, 0).reshape(-1, middle.shape[2])  4.93 us
    ppermute x1, starting transfers between devices, per_device(): lax.ppermute(ends[:, margin:], everyone, neighbour_route(slabs, slots, Tr...  3.88 us
  transfers between devices with their start and end apart: 6, of which 3 were waited for; matrix products, arithmetic and copies ran while one was open for 2% of the time, Pallas kernels for 9%

profile of v6, /device:TPU:2, one launch (start us, length us, event | category | flops | bytes accessed | tf_op | source)
XLA Modules:
  0.0 101.3 jit_solution(2809187108852344727)
XLA Ops:
  0.6 1.7 %ends.1 = bf16[4,16,1536]{2,1,0:T(8,128)(2,1)} custom-call(bf16[16,32768]{1,0:T(8,128)(2,1)} %block_ref.2), custom_call_target="tpu_custom_call" | custom-call | tf_op jit(solution)/shard_map/ends/pallas_call | solution.py:403
  2.4 0.0 copy-start
  2.4 5.7 %all-to-all-start = ((bf16[4,16,1536]{2,1,0:T(8,128)(2,1)}), bf16[4,16,1536]{2,1,0:T(8,128)(2,1)S(1)}, u32[]{:S(2)}, u32[]{:S(2)}) async-start(bf16[4,16,1536]{2,1,0:T(8,128)(2,1)} %ends.1), calls=%async_computation | async-start | bytes 393216 | tf_op jit(solution)/shard_map/all_to_all | solution.py:456
  8.1 0.9 copy.14
  9.0 0.0 copy-start.1
  9.0 0.2 broadcast_multiply_fusion
  9.2 2.0 %middle.1 = bf16[4,16,6656]{2,1,0:T(8,128)(2,1)} custom-call(bf16[16,32768]{1,0:T(8,128)(2,1)} %block_ref.2), custom_call_target="tpu_custom_call" | custom-call | tf_op jit(solution)/shard_map/middle/pallas_call | solution.py:403
  11.3 0.1 pad.20.clone
  11.4 1.6 %all-to-all-done = bf16[4,16,1536]{2,1,0:T(8,128)(2,1)S(1)} async-done(((bf16[4,16,1536]{2,1,0:T(8,128)(2,1)}), bf16[4,16,1536]{2,1,0:T(8,128)(2,1)S(1)}, u32[]{:S(2)}, u32[]{:S(2)}) %all-to-all-start) | async-done | bytes 196640 | tf_op jit(solution)/shard_map/all_to_all | solution.py:456
  13.0 4.9 %all-to-all-start.1 = ((bf16[4,16,6656]{2,1,0:T(8,128)(2,1)}), bf16[4,16,6656]{2,1,0:T(8,128)(2,1)S(1)}, u32[]{:S(2)}, u32[]{:S(2)}) async-start(bf16[4,16,6656]{2,1,0:T(8,128)(2,1)} %middle.1), calls=%async_computation.1 | async-start | bytes 1703936 | tf_op jit(solution)/shard_map/all_to_all | solution.py:458
  17.9 0.0 copy-done
  18.0 0.0 copy-done.1
  18.0 0.1 slice_select_fusion
  18.1 1.3 %collective-permute-start.2 = (f32[2,96,128]{1,2,0:T(8,128)S(1)}, f32[2,96,128]{1,2,0:T(8,128)S(1)}, u32[]{:S(2)}, u32[]{:S(2)}) collective-permute-start(f32[2,96,128]{1,2,0:T(8,128)S(1)} %slice_select_fusion), channel_id=1, source_target_pairs={{0,4},{1,5},{6,2},{7,3},{4,8},{5,9},{10,6},{11,7},{8,12},{9,13},{1... | collective-permute-start | bytes 294920 | tf_op jit(solution)/shard_map/ppermute | solution.py:471
  19.5 2.0 %collective-permute-start.1 = (bf16[64,768]{1,0:T(8,128)(2,1)S(1)}, bf16[64,768]{1,0:T(8,128)(2,1)S(1)}, u32[]{:S(2)}, u32[]{:S(2)}) collective-permute-start(bf16[64,768]{1,0:T(8,128)(2,1)S(1)} %get-tuple-element.24), channel_id=1, source_target_pairs={{1,0},{2,1},{3,2},{4,3},{5,4},{6,5},{7,6},{8,7},{9,8},{10,9},{11,1... | collective-permute-start | bytes 294920 | tf_op jit(solution)/shard_map/ppermute | solution.py:481
  21.4 3.9 %collective-permute-start = (bf16[64,768]{1,0:T(8,128)(2,1)S(1)}, bf16[64,768]{1,0:T(8,128)(2,1)S(1)}, u32[]{:S(2)}, u32[]{:S(2)}) collective-permute-start(bf16[64,768]{1,0:T(8,128)(2,1)S(1)} %get-tuple-element.25), channel_id=1, source_target_pairs={{0,1},{1,2},{2,3},{3,4},{4,5},{5,6},{6,7},{7,8},{8,9},{9,10},{10,1... | collective-permute-start | bytes 294920 | tf_op jit(solution)/shard_map/ppermute | solution.py:480
  25.3 0.0 collective-permute-done.2
  25.3 0.1 maximum_maximum_fusion
  25.4 0.2 copy.13.cells_ref
  25.7 2.9 %all-to-all-done.1 = bf16[4,16,6656]{2,1,0:T(8,128)(2,1)S(1)} async-done(((bf16[4,16,6656]{2,1,0:T(8,128)(2,1)}), bf16[4,16,6656]{2,1,0:T(8,128)(2,1)S(1)}, u32[]{:S(2)}, u32[]{:S(2)}) %all-to-all-start.1) | async-done | bytes 852000 | tf_op jit(solution)/shard_map/all_to_all | solution.py:458
  28.6 6.9 %interior.1 = (f32[64,9984]{1,0:T(8,128)S(1)}, bf16[64,9728]{1,0:T(8,128)(2,1)S(1)}) custom-call(bf16[64,1536]{1,0:T(8,128)(2,1)S(1)} %bitcast.23, bf16[64,6656]{1,0:T(8,128)(2,1)S(1)} %bitcast.21, f32[2,640,128]{2,1,0:T(8,128)S(1)} %copy.13.cells_ref, f32[128,640]{1,0:T(8,128)S(1)} %select_maximum_fusion.1.columns_ref, bf16[256,256]{1,0:T(8,128)(2,1)S(1)} %bitcast.24), custom_call_target="tpu_custom_call" | custom-call | flops 20000000000 | bytes 20000000 | tf_op jit(solution)/shard_map/interior/pallas_call | solution.py:266
  35.6 0.0 collective-permute-done.1.high_ref
  35.6 0.0 collective-permute-done.low_ref
  35.6 11.1 %rest.1 = (bf16[64,8192]{1,0:T(8,128)(2,1)S(1)}, f32[32,128]{1,0:T(8,128)S(1)}, f32[64,9984]{1,0:T(8,128)S(1)}, bf16[64,9728]{1,0:T(8,128)(2,1)S(1)}) custom-call(bf16[64,768]{1,0:T(8,128)(2,1)S(1)} %collective-permute-done.low_ref, bf16[64,768]{1,0:T(8,128)(2,1)S(1)} %collective-permute-done.1.high_ref, ...), custom_call_target="tpu_custom_call", output_to_operand_aliasing={{2}: (5, {}), {3}: (6, {})} | custom-call | tf_op jit(solution)/shard_map/rest/pallas_call | solution.py:277
  46.7 0.0 collective-permute-start.3
  46.7 1.2 %collective-permute-done.3 = f32[32,128]{1,0:T(8,128)S(1)} collective-permute-done((f32[32,128]{1,0:T(8,128)S(1)}, f32[32,128]{1,0:T(8,128)S(1)}, u32[]{:S(2)}, u32[]{:S(2)}) %collective-permute-start.3) | collective-permute-done | bytes 16416 | tf_op jit(solution)/shard_map/ppermute | solution.py:431
  47.9 15.6 %all_to_all.25 = f32[16,32,128]{2,1,0:T(8,128)S(1)} all-to-all(f32[16,32,128]{2,1,0:T(8,128)S(1)} %broadcast_in_dim.11), channel_id=1, replica_groups=mesh['z'=8,'y'=4,'core'=2,'x'=4] {'y','x'}, dimensions={0} | all-to-all | bytes 524288 | tf_op jit(solution)/shard_map/all_to_all | solution.py:434
  63.6 17.3 %all_to_all.26.parts_ref = f32[8,32,128]{2,1,0:T(8,128)S(1)} all-to-all(f32[8,32,128]{2,1,0:T(8,128)S(1)} %broadcast_in_dim.12), channel_id=1, replica_groups=mesh['z'=8,'y'=4,'core'=2,'x'=4] {'z'}, dimensions={0} | all-to-all | bytes 262144 | tf_op jit(solution)/shard_map/all_to_all | solution.py:436
  81.0 3.5 %factor.1 = (bf16[64,8192]{1,0:T(8,128)(2,1)S(1)}, f32[64,64]{1,0:T(8,128)}) custom-call(f32[8,32,128]{2,1,0:T(8,128)S(1)} %all_to_all.26.parts_ref, bf16[64,8192]{1,0:T(8,128)(2,1)S(1)} %get-tuple-element.21.second_ref), custom_call_target="tpu_custom_call" | custom-call | tf_op jit(solution)/shard_map/factor/pallas_call | solution.py:350
  84.4 15.8 %all_to_all.27.pieces_ref = bf16[4,16,8192]{2,1,0:T(8,128)(2,1)S(1)} all-to-all(bf16[4,16,8192]{2,1,0:T(8,128)(2,1)S(1)} %bitcast.20), channel_id=1, replica_groups=mesh['z'=8,'y'=4,'core'=2,'x'=4] {'x'}, dimensions={0} | all-to-all | bytes 2097152 | tf_op jit(solution)/shard_map/all_to_all | solution.py:486
  100.2 1.0 joined.1
  (15 shorter events, 0.2 us)
Async XLA Ops:
  2.4 15.6 %copy-start = (s32[125,512]{1,0:T(8,128)S(1)}, s32[125,512]{1,0:T(8,128)}, u32[]{:S(2)}) copy-start(s32[125,512]{1,0:T(8,128)} %param.5) | copy-start | bytes 768004
  2.4 10.6 %all-to-all-start = ((bf16[4,16,1536]{2,1,0:T(8,128)(2,1)}), bf16[4,16,1536]{2,1,0:T(8,128)(2,1)S(1)}, u32[]{:S(2)}, u32[]{:S(2)}) async-start(bf16[4,16,1536]{2,1,0:T(8,128)(2,1)} %ends.1), calls=%async_computation | async-start | bytes 393216 | tf_op jit(solution)/shard_map/all_to_all | solution.py:456
  9.0 9.0 %copy-start.1 = (f32[125,512]{1,0:T(8,128)S(1)}, f32[125,512]{1,0:T(8,128)}, u32[]{:S(2)}) copy-start(f32[125,512]{1,0:T(8,128)} %param.6) | copy-start | bytes 768004
  13.0 15.6 %all-to-all-start.1 = ((bf16[4,16,6656]{2,1,0:T(8,128)(2,1)}), bf16[4,16,6656]{2,1,0:T(8,128)(2,1)S(1)}, u32[]{:S(2)}, u32[]{:S(2)}) async-start(bf16[4,16,6656]{2,1,0:T(8,128)(2,1)} %middle.1), calls=%async_computation.1 | async-start | bytes 1703936 | tf_op jit(solution)/shard_map/all_to_all | solution.py:458
  18.1 7.2 %collective-permute-start.2 = (f32[2,96,128]{1,2,0:T(8,128)S(1)}, f32[2,96,128]{1,2,0:T(8,128)S(1)}, u32[]{:S(2)}, u32[]{:S(2)}) collective-permute-start(f32[2,96,128]{1,2,0:T(8,128)S(1)} %slice_select_fusion), channel_id=1, source_target_pairs={{0,4},{1,5},{6,2},{7,3},{4,8},{5,9},{10,6},{11,7},{8,12},{9,13},{1... | collective-permute-start | bytes 294920 | tf_op jit(solution)/shard_map/ppermute | solution.py:471
  19.5 16.1 %collective-permute-start.1 = (bf16[64,768]{1,0:T(8,128)(2,1)S(1)}, bf16[64,768]{1,0:T(8,128)(2,1)S(1)}, u32[]{:S(2)}, u32[]{:S(2)}) collective-permute-start(bf16[64,768]{1,0:T(8,128)(2,1)S(1)} %get-tuple-element.24), channel_id=1, source_target_pairs={{1,0},{2,1},{3,2},{4,3},{5,4},{6,5},{7,6},{8,7},{9,8},{10,9},{11,1... | collective-permute-start | bytes 294920 | tf_op jit(solution)/shard_map/ppermute | solution.py:481
  21.4 14.1 %collective-permute-start = (bf16[64,768]{1,0:T(8,128)(2,1)S(1)}, bf16[64,768]{1,0:T(8,128)(2,1)S(1)}, u32[]{:S(2)}, u32[]{:S(2)}) collective-permute-start(bf16[64,768]{1,0:T(8,128)(2,1)S(1)} %get-tuple-element.25), channel_id=1, source_target_pairs={{0,1},{1,2},{2,3},{3,4},{4,5},{5,6},{6,7},{7,8},{8,9},{9,10},{10,1... | collective-permute-start | bytes 294920 | tf_op jit(solution)/shard_map/ppermute | solution.py:480
  46.7 1.2 %collective-permute-start.3 = (f32[32,128]{1,0:T(8,128)S(1)}, f32[32,128]{1,0:T(8,128)S(1)}, u32[]{:S(2)}, u32[]{:S(2)}) collective-permute-start(f32[32,128]{1,0:T(8,128)S(1)} %get-tuple-element.20), channel_id=1, source_target_pairs={{0,4},{4,0},{1,5},{5,1},{2,6},{6,2},{3,7},{7,3},{8,12},{12,8},{9,1... | collective-permute-start | bytes 49160 | tf_op jit(solution)/shard_map/ppermute | solution.py:431

commit v7 on v4

--- a/solution.py
+++ b/solution.py
@@ -159,30 +159,29 @@
     return jnp.clip(tile, low, low + 3), lines_of(line, count, parts, blank)
 
 
-def interior_kernel(owned_ref, cells_ref, columns_ref, matrix_ref, acc_ref):
-    tiles = owned_ref.shape[1] // LANE
+def interior_kernel(window_ref, cells_ref, columns_ref, matrix_ref, acc_ref):
+    states, whole = window_ref.shape
+    tiles = whole // LANE - 2 * HALO
     blank = cells_ref.shape[1] - QUAD
-    whole = owned_ref.shape[1] + 2 * HALO * LANE
-    acc_ref[:, pl.ds(0, whole)] = jnp.zeros((acc_ref.shape[0], whole), jnp.float32)
+    acc_ref[:, pl.ds(0, whole)] = jnp.zeros((states, whole), jnp.float32)
     parts = (tiles - 1) // 3
     inner = [segment(f, 0, tiles - 4, parts, blank) for f in families(tiles)]
-    group_block(owned_ref, 0, acc_ref, cells_ref, columns_ref, matrix_ref, inner)
+    group_block(window_ref, HALO, acc_ref, cells_ref, columns_ref, matrix_ref, inner)
 
 
 def rest_kernel(
-    owned_ref,
-    low_ref,
-    high_ref,
+    swapped_ref,
     cells_ref,
     columns_ref,
     matrix_ref,
     acc_ref,
+    window_ref,
     second_ref,
     gram_ref,
-    sum_ref,
     field,
+    acc,
 ):
-    states, owned = owned_ref.shape
+    states, owned = second_ref.shape
     tiles = owned // LANE
     margin = HALO * LANE
     blank = cells_ref.shape[1] - QUAD
@@ -192,10 +191,18 @@
     for axis in NODE_AXES[1:]:
         slab = slab * lax.axis_size(axis) + lax.axis_index(axis)
         slabs = slabs * lax.axis_size(axis)
-    acc = sum_ref
-    field[:, pl.ds(0, margin)] = low_ref[...]
-    field[:, pl.ds(margin, owned)] = owned_ref[...]
-    field[:, pl.ds(margin + owned, margin)] = high_ref[...]
+    whole = owned + 2 * margin
+    field[...] = window_ref[...]
+    acc[:, pl.ds(0, whole)] = jnp.zeros((states, whole), jnp.float32)
+
+    @pl.when(slot == 0)
+    def _():
+        field[:, pl.ds(0, margin)] = swapped_ref[...]
+
+    @pl.when(slot == lax.axis_size(STATE_AXIS) - 1)
+    def _():
+        field[:, pl.ds(margin + owned, margin)] = swapped_ref[...]
+
 
     ends = [
         segment(family, low, low + HALO - 1, 2, blank)
@@ -205,12 +212,12 @@
     group_block(field, HALO, acc, cells_ref, columns_ref, matrix_ref, ends)
 
     chunk = 4 * LANE
-    whole = owned + 2 * margin
 
     def to_first(step, carry):
         here = pl.ds(pl.multiple_of(step * chunk, LANE), chunk)
         start = field[:, here].astype(jnp.float32)
-        field[:, here] = ((acc[:, here] - CENTER * start) * (1.0 / HALF_WIDTH)).astype(field.dtype)
+        image = acc_ref[:, here] + acc[:, here] - CENTER * start
+        field[:, here] = (image * (1.0 / HALF_WIDTH)).astype(field.dtype)
         acc[:, here] = jnp.zeros((states, chunk), jnp.float32)
         return carry
 
@@ -232,13 +239,13 @@
     ]
     group_block(field, HALO, acc, cells_ref, columns_ref, matrix_ref, whole_range)
 
-    chunk = 8 * LANE
+    chunk = 16 * LANE
 
     def to_second(step, gram):
         at = pl.multiple_of(step * chunk, LANE)
         here = pl.ds(pl.multiple_of(at + margin, LANE), chunk)
         image = acc[:, here] - CENTER * field[:, here].astype(jnp.float32)
-        start = owned_ref[:, pl.ds(at, chunk)].astype(jnp.float32)
+        start = window_ref[:, here].astype(jnp.float32)
         second = (image * (2.0 / HALF_WIDTH) - start).astype(second_ref.dtype)
         second_ref[:, pl.ds(at, chunk)] = second
         return gram + lax.dot_general(
@@ -249,13 +256,14 @@
     gram_ref[...] = jnp.concatenate([gram[: states // 2], gram[states // 2 :]], axis=1)
 
 
-def filtered(owned, low, high, cells, columns, matrix):
-    states, count = owned.shape
-    full = count + (2 * HALO + SPARE) * LANE
+def filtered(window, swapped, cells, columns, matrix):
+    states, width = window.shape
+    count = width - 2 * HALO * LANE
+    total = jax.ShapeDtypeStruct((states, width + SPARE * LANE), jnp.float32)
     params = pltpu.CompilerParams(vmem_limit_bytes=24 << 20)
     acc = pl.pallas_call(
         interior_kernel,
-        out_shape=jax.ShapeDtypeStruct((states, full), jnp.float32),
+        out_shape=total,
         in_specs=[VMEM] * 4,
         out_specs=VMEM,
         compiler_params=params,
@@ -263,22 +271,22 @@
             flops=20_000_000_000, bytes_accessed=20_000_000, transcendentals=0
         ),
         name="interior",
-    )(owned, cells, columns, matrix)
-    second, gram, unused = pl.pallas_call(
+    )(window, cells, columns, matrix)
+    return pl.pallas_call(
         rest_kernel,
         out_shape=(
-            jax.ShapeDtypeStruct((states, count), owned.dtype),
+            jax.ShapeDtypeStruct((states, count), window.dtype),
             jax.ShapeDtypeStruct((states // 2, 2 * states), jnp.float32),
-            jax.ShapeDtypeStruct((states, full), jnp.float32),
         ),
-        in_specs=[VMEM] * 7,
-        out_specs=[VMEM] * 3,
-        input_output_aliases={6: 2},
-        scratch_shapes=[pltpu.VMEM((states, count + 2 * HALO * LANE), owned.dtype)],
+        in_specs=[VMEM] * 6,
+        out_specs=[VMEM] * 2,
+        scratch_shapes=[
+            pltpu.VMEM(window.shape, window.dtype),
+            pltpu.VMEM(total.shape, total.dtype),
+        ],
         compiler_params=params,
         name="rest",
-    )(owned, low, high, cells, columns, matrix, acc)
-    return second, gram
+    )(swapped, cells, columns, matrix, acc, window)
 
 
 def factor_kernel(total_nodes, parts_ref, second_ref, orthonormal_ref, factor_ref):
@@ -349,28 +357,38 @@
     )(parts, second)
 
 
-def split_kernel(block_ref, pieces_ref, held, came, went):
-    count, states, width = pieces_ref.shape
-    tall = 8
-    moves = [(i, r) for r in range(0, states, tall) for i in range(count)]
-
-    def arriving(k):
-        i, r = moves[k]
-        part = block_ref.at[pl.ds(r, tall), pl.ds(i * width, width)]
-        return pltpu.make_async_copy(part, held.at[k], came.at[k])
-
-    def leaving(k):
-        i, r = moves[k]
-        part = pieces_ref.at[i, pl.ds(r, tall), :]
-        return pltpu.make_async_copy(held.at[k], part, went.at[k])
-
-    for k in range(len(moves)):
-        arriving(k).start()
-    for k in range(len(moves)):
-        arriving(k).wait()
-        leaving(k).start()
-    for k in range(len(moves)):
-        leaving(k).wait()
+def window_moves(count, states, owned, margin):
+    moves = []
+    most = 19 * LANE
+    for row in range(0, states, 8):
+        for i in range(count):
+            begin, place, size = owned * i - margin, 0, owned + 2 * margin
+            if i == 0:
+                moves.append((i, row, 0, 0, margin))
+                begin, place, size = 0, margin, size - margin
+            if i == count - 1:
+                moves.append((i, row, owned * count - margin, owned + margin, margin))
+                size -= margin
+            for at in range(0, size, most):
+                moves.append((i, row, begin + at, place + at, min(most, size - at)))
+    return moves
+
+
+def split_kernel(moves, block_ref, pieces_ref, held, came, went):
+    arriving, leaving = [], []
+    for k, (i, row, column, place, size) in enumerate(moves):
+        rows, target = pl.ds(row, 8), pl.ds(place, size)
+        source = block_ref.at[rows, pl.ds(column, size)]
+        arriving.append(pltpu.make_async_copy(source, held.at[i, rows, target], came.at[k]))
+        piece = pieces_ref.at[i, rows, target]
+        leaving.append(pltpu.make_async_copy(held.at[i, rows, target], piece, went.at[k]))
+    for copy in arriving:
+        copy.start()
+    for came_in, copy in zip(arriving, leaving):
+        came_in.wait()
+        copy.start()
+    for copy in leaving:
+        copy.wait()
 
 
 def join_kernel(pieces_ref, block_ref, done):
@@ -385,17 +403,18 @@
 
 
 def quarters(block, count):
-    shape = (count, block.shape[0], block.shape[1] // count)
-    moves = count * block.shape[0] // 8
+    states, owned, margin = block.shape[0], block.shape[1] // count, HALO * LANE
+    moves = window_moves(count, states, owned, margin)
+    shape = (count, states, owned + 2 * margin)
     return pl.pallas_call(
-        split_kernel,
+        functools.partial(split_kernel, moves),
         out_shape=jax.ShapeDtypeStruct(shape, block.dtype),
         in_specs=[pl.BlockSpec(memory_space=pltpu.HBM)],
         out_specs=pl.BlockSpec(memory_space=pltpu.HBM),
         scratch_shapes=[
-            pltpu.VMEM((moves, 8, shape[2]), block.dtype),
-            pltpu.SemaphoreType.DMA((moves,)),
-            pltpu.SemaphoreType.DMA((moves,)),
+            pltpu.VMEM(shape, block.dtype),
+            pltpu.SemaphoreType.DMA((len(moves),)),
+            pltpu.SemaphoreType.DMA((len(moves),)),
         ],
         name="quarters",
     )(block)
@@ -423,11 +442,6 @@
     return lax.all_to_all(copies, "z", 0, 0)
 
 
-def neighbour_route(slabs, slots, up):
-    pairs = [(i, i + 1) for i in range(slabs * slots - 1)]
-    return pairs if up else [(j, i) for i, j in pairs]
-
-
 def per_device(block, connectivity, potential, cell_matrix):
     nodes, cells = connectivity.shape
     slots = lax.axis_size(STATE_AXIS)
@@ -440,7 +454,7 @@
         (quarters(block, slots), connectivity, potential)
     )
     pieces = lax.all_to_all(pieces, STATE_AXIS, 0, 0)
-    owned = pieces.reshape(-1, pieces.shape[2])
+    window = pieces.reshape(-1, pieces.shape[2])
 
     stride = 3 * LANE // QUAD
     local = connectivity - (jnp.arange(cells, dtype=jnp.int32) * stride + ABSENT)[None, :]
@@ -462,9 +476,11 @@
     matrix = jnp.pad(cell_matrix.T, ((0, LANE - nodes), (0, LANE - nodes)))
     matrix = jnp.kron(jnp.eye(2, dtype=matrix.dtype), matrix)
 
-    low = lax.ppermute(owned[:, -margin:], everyone, neighbour_route(slabs, slots, True))
-    high = lax.ppermute(owned[:, :margin], everyone, neighbour_route(slabs, slots, False))
-    second, gram = filtered(owned, low, high, lines, columns, matrix)
+    first, last = window[:, margin : 2 * margin], window[:, -2 * margin : -margin]
+    borders = [(slots * i - 1, slots * i) for i in range(1, slabs)]
+    borders += [(upper, lower) for lower, upper in borders]
+    swapped = lax.ppermute(jnp.where(slot == 0, first, last), everyone, borders)
+    second, gram = filtered(window, swapped, lines, columns, matrix)
     parts = gathered_terms(gram)
     orthonormal, factor = orthonormalized(parts, second, block.shape[1] * slabs)
     pieces = orthonormal.reshape(slots, -1, orthonormal.shape[1])

time: 101 us -> 100 us (0.990)
  starting transfers between devices: 12.9 us -> 7.92 us
  blocking collectives: 49.3 us -> 51.1 us
  local copies, waits for them, and re-layouts: 0.54 us -> 1.61 us
    ppermute x2 -> x1, starting transfers between devices: 5.84 us -> 0.67 us  [per_device(): swapped = lax.ppermute(jnp.where(slot == 0, first, last), everyone, borders)]
    all_to_all x1, blocking collectives: 16.2 us -> 18.1 us  [gathered_terms(): lax.all_to_all(jnp.broadcast_to(x[None], (size, *x.shape)), group, 0, 0)]
    concatenate x2, local copies, waits for them, and re-layouts: 0.3 us -> 1.38 us  [per_device(): lines = jnp.concatenate([lines, other], axis=1)]
  transfers between devices with their start and end apart: 5 -> 4, of which waited for: 3 -> 3; matrix products, arithmetic and copies ran while one was open for 1% -> 3% of each run, Pallas kernels for 7% -> 7%
where the time goes in v7:
time: 100 us; the launch traced here: 99.5 us
  blocking collectives  51.1 us (51%)
  Pallas kernels  24.9 us (25%)
  waiting for transfers between devices  11.7 us (12%)
  starting transfers between devices  7.92 us (8%)
  local copies, waits for them, and re-layouts  1.61 us (2%)
  other arithmetic  1.33 us (1%)
    all_to_all x1, blocking collectives, gathered_terms(): lax.all_to_all(jnp.broadcast_to(x[None], (size, *x.shape)), group, 0, 0)  18.1 us
    all_to_all x1, blocking collectives, gathered_terms(): return lax.all_to_all(copies, 'z', 0, 0)  17.2 us
    all_to_all x1, blocking collectives, per_device(): pieces = lax.all_to_all(pieces, STATE_AXIS, 0, 0)  15.8 us
    pallas_call x1, Pallas kernels, filtered(): pl.pallas_call(rest_kernel, out_shape=(jax.ShapeDtypeStruct((states, coun...  10.9 us
    all_to_all x1, waiting for transfers between devices, per_device(): pieces = lax.all_to_all(pieces, STATE_AXIS, 0, 0)  10.1 us
    pallas_call x1, Pallas kernels, filtered(): pl.pallas_call(interior_kernel, out_shape=total, in_specs=[VMEM] * 4, out...  6.78 us
    all_to_all x1, starting transfers between devices, per_device(): pieces = lax.all_to_all(pieces, STATE_AXIS, 0, 0)  5.91 us
    pallas_call x1, Pallas kernels, orthonormalized(): pl.pallas_call(functools.partial(factor_kernel, total_nodes), out_shape=(...  3.47 us
  transfers between devices with their start and end apart: 4, of which 3 were waited for; matrix products, arithmetic and copies ran while one was open for 3% of the time, Pallas kernels for 7%

profile of v7, /device:TPU:2, one launch (start us, length us, event | category | flops | bytes accessed | tf_op | source)
XLA Modules:
  0.0 99.5 jit_solution(1128170241010055379)
XLA Ops:
  0.6 2.8 %quarters.1 = bf16[4,16,9728]{2,1,0:T(8,128)(2,1)} custom-call(bf16[16,32768]{1,0:T(8,128)(2,1)} %block_ref.1), custom_call_target="tpu_custom_call" | custom-call | tf_op jit(solution)/shard_map/quarters/pallas_call | solution.py:409
  3.4 0.0 copy-start
  3.4 0.0 copy-start.1
  3.4 5.9 %all-to-all-start = ((bf16[4,16,9728]{2,1,0:T(8,128)(2,1)}), bf16[4,16,9728]{2,1,0:T(8,128)(2,1)S(1)}, u32[]{:S(2)}, u32[]{:S(2)}) async-start(bf16[4,16,9728]{2,1,0:T(8,128)(2,1)} %quarters.1), calls=%async_computation | async-start | bytes 2490368 | tf_op jit(solution)/shard_map/all_to_all | solution.py:456
  9.4 0.0 copy-start.2
  9.4 0.0 copy-done
  9.4 0.0 copy-done.1
  9.5 0.1 slice_select_fusion
  9.6 1.3 %collective-permute-start.1 = (f32[2,96,128]{1,2,0:T(8,128)S(1)}, f32[2,96,128]{1,2,0:T(8,128)S(1)}, u32[]{:S(2)}, u32[]{:S(2)}) collective-permute-start(f32[2,96,128]{1,2,0:T(8,128)S(1)} %slice_select_fusion), channel_id=1, source_target_pairs={{0,4},{1,5},{6,2},{7,3},{4,8},{5,9},{10,6},{11,7},{8,12},{9,13},{1... | collective-permute-start | bytes 294920 | tf_op jit(solution)/shard_map/ppermute | solution.py:470
  10.9 0.0 copy-done.2
  10.9 0.1 copy.12
  11.1 0.2 broadcast_multiply_fusion
  11.3 0.1 pad.20.clone
  11.4 0.5 collective-permute-done.1
  11.8 0.9 maximum_maximum_fusion
  12.7 1.3 %copy.11.cells_ref = f32[2,640,128]{2,1,0:T(8,128)S(1)} copy(f32[2,640,128]{1,2,0:T(8,128)} %maximum_maximum_fusion) | data formatting | bytes 1310720 | tf_op jit(solution)/shard_map/concatenate | solution.py:473
  14.1 10.1 %all-to-all-done = bf16[4,16,9728]{2,1,0:T(8,128)(2,1)S(1)} async-done(((bf16[4,16,9728]{2,1,0:T(8,128)(2,1)}), bf16[4,16,9728]{2,1,0:T(8,128)(2,1)S(1)}, u32[]{:S(2)}, u32[]{:S(2)}) %all-to-all-start) | async-done | bytes 1245216 | tf_op jit(solution)/shard_map/all_to_all | solution.py:456
  24.2 0.7 collective-permute-start
  24.8 6.8 %interior.1.acc_ref = f32[64,9984]{1,0:T(8,128)S(1)} custom-call(bf16[64,9728]{1,0:T(8,128)(2,1)S(1)} %bitcast.20, f32[2,640,128]{2,1,0:T(8,128)S(1)} %copy.11.cells_ref, f32[128,640]{1,0:T(8,128)S(1)} %select_maximum_fusion.1.columns_ref, bf16[256,256]{1,0:T(8,128)(2,1)S(1)} %bitcast.23), custom_call_target="tpu_custom_call" | custom-call | flops 20000000000 | bytes 20000000 | tf_op jit(solution)/shard_map/interior/pallas_call | solution.py:264
  31.6 0.0 collective-permute-done.swapped_ref
  31.6 10.9 %rest.1 = (bf16[64,8192]{1,0:T(8,128)(2,1)S(1)}, f32[32,128]{1,0:T(8,128)S(1)}) custom-call(bf16[64,768]{1,0:T(8,128)(2,1)S(1)} %collective-permute-done.swapped_ref, f32[2,640,128]{2,1,0:T(8,128)S(1)} %copy.11.cells_ref, f32[128,640]{1,0:T(8,128)S(1)} %select_maximum_fusion.1.columns_ref, bf16[256,256]{1,0:T(8,128)(2,1)S(1)} %bitcast.24, ...), custom_call_target="tpu_custom_call" | custom-call | tf_op jit(solution)/shard_map/rest/pallas_call | solution.py:275
  42.5 0.0 collective-permute-start.2
  42.6 1.2 %collective-permute-done.2 = f32[32,128]{1,0:T(8,128)S(1)} collective-permute-done((f32[32,128]{1,0:T(8,128)S(1)}, f32[32,128]{1,0:T(8,128)S(1)}, u32[]{:S(2)}, u32[]{:S(2)}) %collective-permute-start.2) | collective-permute-done | bytes 16416 | tf_op jit(solution)/shard_map/ppermute | solution.py:437
  43.8 18.1 %all_to_all.20 = f32[16,32,128]{2,1,0:T(8,128)S(1)} all-to-all(f32[16,32,128]{2,1,0:T(8,128)S(1)} %broadcast_in_dim.11), channel_id=1, replica_groups=mesh['z'=8,'y'=4,'core'=2,'x'=4] {'y','x'}, dimensions={0} | all-to-all | bytes 524288 | tf_op jit(solution)/shard_map/all_to_all | solution.py:440
  61.9 17.2 %all_to_all.21.parts_ref = f32[8,32,128]{2,1,0:T(8,128)S(1)} all-to-all(f32[8,32,128]{2,1,0:T(8,128)S(1)} %broadcast_in_dim.12), channel_id=1, replica_groups=mesh['z'=8,'y'=4,'core'=2,'x'=4] {'z'}, dimensions={0} | all-to-all | bytes 262144 | tf_op jit(solution)/shard_map/all_to_all | solution.py:442
  79.1 3.5 %factor.1 = (bf16[64,8192]{1,0:T(8,128)(2,1)S(1)}, f32[64,64]{1,0:T(8,128)}) custom-call(f32[8,32,128]{2,1,0:T(8,128)S(1)} %all_to_all.21.parts_ref, bf16[64,8192]{1,0:T(8,128)(2,1)S(1)} %get-tuple-element.13.second_ref), custom_call_target="tpu_custom_call" | custom-call | tf_op jit(solution)/shard_map/factor/pallas_call | solution.py:347
  82.6 15.8 %all_to_all.22.pieces_ref = bf16[4,16,8192]{2,1,0:T(8,128)(2,1)S(1)} all-to-all(bf16[4,16,8192]{2,1,0:T(8,128)(2,1)S(1)} %bitcast.22), channel_id=1, replica_groups=mesh['z'=8,'y'=4,'core'=2,'x'=4] {'x'}, dimensions={0} | all-to-all | bytes 2097152 | tf_op jit(solution)/shard_map/all_to_all | solution.py:487
  98.4 1.0 joined.1
  (15 shorter events, 0.2 us)
Async XLA Ops:
  3.4 5.9 %copy-start = (s32[125,512]{1,0:T(8,128)S(1)}, s32[125,512]{1,0:T(8,128)}, u32[]{:S(2)}) copy-start(s32[125,512]{1,0:T(8,128)} %param.5) | copy-start | bytes 768004
  3.4 6.0 %copy-start.1 = (f32[125,512]{1,0:T(8,128)S(1)}, f32[125,512]{1,0:T(8,128)}, u32[]{:S(2)}) copy-start(f32[125,512]{1,0:T(8,128)} %param.6) | copy-start | bytes 768004
  3.4 20.7 %all-to-all-start = ((bf16[4,16,9728]{2,1,0:T(8,128)(2,1)}), bf16[4,16,9728]{2,1,0:T(8,128)(2,1)S(1)}, u32[]{:S(2)}, u32[]{:S(2)}) async-start(bf16[4,16,9728]{2,1,0:T(8,128)(2,1)} %quarters.1), calls=%async_computation | async-start | bytes 2490368 | tf_op jit(solution)/shard_map/all_to_all | solution.py:456
  9.4 1.5 %copy-start.2 = (bf16[125,125]{1,0:T(8,128)(2,1)S(1)}, bf16[125,125]{1,0:T(8,128)(2,1)}, u32[]{:S(2)}) copy-start(bf16[125,125]{1,0:T(8,128)(2,1)} %param.7) | copy-start | bytes 93754
  9.6 2.3 %collective-permute-start.1 = (f32[2,96,128]{1,2,0:T(8,128)S(1)}, f32[2,96,128]{1,2,0:T(8,128)S(1)}, u32[]{:S(2)}, u32[]{:S(2)}) collective-permute-start(f32[2,96,128]{1,2,0:T(8,128)S(1)} %slice_select_fusion), channel_id=1, source_target_pairs={{0,4},{1,5},{6,2},{7,3},{4,8},{5,9},{10,6},{11,7},{8,12},{9,13},{1... | collective-permute-start | bytes 294920 | tf_op jit(solution)/shard_map/ppermute | solution.py:470
  24.2 7.5 %collective-permute-start = (bf16[64,768]{1,0:T(8,128)(2,1)S(1)}, bf16[64,768]{1,0:T(8,128)(2,1)S(1)}, u32[]{:S(2)}, u32[]{:S(2)}) collective-permute-start(bf16[64,768]{1,0:T(8,128)(2,1)S(1)} %slice_select_fusion.1), channel_id=1, source_target_pairs={{3,4},{7,8},{11,12},{15,16},{19,20},{23,24},{27,28},{31,32},{35,36... | collective-permute-start | bytes 294920 | tf_op jit(solution)/shard_map/ppermute | solution.py:482
  42.5 1.2 %collective-permute-start.2 = (f32[32,128]{1,0:T(8,128)S(1)}, f32[32,128]{1,0:T(8,128)S(1)}, u32[]{:S(2)}, u32[]{:S(2)}) collective-permute-start(f32[32,128]{1,0:T(8,128)S(1)} %get-tuple-element.12), channel_id=1, source_target_pairs={{0,4},{4,0},{1,5},{5,1},{2,6},{6,2},{3,7},{7,3},{8,12},{12,8},{9,1... | collective-permute-start | bytes 49160 | tf_op jit(solution)/shard_map/ppermute | solution.py:437

commit v8 on v7

--- a/solution.py
+++ b/solution.py
@@ -49,11 +49,14 @@
 
 
 def group_block(source, origin, acc, cells_ref, columns_ref, matrix_ref, segments):
-    def counted(axis):
-        index = lax.broadcasted_iota(jnp.int32, (LANE, LANE), axis)
-        return index.astype(jnp.float32).astype(jnp.bfloat16)
-
-    down, along = counted(0), counted(1)
+    down = lax.broadcasted_iota(jnp.int32, (LANE, LANE), 0)
+    down = down.astype(jnp.float32).astype(jnp.bfloat16)
+    lane = lax.broadcasted_iota(jnp.int32, (16, LANE), 1)
+    targets = {}
+    for cell in range(QUAD):
+        for t in CELL_TILES[cell]:
+            row = (lane + (128 * t - 96 * cell)).astype(jnp.float32).astype(jnp.bfloat16)
+            targets[cell, t] = jnp.concatenate([row] * (LANE // 16), axis=0)
     one = jnp.ones((LANE, LANE), jnp.bfloat16)
     none = jnp.zeros((LANE, LANE), jnp.bfloat16)
     states, width = source.shape
@@ -107,15 +110,20 @@
 
     def scatter(terms, index, part, tile, line):
         begin = pl.multiple_of(line // LANE * LANE, LANE)
-        columns = pltpu.roll(columns_ref[:, pl.ds(begin, LANE)], LANE - (line - begin), 1)
+        columns = columns_ref[:, pl.ds(begin, LANE)]
         placers = []
         for cell in range(QUAD):
-            node = jnp.broadcast_to(columns[:, cell : cell + 1], (LANE, LANE))
+            lanes = jnp.full((8, LANE), line - begin + cell, jnp.int32)
+            node = jnp.concatenate(
+                [
+                    jnp.take_along_axis(columns[k : k + 8], lanes, axis=1)
+                    for k in range(0, LANE, 8)
+                ],
+                axis=0,
+            )
+            node = (node + ABSENT).astype(jnp.bfloat16)
             placers.append(
-                {
-                    t: jnp.where(along == (node + shift(cell, t)).astype(jnp.bfloat16), one, none)
-                    for t in CELL_TILES[cell]
-                }
+                {t: jnp.where(node == targets[cell, t], one, none) for t in CELL_TILES[cell]}
             )
         for begin, cells in ((0, (0, 1, 2)), (2, (1, 2, 3))):
             weights = jnp.concatenate(
@@ -357,38 +365,48 @@
     )(parts, second)
 
 
-def window_moves(count, states, owned, margin):
-    moves = []
-    most = 19 * LANE
-    for row in range(0, states, 8):
+def split_kernel(block_ref, pieces_ref, held, came, went):
+    count, states, width = pieces_ref.shape
+    total = block_ref.shape[1]
+    margin = HALO * LANE
+    owned = total // count
+    tall, wide = 8, total // 2
+    arriving = [(row, at) for row in range(0, states, tall) for at in range(0, total, wide)]
+    leaving = []
+    for row in range(0, states, tall):
         for i in range(count):
-            begin, place, size = owned * i - margin, 0, owned + 2 * margin
+            begin, place, size = owned * i - margin, 0, width
             if i == 0:
-                moves.append((i, row, 0, 0, margin))
+                leaving.append((i, row, 0, 0, margin))
                 begin, place, size = 0, margin, size - margin
             if i == count - 1:
-                moves.append((i, row, owned * count - margin, owned + margin, margin))
+                leaving.append((i, row, total - margin, width - margin, margin))
                 size -= margin
-            for at in range(0, size, most):
-                moves.append((i, row, begin + at, place + at, min(most, size - at)))
-    return moves
-
-
-def split_kernel(moves, block_ref, pieces_ref, held, came, went):
-    arriving, leaving = [], []
-    for k, (i, row, column, place, size) in enumerate(moves):
-        rows, target = pl.ds(row, 8), pl.ds(place, size)
-        source = block_ref.at[rows, pl.ds(column, size)]
-        arriving.append(pltpu.make_async_copy(source, held.at[i, rows, target], came.at[k]))
-        piece = pieces_ref.at[i, rows, target]
-        leaving.append(pltpu.make_async_copy(held.at[i, rows, target], piece, went.at[k]))
-    for copy in arriving:
-        copy.start()
-    for came_in, copy in zip(arriving, leaving):
-        came_in.wait()
-        copy.start()
-    for copy in leaving:
-        copy.wait()
+            leaving.append((i, row, begin, place, size))
+
+    def copy_in(k):
+        row, at = arriving[k]
+        part = (pl.ds(row, tall), pl.ds(at, wide))
+        return pltpu.make_async_copy(block_ref.at[part], held.at[part], came.at[k])
+
+    def copy_out(k):
+        i, row, column, place, size = leaving[k]
+        source = held.at[pl.ds(row, tall), pl.ds(column, size)]
+        target = pieces_ref.at[i, pl.ds(row, tall), pl.ds(place, size)]
+        return pltpu.make_async_copy(source, target, went.at[k])
+
+    for k in range(len(arriving)):
+        copy_in(k).start()
+    left = list(range(len(leaving)))
+    for k, (row, at) in enumerate(arriving):
+        copy_in(k).wait()
+        for j in list(left):
+            i, state, column, place, size = leaving[j]
+            if state < row or (state == row and column + size <= at + wide):
+                copy_out(j).start()
+                left.remove(j)
+    for k in range(len(leaving)):
+        copy_out(k).wait()
 
 
 def join_kernel(pieces_ref, block_ref, done):
@@ -403,18 +421,17 @@
 
 
 def quarters(block, count):
-    states, owned, margin = block.shape[0], block.shape[1] // count, HALO * LANE
-    moves = window_moves(count, states, owned, margin)
-    shape = (count, states, owned + 2 * margin)
+    states, total = block.shape
+    shape = (count, states, total // count + 2 * HALO * LANE)
     return pl.pallas_call(
-        functools.partial(split_kernel, moves),
+        split_kernel,
         out_shape=jax.ShapeDtypeStruct(shape, block.dtype),
         in_specs=[pl.BlockSpec(memory_space=pltpu.HBM)],
         out_specs=pl.BlockSpec(memory_space=pltpu.HBM),
         scratch_shapes=[
-            pltpu.VMEM(shape, block.dtype),
-            pltpu.SemaphoreType.DMA((len(moves),)),
-            pltpu.SemaphoreType.DMA((len(moves),)),
+            pltpu.VMEM(block.shape, block.dtype),
+            pltpu.SemaphoreType.DMA((states // 4,)),
+            pltpu.SemaphoreType.DMA((states // 8 * (count + 2),)),
         ],
         name="quarters",
     )(block)

time: 100 us -> 97.5 us (0.975)
  Pallas kernels: 24.9 us -> 22.5 us
  transfers between devices with their start and end apart: 4 -> 4, of which waited for: 3 -> 3; matrix products, arithmetic and copies ran while one was open for 3% -> 3% of each run, Pallas kernels for 7% -> 6%
where the time goes in v8:
time: 97.5 us; the launch traced here: 97.1 us
  blocking collectives  51.1 us (52%)
  Pallas kernels  22.5 us (23%)
  waiting for transfers between devices  11.7 us (12%)
  starting transfers between devices  7.92 us (8%)
  local copies, waits for them, and re-layouts  1.61 us (2%)
  other arithmetic  1.33 us (1%)
  between operations  0.99 us (1%)
    all_to_all x1, blocking collectives, gathered_terms(): lax.all_to_all(jnp.broadcast_to(x[None], (size, *x.shape)), group, 0, 0)  18.1 us
    all_to_all x1, blocking collectives, gathered_terms(): return lax.all_to_all(copies, 'z', 0, 0)  17.2 us
    all_to_all x1, blocking collectives, per_device(): pieces = lax.all_to_all(pieces, STATE_AXIS, 0, 0)  15.8 us
    all_to_all x1, waiting for transfers between devices, per_device(): pieces = lax.all_to_all(pieces, STATE_AXIS, 0, 0)  10.1 us
    pallas_call x1, Pallas kernels, filtered(): pl.pallas_call(rest_kernel, out_shape=(jax.ShapeDtypeStruct((states, coun...  9.87 us
    pallas_call x1, Pallas kernels, filtered(): pl.pallas_call(interior_kernel, out_shape=total, in_specs=[VMEM] * 4, out...  5.96 us
    all_to_all x1, starting transfers between devices, per_device(): pieces = lax.all_to_all(pieces, STATE_AXIS, 0, 0)  5.91 us
    pallas_call x1, Pallas kernels, orthonormalized(): pl.pallas_call(functools.partial(factor_kernel, total_nodes), out_shape=(...  3.47 us
  transfers between devices with their start and end apart: 4, of which 3 were waited for; matrix products, arithmetic and copies ran while one was open for 3% of the time, Pallas kernels for 6%

profile of v8, /device:TPU:2, one launch (start us, length us, event | category | flops | bytes accessed | tf_op | source)
XLA Modules:
  0.0 97.1 jit_solution(768458185615381580)
XLA Ops:
  0.6 2.2 %quarters.1 = bf16[4,16,9728]{2,1,0:T(8,128)(2,1)} custom-call(bf16[16,32768]{1,0:T(8,128)(2,1)} %block_ref.1), custom_call_target="tpu_custom_call" | custom-call | tf_op jit(solution)/shard_map/quarters/pallas_call | solution.py:426
  2.8 0.0 copy-start
  2.8 0.0 copy-start.1
  2.8 5.9 %all-to-all-start = ((bf16[4,16,9728]{2,1,0:T(8,128)(2,1)}), bf16[4,16,9728]{2,1,0:T(8,128)(2,1)S(1)}, u32[]{:S(2)}, u32[]{:S(2)}) async-start(bf16[4,16,9728]{2,1,0:T(8,128)(2,1)} %quarters.1), calls=%async_computation | async-start | bytes 2490368 | tf_op jit(solution)/shard_map/all_to_all | solution.py:473
  8.8 0.0 copy-start.2
  8.8 0.0 copy-done
  8.8 0.0 copy-done.1
  8.9 0.1 slice_select_fusion
  9.0 1.3 %collective-permute-start.1 = (f32[2,96,128]{1,2,0:T(8,128)S(1)}, f32[2,96,128]{1,2,0:T(8,128)S(1)}, u32[]{:S(2)}, u32[]{:S(2)}) collective-permute-start(f32[2,96,128]{1,2,0:T(8,128)S(1)} %slice_select_fusion), channel_id=1, source_target_pairs={{0,4},{1,5},{6,2},{7,3},{4,8},{5,9},{10,6},{11,7},{8,12},{9,13},{1... | collective-permute-start | bytes 294920 | tf_op jit(solution)/shard_map/ppermute | solution.py:487
  10.3 0.0 copy-done.2
  10.3 0.1 copy.12
  10.5 0.2 broadcast_multiply_fusion
  10.7 0.1 pad.20.clone
  10.8 0.5 collective-permute-done.1
  11.2 0.9 maximum_maximum_fusion
  12.1 1.3 %copy.11.cells_ref = f32[2,640,128]{2,1,0:T(8,128)S(1)} copy(f32[2,640,128]{1,2,0:T(8,128)} %maximum_maximum_fusion) | data formatting | bytes 1310720 | tf_op jit(solution)/shard_map/concatenate | solution.py:490
  13.5 10.1 %all-to-all-done = bf16[4,16,9728]{2,1,0:T(8,128)(2,1)S(1)} async-done(((bf16[4,16,9728]{2,1,0:T(8,128)(2,1)}), bf16[4,16,9728]{2,1,0:T(8,128)(2,1)S(1)}, u32[]{:S(2)}, u32[]{:S(2)}) %all-to-all-start) | async-done | bytes 1245216 | tf_op jit(solution)/shard_map/all_to_all | solution.py:473
  23.6 0.7 collective-permute-start
  24.2 6.0 %interior.1.acc_ref = f32[64,9984]{1,0:T(8,128)S(1)} custom-call(bf16[64,9728]{1,0:T(8,128)(2,1)S(1)} %bitcast.20, f32[2,640,128]{2,1,0:T(8,128)S(1)} %copy.11.cells_ref, f32[128,640]{1,0:T(8,128)S(1)} %select_maximum_fusion.1.columns_ref, bf16[256,256]{1,0:T(8,128)(2,1)S(1)} %bitcast.23), custom_call_target="tpu_custom_call" | custom-call | flops 20000000000 | bytes 20000000 | tf_op jit(solution)/shard_map/interior/pallas_call | solution.py:272
  30.2 0.0 collective-permute-done.swapped_ref
  30.2 9.9 %rest.1 = (bf16[64,8192]{1,0:T(8,128)(2,1)S(1)}, f32[32,128]{1,0:T(8,128)S(1)}) custom-call(bf16[64,768]{1,0:T(8,128)(2,1)S(1)} %collective-permute-done.swapped_ref, f32[2,640,128]{2,1,0:T(8,128)S(1)} %copy.11.cells_ref, f32[128,640]{1,0:T(8,128)S(1)} %select_maximum_fusion.1.columns_ref, bf16[256,256]{1,0:T(8,128)(2,1)S(1)} %bitcast.24, ...), custom_call_target="tpu_custom_call" | custom-call | tf_op jit(solution)/shard_map/rest/pallas_call | solution.py:283
  40.1 0.0 collective-permute-start.2
  40.1 1.2 %collective-permute-done.2 = f32[32,128]{1,0:T(8,128)S(1)} collective-permute-done((f32[32,128]{1,0:T(8,128)S(1)}, f32[32,128]{1,0:T(8,128)S(1)}, u32[]{:S(2)}, u32[]{:S(2)}) %collective-permute-start.2) | collective-permute-done | bytes 16416 | tf_op jit(solution)/shard_map/ppermute | solution.py:454
  41.3 18.1 %all_to_all.20 = f32[16,32,128]{2,1,0:T(8,128)S(1)} all-to-all(f32[16,32,128]{2,1,0:T(8,128)S(1)} %broadcast_in_dim.11), channel_id=1, replica_groups=mesh['z'=8,'y'=4,'core'=2,'x'=4] {'y','x'}, dimensions={0} | all-to-all | bytes 524288 | tf_op jit(solution)/shard_map/all_to_all | solution.py:457
  59.5 17.2 %all_to_all.21.parts_ref = f32[8,32,128]{2,1,0:T(8,128)S(1)} all-to-all(f32[8,32,128]{2,1,0:T(8,128)S(1)} %broadcast_in_dim.12), channel_id=1, replica_groups=mesh['z'=8,'y'=4,'core'=2,'x'=4] {'z'}, dimensions={0} | all-to-all | bytes 262144 | tf_op jit(solution)/shard_map/all_to_all | solution.py:459
  76.7 3.5 %factor.1 = (bf16[64,8192]{1,0:T(8,128)(2,1)S(1)}, f32[64,64]{1,0:T(8,128)}) custom-call(f32[8,32,128]{2,1,0:T(8,128)S(1)} %all_to_all.21.parts_ref, bf16[64,8192]{1,0:T(8,128)(2,1)S(1)} %get-tuple-element.13.second_ref), custom_call_target="tpu_custom_call" | custom-call | tf_op jit(solution)/shard_map/factor/pallas_call | solution.py:355
  80.2 15.8 %all_to_all.22.pieces_ref = bf16[4,16,8192]{2,1,0:T(8,128)(2,1)S(1)} all-to-all(bf16[4,16,8192]{2,1,0:T(8,128)(2,1)S(1)} %bitcast.22), channel_id=1, replica_groups=mesh['z'=8,'y'=4,'core'=2,'x'=4] {'x'}, dimensions={0} | all-to-all | bytes 2097152 | tf_op jit(solution)/shard_map/all_to_all | solution.py:504
  95.9 1.0 %joined.1 = bf16[16,32768]{1,0:T(8,128)(2,1)} custom-call(bf16[4,16,8192]{2,1,0:T(8,128)(2,1)S(1)} %all_to_all.22.pieces_ref), custom_call_target="tpu_custom_call" | custom-call | tf_op jit(solution)/shard_map/joined/pallas_call | solution.py:442
  (15 shorter events, 0.2 us)
Async XLA Ops:
  2.8 5.9 %copy-start = (s32[125,512]{1,0:T(8,128)S(1)}, s32[125,512]{1,0:T(8,128)}, u32[]{:S(2)}) copy-start(s32[125,512]{1,0:T(8,128)} %param.5) | copy-start | bytes 768004
  2.8 6.0 %copy-start.1 = (f32[125,512]{1,0:T(8,128)S(1)}, f32[125,512]{1,0:T(8,128)}, u32[]{:S(2)}) copy-start(f32[125,512]{1,0:T(8,128)} %param.6) | copy-start | bytes 768004
  2.8 20.7 %all-to-all-start = ((bf16[4,16,9728]{2,1,0:T(8,128)(2,1)}), bf16[4,16,9728]{2,1,0:T(8,128)(2,1)S(1)}, u32[]{:S(2)}, u32[]{:S(2)}) async-start(bf16[4,16,9728]{2,1,0:T(8,128)(2,1)} %quarters.1), calls=%async_computation | async-start | bytes 2490368 | tf_op jit(solution)/shard_map/all_to_all | solution.py:473
  8.8 1.5 %copy-start.2 = (bf16[125,125]{1,0:T(8,128)(2,1)S(1)}, bf16[125,125]{1,0:T(8,128)(2,1)}, u32[]{:S(2)}) copy-start(bf16[125,125]{1,0:T(8,128)(2,1)} %param.7) | copy-start | bytes 93754
  9.0 2.3 %collective-permute-start.1 = (f32[2,96,128]{1,2,0:T(8,128)S(1)}, f32[2,96,128]{1,2,0:T(8,128)S(1)}, u32[]{:S(2)}, u32[]{:S(2)}) collective-permute-start(f32[2,96,128]{1,2,0:T(8,128)S(1)} %slice_select_fusion), channel_id=1, source_target_pairs={{0,4},{1,5},{6,2},{7,3},{4,8},{5,9},{10,6},{11,7},{8,12},{9,13},{1... | collective-permute-start | bytes 294920 | tf_op jit(solution)/shard_map/ppermute | solution.py:487
  23.6 6.6 %collective-permute-start = (bf16[64,768]{1,0:T(8,128)(2,1)S(1)}, bf16[64,768]{1,0:T(8,128)(2,1)S(1)}, u32[]{:S(2)}, u32[]{:S(2)}) collective-permute-start(bf16[64,768]{1,0:T(8,128)(2,1)S(1)} %slice_select_fusion.1), channel_id=1, source_target_pairs={{3,4},{7,8},{11,12},{15,16},{19,20},{23,24},{27,28},{31,32},{35,36... | collective-permute-start | bytes 294920 | tf_op jit(solution)/shard_map/ppermute | solution.py:499
  40.1 1.2 %collective-permute-start.2 = (f32[32,128]{1,0:T(8,128)S(1)}, f32[32,128]{1,0:T(8,128)S(1)}, u32[]{:S(2)}, u32[]{:S(2)}) collective-permute-start(f32[32,128]{1,0:T(8,128)S(1)} %get-tuple-element.12), channel_id=1, source_target_pairs={{0,4},{4,0},{1,5},{5,1},{2,6},{6,2},{3,7},{7,3},{8,12},{12,8},{9,1... | collective-permute-start | bytes 49160 | tf_op jit(solution)/shard_map/ppermute | solution.py:454

commit v9 on v8

--- a/solution.py
+++ b/solution.py
@@ -83,15 +83,9 @@
                 picked[t] = jnp.where(down == row, one, none)
             pickers.append(picked)
         values = []
-        for pair, begin in (((0, 1), 0), ((2, 3), 1)):
-            weights = jnp.concatenate(
-                [
-                    jnp.concatenate([pickers[c].get(t, none) for c in pair], axis=1)
-                    for t in range(begin, begin + 3)
-                ],
-                axis=0,
-            )
-            x_part = x[:, begin * LANE : (begin + 3) * LANE]
+        for cell, touched in enumerate(CELL_TILES):
+            weights = jnp.concatenate([pickers[cell][t] for t in touched], axis=0)
+            x_part = x[:, touched[0] * LANE : (touched[-1] + 1) * LANE]
             values.append(jnp.dot(x_part, weights, preferred_element_type=jnp.float32))
         return values
 
@@ -99,13 +93,10 @@
         half = jnp.concatenate([v.astype(jnp.bfloat16) for v in values], axis=0)
         mixed = jnp.dot(half, matrix_ref[...], preferred_element_type=jnp.float32)
         terms = []
-        for pair in range(2):
-            level = jnp.concatenate(
-                [cells_ref[1, pl.ds(line + 2 * pair + i, 1), :] for i in range(2)], axis=1
-            )
-            term = mixed[states * pair : states * (pair + 1)] + level * values[pair]
-            term = term.astype(jnp.bfloat16)
-            terms += [term[:, :LANE], term[:, LANE:]]
+        for cell in range(QUAD):
+            level = cells_ref[1, pl.ds(line + cell, 1), :]
+            term = mixed[states * cell : states * (cell + 1)] + level * values[cell]
+            terms.append(term.astype(jnp.bfloat16))
         return terms
 
     def scatter(terms, index, part, tile, line):
@@ -491,7 +482,6 @@
     columns = jnp.pad(local.astype(jnp.float32), ((0, LANE - nodes), (0, 0)))
     columns = jnp.concatenate([columns, other[0].T], axis=1)
     matrix = jnp.pad(cell_matrix.T, ((0, LANE - nodes), (0, LANE - nodes)))
-    matrix = jnp.kron(jnp.eye(2, dtype=matrix.dtype), matrix)
 
     first, last = window[:, margin : 2 * margin], window[:, -2 * margin : -margin]
     borders = [(slots * i - 1, slots * i) for i in range(1, slabs)]

time: 97.5 us -> 95.7 us (0.982)
  Pallas kernels: 22.5 us -> 20.7 us
  transfers between devices with their start and end apart: 4 -> 4, of which waited for: 3 -> 3; matrix products, arithmetic and copies ran while one was open for 3% -> 3% of each run, Pallas kernels for 6% -> 5%
where the time goes in v9:
time: 95.7 us; the launch traced here: 95.3 us
  blocking collectives  51.1 us (53%)
  Pallas kernels  20.7 us (22%)
  waiting for transfers between devices  11.9 us (12%)
  starting transfers between devices  7.92 us (8%)
  local copies, waits for them, and re-layouts  1.58 us (2%)
  other arithmetic  1.15 us (1%)
  between operations  0.98 us (1%)
    all_to_all x1, blocking collectives, gathered_terms(): lax.all_to_all(jnp.broadcast_to(x[None], (size, *x.shape)), group, 0, 0)  18.1 us
    all_to_all x1, blocking collectives, gathered_terms(): return lax.all_to_all(copies, 'z', 0, 0)  17.2 us
    all_to_all x1, blocking collectives, per_device(): pieces = lax.all_to_all(pieces, STATE_AXIS, 0, 0)  15.8 us
    all_to_all x1, waiting for transfers between devices, per_device(): pieces = lax.all_to_all(pieces, STATE_AXIS, 0, 0)  10.1 us
    pallas_call x1, Pallas kernels, filtered(): pl.pallas_call(rest_kernel, out_shape=(jax.ShapeDtypeStruct((states, coun...  8.91 us
    all_to_all x1, starting transfers between devices, per_device(): pieces = lax.all_to_all(pieces, STATE_AXIS, 0, 0)  5.91 us
    pallas_call x1, Pallas kernels, filtered(): pl.pallas_call(interior_kernel, out_shape=total, in_specs=[VMEM] * 4, out...  5.12 us
    pallas_call x1, Pallas kernels, orthonormalized(): pl.pallas_call(functools.partial(factor_kernel, total_nodes), out_shape=(...  3.47 us
  transfers between devices with their start and end apart: 4, of which 3 were waited for; matrix products, arithmetic and copies ran while one was open for 3% of the time, Pallas kernels for 5%

profile of v9, /device:TPU:2, one launch (start us, length us, event | category | flops | bytes accessed | tf_op | source)
XLA Modules:
  0.0 95.3 jit_solution(8039515020933155175)
XLA Ops:
  0.6 2.2 %quarters.1 = bf16[4,16,9728]{2,1,0:T(8,128)(2,1)} custom-call(bf16[16,32768]{1,0:T(8,128)(2,1)} %block_ref.1), custom_call_target="tpu_custom_call" | custom-call | tf_op jit(solution)/shard_map/quarters/pallas_call | solution.py:417
  2.8 0.0 copy-start
  2.8 0.0 copy-start.1
  2.8 5.9 %all-to-all-start = ((bf16[4,16,9728]{2,1,0:T(8,128)(2,1)}), bf16[4,16,9728]{2,1,0:T(8,128)(2,1)S(1)}, u32[]{:S(2)}, u32[]{:S(2)}) async-start(bf16[4,16,9728]{2,1,0:T(8,128)(2,1)} %quarters.1), calls=%async_computation | async-start | bytes 2490368 | tf_op jit(solution)/shard_map/all_to_all | solution.py:464
  8.8 0.0 copy-done
  8.8 0.0 copy-start.2
  8.8 0.0 copy-done.1
  8.9 0.1 slice_select_fusion
  9.0 1.3 %collective-permute-start.1 = (f32[2,96,128]{1,2,0:T(8,128)S(1)}, f32[2,96,128]{1,2,0:T(8,128)S(1)}, u32[]{:S(2)}, u32[]{:S(2)}) collective-permute-start(f32[2,96,128]{1,2,0:T(8,128)S(1)} %slice_select_fusion), channel_id=1, source_target_pairs={{0,4},{1,5},{6,2},{7,3},{4,8},{5,9},{10,6},{11,7},{8,12},{9,13},{1... | collective-permute-start | bytes 294920 | tf_op jit(solution)/shard_map/ppermute | solution.py:478
  10.3 0.0 copy-done.2
  10.3 0.1 copy.9
  10.4 0.1 pad.20.clone
  10.5 0.7 collective-permute-done.1
  11.2 0.9 maximum_maximum_fusion
  12.1 1.3 %copy.11.cells_ref = f32[2,640,128]{2,1,0:T(8,128)S(1)} copy(f32[2,640,128]{1,2,0:T(8,128)} %maximum_maximum_fusion) | data formatting | bytes 1310720 | tf_op jit(solution)/shard_map/concatenate | solution.py:481
  13.5 10.1 %all-to-all-done = bf16[4,16,9728]{2,1,0:T(8,128)(2,1)S(1)} async-done(((bf16[4,16,9728]{2,1,0:T(8,128)(2,1)}), bf16[4,16,9728]{2,1,0:T(8,128)(2,1)S(1)}, u32[]{:S(2)}, u32[]{:S(2)}) %all-to-all-start) | async-done | bytes 1245216 | tf_op jit(solution)/shard_map/all_to_all | solution.py:464
  23.6 0.7 collective-permute-start
  24.2 5.1 %interior.1.acc_ref = f32[64,9984]{1,0:T(8,128)S(1)} custom-call(bf16[64,9728]{1,0:T(8,128)(2,1)S(1)} %bitcast.15, f32[2,640,128]{2,1,0:T(8,128)S(1)} %copy.11.cells_ref, f32[128,640]{1,0:T(8,128)S(1)} %select_maximum_fusion.1.columns_ref, bf16[128,128]{1,0:T(8,128)(2,1)S(1)} %pad.15.matrix_ref), custom_call_target="tpu_custom_call" | custom-call | flops 20000000000 | bytes 20000000 | tf_op jit(solution)/shard_map/interior/pallas_call | solution.py:263
  29.4 0.0 collective-permute-done.swapped_ref
  29.4 8.9 %rest.1 = (bf16[64,8192]{1,0:T(8,128)(2,1)S(1)}, f32[32,128]{1,0:T(8,128)S(1)}) custom-call(bf16[64,768]{1,0:T(8,128)(2,1)S(1)} %collective-permute-done.swapped_ref, f32[2,640,128]{2,1,0:T(8,128)S(1)} %copy.11.cells_ref, f32[128,640]{1,0:T(8,128)S(1)} %select_maximum_fusion.1.columns_ref, bf16[128,128]{1,0:T(8,128)(2,1)S(1)} %pad.15.matrix_ref, ...), custom_call_target="tpu_custom_call" | custom-call | tf_op jit(solution)/shard_map/rest/pallas_call | solution.py:274
  38.3 0.0 collective-permute-start.2
  38.3 1.2 %collective-permute-done.2 = f32[32,128]{1,0:T(8,128)S(1)} collective-permute-done((f32[32,128]{1,0:T(8,128)S(1)}, f32[32,128]{1,0:T(8,128)S(1)}, u32[]{:S(2)}, u32[]{:S(2)}) %collective-permute-start.2) | collective-permute-done | bytes 16416 | tf_op jit(solution)/shard_map/ppermute | solution.py:445
  39.5 18.1 %all_to_all.20 = f32[16,32,128]{2,1,0:T(8,128)S(1)} all-to-all(f32[16,32,128]{2,1,0:T(8,128)S(1)} %broadcast_in_dim.7), channel_id=1, replica_groups=mesh['z'=8,'y'=4,'core'=2,'x'=4] {'y','x'}, dimensions={0} | all-to-all | bytes 524288 | tf_op jit(solution)/shard_map/all_to_all | solution.py:448
  57.7 17.2 %all_to_all.21.parts_ref = f32[8,32,128]{2,1,0:T(8,128)S(1)} all-to-all(f32[8,32,128]{2,1,0:T(8,128)S(1)} %broadcast_in_dim.8), channel_id=1, replica_groups=mesh['z'=8,'y'=4,'core'=2,'x'=4] {'z'}, dimensions={0} | all-to-all | bytes 262144 | tf_op jit(solution)/shard_map/all_to_all | solution.py:450
  74.9 3.5 %factor.1 = (bf16[64,8192]{1,0:T(8,128)(2,1)S(1)}, f32[64,64]{1,0:T(8,128)}) custom-call(f32[8,32,128]{2,1,0:T(8,128)S(1)} %all_to_all.21.parts_ref, bf16[64,8192]{1,0:T(8,128)(2,1)S(1)} %get-tuple-element.13.second_ref), custom_call_target="tpu_custom_call" | custom-call | tf_op jit(solution)/shard_map/factor/pallas_call | solution.py:346
  78.4 15.8 %all_to_all.22.pieces_ref = bf16[4,16,8192]{2,1,0:T(8,128)(2,1)S(1)} all-to-all(bf16[4,16,8192]{2,1,0:T(8,128)(2,1)S(1)} %bitcast.17), channel_id=1, replica_groups=mesh['z'=8,'y'=4,'core'=2,'x'=4] {'x'}, dimensions={0} | all-to-all | bytes 2097152 | tf_op jit(solution)/shard_map/all_to_all | solution.py:494
  94.1 1.0 %joined.1 = bf16[16,32768]{1,0:T(8,128)(2,1)} custom-call(bf16[4,16,8192]{2,1,0:T(8,128)(2,1)S(1)} %all_to_all.22.pieces_ref), custom_call_target="tpu_custom_call" | custom-call | tf_op jit(solution)/shard_map/joined/pallas_call | solution.py:433
  (13 shorter events, 0.2 us)
Async XLA Ops:
  2.8 5.9 %copy-start = (s32[125,512]{1,0:T(8,128)S(1)}, s32[125,512]{1,0:T(8,128)}, u32[]{:S(2)}) copy-start(s32[125,512]{1,0:T(8,128)} %param.5) | copy-start | bytes 768004
  2.8 6.0 %copy-start.1 = (f32[125,512]{1,0:T(8,128)S(1)}, f32[125,512]{1,0:T(8,128)}, u32[]{:S(2)}) copy-start(f32[125,512]{1,0:T(8,128)} %param.6) | copy-start | bytes 768004
  2.8 20.7 %all-to-all-start = ((bf16[4,16,9728]{2,1,0:T(8,128)(2,1)}), bf16[4,16,9728]{2,1,0:T(8,128)(2,1)S(1)}, u32[]{:S(2)}, u32[]{:S(2)}) async-start(bf16[4,16,9728]{2,1,0:T(8,128)(2,1)} %quarters.1), calls=%async_computation | async-start | bytes 2490368 | tf_op jit(solution)/shard_map/all_to_all | solution.py:464
  8.8 1.5 %copy-start.2 = (bf16[125,125]{1,0:T(8,128)(2,1)S(1)}, bf16[125,125]{1,0:T(8,128)(2,1)}, u32[]{:S(2)}) copy-start(bf16[125,125]{1,0:T(8,128)(2,1)} %param.7) | copy-start | bytes 93754
  9.0 2.3 %collective-permute-start.1 = (f32[2,96,128]{1,2,0:T(8,128)S(1)}, f32[2,96,128]{1,2,0:T(8,128)S(1)}, u32[]{:S(2)}, u32[]{:S(2)}) collective-permute-start(f32[2,96,128]{1,2,0:T(8,128)S(1)} %slice_select_fusion), channel_id=1, source_target_pairs={{0,4},{1,5},{6,2},{7,3},{4,8},{5,9},{10,6},{11,7},{8,12},{9,13},{1... | collective-permute-start | bytes 294920 | tf_op jit(solution)/shard_map/ppermute | solution.py:478
  23.6 5.8 %collective-permute-start = (bf16[64,768]{1,0:T(8,128)(2,1)S(1)}, bf16[64,768]{1,0:T(8,128)(2,1)S(1)}, u32[]{:S(2)}, u32[]{:S(2)}) collective-permute-start(bf16[64,768]{1,0:T(8,128)(2,1)S(1)} %slice_select_fusion.1), channel_id=1, source_target_pairs={{3,4},{7,8},{11,12},{15,16},{19,20},{23,24},{27,28},{31,32},{35,36... | collective-permute-start | bytes 294920 | tf_op jit(solution)/shard_map/ppermute | solution.py:489
  38.3 1.2 %collective-permute-start.2 = (f32[32,128]{1,0:T(8,128)S(1)}, f32[32,128]{1,0:T(8,128)S(1)}, u32[]{:S(2)}, u32[]{:S(2)}) collective-permute-start(f32[32,128]{1,0:T(8,128)S(1)} %get-tuple-element.12), channel_id=1, source_target_pairs={{0,4},{4,0},{1,5},{5,1},{2,6},{6,2},{3,7},{7,3},{8,12},{12,8},{9,1... | collective-permute-start | bytes 49160 | tf_op jit(solution)/shard_map/ppermute | solution.py:445

commit v10 on v9

--- a/solution.py
+++ b/solution.py
@@ -192,7 +192,9 @@
         slabs = slabs * lax.axis_size(axis)
     whole = owned + 2 * margin
     field[...] = window_ref[...]
-    acc[:, pl.ds(0, whole)] = jnp.zeros((states, whole), jnp.float32)
+    reach = 2 * margin
+    for begin in (0, whole - reach):
+        acc[:, pl.ds(begin, reach)] = jnp.zeros((states, reach), jnp.float32)
 
     @pl.when(slot == 0)
     def _():
@@ -212,15 +214,20 @@
 
     chunk = 4 * LANE
 
-    def to_first(step, carry):
+    def to_first(near, step, carry):
         here = pl.ds(pl.multiple_of(step * chunk, LANE), chunk)
         start = field[:, here].astype(jnp.float32)
-        image = acc_ref[:, here] + acc[:, here] - CENTER * start
+        image = acc_ref[:, here] - CENTER * start
+        if near:
+            image = image + acc[:, here]
         field[:, here] = (image * (1.0 / HALF_WIDTH)).astype(field.dtype)
         acc[:, here] = jnp.zeros((states, chunk), jnp.float32)
         return carry
 
-    lax.fori_loop(0, whole // chunk, to_first, 0)
+    steps, ends_steps = whole // chunk, reach // chunk
+    lax.fori_loop(0, ends_steps, functools.partial(to_first, True), 0)
+    lax.fori_loop(ends_steps, steps - ends_steps, functools.partial(to_first, False), 0)
+    lax.fori_loop(steps - ends_steps, steps, functools.partial(to_first, True), 0)
 
     @pl.when((slab == 0) & (slot == 0))
     def _():
@@ -238,7 +245,7 @@
     ]
     group_block(field, HALO, acc, cells_ref, columns_ref, matrix_ref, whole_range)
 
-    chunk = 16 * LANE
+    chunk = 32 * LANE
 
     def to_second(step, gram):
         at = pl.multiple_of(step * chunk, LANE)

time: 95.7 us -> 95.4 us (level)
  no operation moved by 1% of the time
where the time goes in v10:
time: 95.4 us; the launch traced here: 95 us
  blocking collectives  51.1 us (54%)
  Pallas kernels  20.3 us (21%)
  waiting for transfers between devices  11.9 us (12%)
  starting transfers between devices  7.92 us (8%)
  local copies, waits for them, and re-layouts  1.58 us (2%)
  other arithmetic  1.15 us (1%)
  between operations  0.98 us (1%)
    all_to_all x1, blocking collectives, gathered_terms(): lax.all_to_all(jnp.broadcast_to(x[None], (size, *x.shape)), group, 0, 0)  18.1 us
    all_to_all x1, blocking collectives, gathered_terms(): return lax.all_to_all(copies, 'z', 0, 0)  17.2 us
    all_to_all x1, blocking collectives, per_device(): pieces = lax.all_to_all(pieces, STATE_AXIS, 0, 0)  15.8 us
    all_to_all x1, waiting for transfers between devices, per_device(): pieces = lax.all_to_all(pieces, STATE_AXIS, 0, 0)  10.1 us
    pallas_call x1, Pallas kernels, filtered(): pl.pallas_call(rest_kernel, out_shape=(jax.ShapeDtypeStruct((states, coun...  8.55 us
    all_to_all x1, starting transfers between devices, per_device(): pieces = lax.all_to_all(pieces, STATE_AXIS, 0, 0)  5.91 us
    pallas_call x1, Pallas kernels, filtered(): pl.pallas_call(interior_kernel, out_shape=total, in_specs=[VMEM] * 4, out...  5.12 us
    pallas_call x1, Pallas kernels, orthonormalized(): pl.pallas_call(functools.partial(factor_kernel, total_nodes), out_shape=(...  3.47 us
  transfers between devices with their start and end apart: 4, of which 3 were waited for; matrix products, arithmetic and copies ran while one was open for 3% of the time, Pallas kernels for 5%

profile of v10, /device:TPU:2, one launch (start us, length us, event | category | flops | bytes accessed | tf_op | source)
XLA Modules:
  0.0 95.0 jit_solution(343616119485806162)
XLA Ops:
  0.6 2.2 %quarters.1 = bf16[4,16,9728]{2,1,0:T(8,128)(2,1)} custom-call(bf16[16,32768]{1,0:T(8,128)(2,1)} %block_ref.1), custom_call_target="tpu_custom_call" | custom-call | tf_op jit(solution)/shard_map/quarters/pallas_call | solution.py:424
  2.8 0.0 copy-start
  2.8 0.0 copy-start.1
  2.8 5.9 %all-to-all-start = ((bf16[4,16,9728]{2,1,0:T(8,128)(2,1)}), bf16[4,16,9728]{2,1,0:T(8,128)(2,1)S(1)}, u32[]{:S(2)}, u32[]{:S(2)}) async-start(bf16[4,16,9728]{2,1,0:T(8,128)(2,1)} %quarters.1), calls=%async_computation | async-start | bytes 2490368 | tf_op jit(solution)/shard_map/all_to_all | solution.py:471
  8.8 0.0 copy-done
  8.8 0.0 copy-start.2
  8.8 0.0 copy-done.1
  8.9 0.1 slice_select_fusion
  9.0 1.3 %collective-permute-start.1 = (f32[2,96,128]{1,2,0:T(8,128)S(1)}, f32[2,96,128]{1,2,0:T(8,128)S(1)}, u32[]{:S(2)}, u32[]{:S(2)}) collective-permute-start(f32[2,96,128]{1,2,0:T(8,128)S(1)} %slice_select_fusion), channel_id=1, source_target_pairs={{0,4},{1,5},{6,2},{7,3},{4,8},{5,9},{10,6},{11,7},{8,12},{9,13},{1... | collective-permute-start | bytes 294920 | tf_op jit(solution)/shard_map/ppermute | solution.py:485
  10.3 0.0 copy-done.2
  10.3 0.1 copy.9
  10.4 0.1 pad.20.clone
  10.5 0.7 collective-permute-done.1
  11.2 0.9 maximum_maximum_fusion
  12.1 1.3 %copy.11.cells_ref = f32[2,640,128]{2,1,0:T(8,128)S(1)} copy(f32[2,640,128]{1,2,0:T(8,128)} %maximum_maximum_fusion) | data formatting | bytes 1310720 | tf_op jit(solution)/shard_map/concatenate | solution.py:488
  13.5 10.1 %all-to-all-done = bf16[4,16,9728]{2,1,0:T(8,128)(2,1)S(1)} async-done(((bf16[4,16,9728]{2,1,0:T(8,128)(2,1)}), bf16[4,16,9728]{2,1,0:T(8,128)(2,1)S(1)}, u32[]{:S(2)}, u32[]{:S(2)}) %all-to-all-start) | async-done | bytes 1245216 | tf_op jit(solution)/shard_map/all_to_all | solution.py:471
  23.6 0.7 collective-permute-start
  24.2 5.1 %interior.1.acc_ref = f32[64,9984]{1,0:T(8,128)S(1)} custom-call(bf16[64,9728]{1,0:T(8,128)(2,1)S(1)} %bitcast.15, f32[2,640,128]{2,1,0:T(8,128)S(1)} %copy.11.cells_ref, f32[128,640]{1,0:T(8,128)S(1)} %select_maximum_fusion.1.columns_ref, bf16[128,128]{1,0:T(8,128)(2,1)S(1)} %pad.15.matrix_ref), custom_call_target="tpu_custom_call" | custom-call | flops 20000000000 | bytes 20000000 | tf_op jit(solution)/shard_map/interior/pallas_call | solution.py:270
  29.4 0.0 collective-permute-done.swapped_ref
  29.4 8.5 %rest.1 = (bf16[64,8192]{1,0:T(8,128)(2,1)S(1)}, f32[32,128]{1,0:T(8,128)S(1)}) custom-call(bf16[64,768]{1,0:T(8,128)(2,1)S(1)} %collective-permute-done.swapped_ref, f32[2,640,128]{2,1,0:T(8,128)S(1)} %copy.11.cells_ref, f32[128,640]{1,0:T(8,128)S(1)} %select_maximum_fusion.1.columns_ref, bf16[128,128]{1,0:T(8,128)(2,1)S(1)} %pad.15.matrix_ref, ...), custom_call_target="tpu_custom_call" | custom-call | tf_op jit(solution)/shard_map/rest/pallas_call | solution.py:281
  37.9 0.0 collective-permute-start.2
  38.0 1.2 %collective-permute-done.2 = f32[32,128]{1,0:T(8,128)S(1)} collective-permute-done((f32[32,128]{1,0:T(8,128)S(1)}, f32[32,128]{1,0:T(8,128)S(1)}, u32[]{:S(2)}, u32[]{:S(2)}) %collective-permute-start.2) | collective-permute-done | bytes 16416 | tf_op jit(solution)/shard_map/ppermute | solution.py:452
  39.2 18.1 %all_to_all.20 = f32[16,32,128]{2,1,0:T(8,128)S(1)} all-to-all(f32[16,32,128]{2,1,0:T(8,128)S(1)} %broadcast_in_dim.7), channel_id=1, replica_groups=mesh['z'=8,'y'=4,'core'=2,'x'=4] {'y','x'}, dimensions={0} | all-to-all | bytes 524288 | tf_op jit(solution)/shard_map/all_to_all | solution.py:455
  57.3 17.2 %all_to_all.21.parts_ref = f32[8,32,128]{2,1,0:T(8,128)S(1)} all-to-all(f32[8,32,128]{2,1,0:T(8,128)S(1)} %broadcast_in_dim.8), channel_id=1, replica_groups=mesh['z'=8,'y'=4,'core'=2,'x'=4] {'z'}, dimensions={0} | all-to-all | bytes 262144 | tf_op jit(solution)/shard_map/all_to_all | solution.py:457
  74.6 3.5 %factor.1 = (bf16[64,8192]{1,0:T(8,128)(2,1)S(1)}, f32[64,64]{1,0:T(8,128)}) custom-call(f32[8,32,128]{2,1,0:T(8,128)S(1)} %all_to_all.21.parts_ref, bf16[64,8192]{1,0:T(8,128)(2,1)S(1)} %get-tuple-element.13.second_ref), custom_call_target="tpu_custom_call" | custom-call | tf_op jit(solution)/shard_map/factor/pallas_call | solution.py:353
  78.0 15.8 %all_to_all.22.pieces_ref = bf16[4,16,8192]{2,1,0:T(8,128)(2,1)S(1)} all-to-all(bf16[4,16,8192]{2,1,0:T(8,128)(2,1)S(1)} %bitcast.17), channel_id=1, replica_groups=mesh['z'=8,'y'=4,'core'=2,'x'=4] {'x'}, dimensions={0} | all-to-all | bytes 2097152 | tf_op jit(solution)/shard_map/all_to_all | solution.py:501
  93.8 1.0 %joined.1 = bf16[16,32768]{1,0:T(8,128)(2,1)} custom-call(bf16[4,16,8192]{2,1,0:T(8,128)(2,1)S(1)} %all_to_all.22.pieces_ref), custom_call_target="tpu_custom_call" | custom-call | tf_op jit(solution)/shard_map/joined/pallas_call | solution.py:440
  (13 shorter events, 0.2 us)
Async XLA Ops:
  2.8 5.9 %copy-start = (s32[125,512]{1,0:T(8,128)S(1)}, s32[125,512]{1,0:T(8,128)}, u32[]{:S(2)}) copy-start(s32[125,512]{1,0:T(8,128)} %param.5) | copy-start | bytes 768004
  2.8 6.0 %copy-start.1 = (f32[125,512]{1,0:T(8,128)S(1)}, f32[125,512]{1,0:T(8,128)}, u32[]{:S(2)}) copy-start(f32[125,512]{1,0:T(8,128)} %param.6) | copy-start | bytes 768004
  2.8 20.7 %all-to-all-start = ((bf16[4,16,9728]{2,1,0:T(8,128)(2,1)}), bf16[4,16,9728]{2,1,0:T(8,128)(2,1)S(1)}, u32[]{:S(2)}, u32[]{:S(2)}) async-start(bf16[4,16,9728]{2,1,0:T(8,128)(2,1)} %quarters.1), calls=%async_computation | async-start | bytes 2490368 | tf_op jit(solution)/shard_map/all_to_all | solution.py:471
  8.8 1.5 %copy-start.2 = (bf16[125,125]{1,0:T(8,128)(2,1)S(1)}, bf16[125,125]{1,0:T(8,128)(2,1)}, u32[]{:S(2)}) copy-start(bf16[125,125]{1,0:T(8,128)(2,1)} %param.7) | copy-start | bytes 93754
  9.0 2.3 %collective-permute-start.1 = (f32[2,96,128]{1,2,0:T(8,128)S(1)}, f32[2,96,128]{1,2,0:T(8,128)S(1)}, u32[]{:S(2)}, u32[]{:S(2)}) collective-permute-start(f32[2,96,128]{1,2,0:T(8,128)S(1)} %slice_select_fusion), channel_id=1, source_target_pairs={{0,4},{1,5},{6,2},{7,3},{4,8},{5,9},{10,6},{11,7},{8,12},{9,13},{1... | collective-permute-start | bytes 294920 | tf_op jit(solution)/shard_map/ppermute | solution.py:485
  23.6 5.8 %collective-permute-start = (bf16[64,768]{1,0:T(8,128)(2,1)S(1)}, bf16[64,768]{1,0:T(8,128)(2,1)S(1)}, u32[]{:S(2)}, u32[]{:S(2)}) collective-permute-start(bf16[64,768]{1,0:T(8,128)(2,1)S(1)} %slice_select_fusion.1), channel_id=1, source_target_pairs={{3,4},{7,8},{11,12},{15,16},{19,20},{23,24},{27,28},{31,32},{35,36... | collective-permute-start | bytes 294920 | tf_op jit(solution)/shard_map/ppermute | solution.py:496
  37.9 1.2 %collective-permute-start.2 = (f32[32,128]{1,0:T(8,128)S(1)}, f32[32,128]{1,0:T(8,128)S(1)}, u32[]{:S(2)}, u32[]{:S(2)}) collective-permute-start(f32[32,128]{1,0:T(8,128)S(1)} %get-tuple-element.12), channel_id=1, source_target_pairs={{0,4},{4,0},{1,5},{5,1},{2,6},{6,2},{3,7},{7,3},{8,12},{12,8},{9,1... | collective-permute-start | bytes 49160 | tf_op jit(solution)/shard_map/ppermute | solution.py:452
